TPU v7x, 32 devices: a whole 2x2x4 slice. The times are simulated.
32 devices in a mesh: groups: 2 (over y), gx: 4 (over z), gy: 2 (over x), vert: 2 (over core).
Axes of the slice: x: 2, y: 2, z: 4, core: 2. Of those that a mesh axis runs over, the one named last changes fastest.
Arguments:
- tiles: bfloat16 [6, 2, 128, 8, 16, 128], P('vert', 'gy', ('groups', 'gx')), parts along dimension 2, may hold values from 0.19921875 to 5
- tile_block: int32 [6, 2, 128, 1], P(None, None, 'groups'), parts along dimension 2, may hold values from 0 to 3; in each aligned block of 16 rows (0 to 15, 16 to 31, ..., all dimensions but the last counted through in order) at most 8 rows name the same one
- tile_x: int32 [6, 2, 128], P(None, None, 'groups'), parts along dimension 2, may hold values from 0 to 24
- tile_y: int32 [6, 2, 128], P(None, None, 'groups'), parts along dimension 2, may hold values from 0 to 48
- psf: float32 [6, 3, 15], replicated, may hold values from 0.03 to 0.1
- initial: float32 [256, 128, 128], P(('groups', 'gx'), 'gy'), parts along dimension 0, may hold values from 0.5 to 2
Outputs:
- estimate: float32 [256, 128, 128], P(('groups', 'gx'), 'gy'), parts along dimension 0
There are 2 independent parts, one for each index of `groups`. A program takes and returns all parts, laid end to end along the dimension named above; an argument that names none is the same for every part. Nothing has to cross between parts.
Inputs may be any that keep to these rules, and one draw needn't show every extreme that they name: `tile_block`: among the 16 tiles of one view held by one device (tile numbers in aligned groups of 16 within a block row), no block column is named more than 8 times.
All inputs are finite; a program needn't handle non-finite values.
Results may differ from a plain program's by a relative error of at most 0.0009.
Values may be sent and summed in bfloat16 or wider, within the bound.
A program may use at most 128 MiB of HBM per device.

v0:
```python
import jax
import jax.numpy as jnp
from jax import lax
from jax.sharding import PartitionSpec as P

ITERS = 2


soft_floor = 0.01
damping = 0.5


def extended(block, sides, width):
    for axis, dim in sides:
        count = lax.axis_size(axis)
        forward = [(i, i + 1) for i in range(count - 1)]
        backward = [(target, source) for source, target in forward]
        low = lax.ppermute(
            lax.slice_in_dim(block, block.shape[dim] - width, None, axis=dim), axis, forward
        )
        high = lax.ppermute(lax.slice_in_dim(block, 0, width, axis=dim), axis, backward)
        block = jnp.concatenate([low, block, high], axis=dim)
    return block


def valid_pass(volume, kernel, dimension, adjoint):
    radius = kernel.shape[0] // 2
    length = volume.shape[dimension] - 2 * radius
    summed = None
    for tap_index in range(kernel.shape[0]):
        offset = 2 * radius - tap_index if adjoint else tap_index
        weighted = kernel[tap_index] * lax.slice_in_dim(
            volume, offset, offset + length, axis=dimension
        )
        summed = weighted if summed is None else summed + weighted
    return summed


def padded_pass(volume, kernel, dimension, adjoint):
    radius = kernel.shape[0] // 2
    margins = [(0, 0)] * volume.ndim
    margins[dimension] = (radius, radius)
    return valid_pass(jnp.pad(volume, margins), kernel, dimension, adjoint)


def shards(tiles, tile_block, tile_x, tile_y, psf, initial):
    column_count = lax.axis_size("gx")
    column_index = lax.axis_index("gx")
    row_index = lax.axis_index("gy")
    core_index = lax.axis_index("vert")
    local_views = tiles.shape[0]
    all_views = psf.shape[0]
    per_device = tiles.shape[2]
    tile_wide = tiles.shape[3]
    tile_tall = tiles.shape[4]
    block_x = initial.shape[0]
    block_y = initial.shape[1]
    capacity = max(2, 2 * per_device // column_count)
    radius = psf.shape[2] // 2
    first_view = core_index * local_views
    mine_psf = lax.dynamic_slice_in_dim(psf, first_view, local_views, 0)

    def my_rows(table):
        chosen = lax.dynamic_slice_in_dim(table, first_view, local_views, 0)
        chosen = lax.dynamic_slice_in_dim(chosen, row_index, 1, 1)[:, 0]
        return chosen.reshape(local_views, column_count, per_device)

    targets = my_rows(tile_block[:, :, :, 0])
    offsets_x = my_rows(tile_x)
    offsets_y = my_rows(tile_y)
    columns_iota = jnp.arange(column_count, dtype=jnp.int32)
    hits = (targets[..., None] == columns_iota).astype(jnp.int32)
    ranks = jnp.cumsum(hits, axis=2, dtype=jnp.int32)
    slot_ids = jnp.arange(capacity, dtype=jnp.int32) + 1
    sent_hits = jnp.swapaxes(lax.dynamic_slice_in_dim(hits, column_index, 1, 1)[:, 0], 1, 2)
    sent_ranks = jnp.swapaxes(lax.dynamic_slice_in_dim(ranks, column_index, 1, 1)[:, 0], 1, 2)
    chooser = sent_hits[:, :, None, :] * (
        sent_ranks[:, :, None, :] == slot_ids[None, None, :, None]
    ).astype(jnp.int32)
    outgoing = jnp.einsum(
        "vgkj,vjabz->gvkabz",
        chooser.astype(jnp.bfloat16),
        tiles[:, 0],
        preferred_element_type=jnp.bfloat16,
    )
    arrived = lax.all_to_all(outgoing, "gx", split_axis=0, concat_axis=0, tiled=True)
    from_hits = lax.dynamic_slice_in_dim(hits, column_index, 1, 3)[..., 0]
    from_ranks = lax.dynamic_slice_in_dim(ranks, column_index, 1, 3)[..., 0]
    picks = from_hits[:, :, None, :] * (
        from_ranks[:, :, None, :] == slot_ids[None, None, :, None]
    ).astype(jnp.int32)
    filled = jnp.sum(picks, axis=3)
    corner_x = jnp.sum(picks * offsets_x[:, :, None, :], axis=3)
    corner_y = jnp.sum(picks * offsets_y[:, :, None, :], axis=3)
    lanes_x = jnp.arange(block_x, dtype=jnp.int32)
    lanes_y = jnp.arange(block_y, dtype=jnp.int32)
    steps_x = jnp.arange(tile_wide, dtype=jnp.int32)
    steps_y = jnp.arange(tile_tall, dtype=jnp.int32)
    place_x = (
        (
            lanes_x[None, None, None, None, :]
            == corner_x[..., None, None] + steps_x[None, None, None, :, None]
        ).astype(jnp.int32)
        * filled[..., None, None]
    ).astype(jnp.bfloat16)
    place_y = (
        (
            lanes_y[None, None, None, None, :]
            == corner_y[..., None, None] + steps_y[None, None, None, :, None]
        ).astype(jnp.int32)
        * filled[..., None, None]
    ).astype(jnp.bfloat16)
    row_iota = jnp.arange(tile_block.shape[1], dtype=jnp.int32)
    global_x = (tile_block[..., 0] * block_x + tile_x).reshape(all_views, -1)
    global_y = (row_iota[None, :, None] * block_y + tile_y).reshape(all_views, -1)
    cells_x = column_index * block_x - radius + jnp.arange(block_x + 2 * radius, dtype=jnp.int32)
    cells_y = row_index * block_y - radius + jnp.arange(block_y + 2 * radius, dtype=jnp.int32)
    cover_x = (
        (cells_x >= global_x[..., None]) & (cells_x < global_x[..., None] + tile_wide)
    ).astype(jnp.bfloat16)
    cover_y = (
        (cells_y >= global_y[..., None]) & (cells_y < global_y[..., None] + tile_tall)
    ).astype(jnp.bfloat16)
    counts = jnp.einsum("vti,vtj->vij", cover_x, cover_y, preferred_element_type=jnp.float32)
    unit_column = jnp.ones((initial.shape[2],), jnp.float32)
    norm_field = None
    for view_index in range(all_views):
        weight_plane = jnp.minimum(counts[view_index], 1.0)
        profile = padded_pass(unit_column, psf[view_index, 2], 0, True)
        spread = valid_pass(
            valid_pass(weight_plane, psf[view_index, 0], 0, True), psf[view_index, 1], 1, True
        )
        contribution = spread[:, :, None] * profile
        norm_field = contribution if norm_field is None else norm_field + contribution
    mine_counts = lax.dynamic_slice_in_dim(counts, first_view, local_views, 0)[
        :, radius : radius + block_x, radius : radius + block_y
    ]
    observed = []
    for view_index in range(local_views):
        stretched = jnp.einsum(
            "skabz,skai->skibz",
            arrived[:, view_index],
            place_x[view_index],
            preferred_element_type=jnp.bfloat16,
        )
        summed = jnp.einsum(
            "skibz,skbj->ijz", stretched, place_y[view_index], preferred_element_type=jnp.float32
        )
        observed.append(summed / jnp.maximum(mine_counts[view_index], 1.0)[:, :, None])
    estimate = initial
    for sweep_index in range(ITERS):
        widened = extended(estimate.astype(jnp.bfloat16), (("gx", 0), ("gy", 1)), radius).astype(
            estimate.dtype
        )
        ratios = []
        for view_index in range(local_views):
            blurred = valid_pass(widened, mine_psf[view_index, 0], 0, False)
            blurred = valid_pass(blurred, mine_psf[view_index, 1], 1, False)
            blurred = padded_pass(blurred, mine_psf[view_index, 2], 2, False)
            quotient = observed[view_index] / (blurred + soft_floor)
            ratios.append(padded_pass(quotient, mine_psf[view_index, 2], 2, True))
        stacked = jnp.stack(ratios)
        widened_ratio = extended(
            stacked.astype(jnp.bfloat16), (("gx", 1), ("gy", 2)), radius
        ).astype(stacked.dtype)
        partial_value = None
        for view_index in range(local_views):
            spread = valid_pass(widened_ratio[view_index], mine_psf[view_index, 0], 0, True)
            spread = valid_pass(spread, mine_psf[view_index, 1], 1, True)
            partial_value = spread if partial_value is None else partial_value + spread
        combined = lax.psum(partial_value, "vert")
        estimate = estimate * (combined + damping) / (norm_field + damping)
    return estimate


def solution(mesh):
    in_specs = (
        P("vert", "gy", ("groups", "gx"), None, None, None),
        P(None, None, "groups", None),
        P(None, None, "groups"),
        P(None, None, "groups"),
        P(),
        P(("groups", "gx"), "gy", None),
    )
    out_specs = P(("groups", "gx"), "gy", None)
    return jax.shard_map(shards, mesh=mesh, in_specs=in_specs, out_specs=out_specs, check_vma=False)
```

profile of v0, /device:TPU:0, one launch (start us, length us, event | category | flops | bytes accessed | tf_op | source)
XLA Modules:
  0.0 781.6 jit_solution(13534718927463042070)
XLA Ops:
  37.8 9.6 %fusion.811 = f32[32,78]{1,0:T(8,128)S(1)} fusion(f32[1,46,78]{2,1,0:T(8,128)S(1)} %get-tuple-element.32, f32[]{:T(128)} %bitcast.201, f32[]{:T(128)} %bitcast.200, f32[]{:T(128)} %bitcast.199, f32[]{:T(128)} %bitcast.198, f32[]{:T(128)} %bitcast.197, f32[]{:T(128)} %bitcast.196, f32[]{:T(128)} %bitcast.195, f32[]{:T(128)} %bitcast.194, f32[]{:T(128)} %bitcast.193, ...), kind=kLoop, calls=%fused_computation.1477 | loop fusion | flops 72384 | bytes 159804 | tf_op jit(solution)/shard_map/add | solution.py:35
  47.4 9.3 %fusion.796 = f32[32,64]{1,0:T(8,128)S(1)} fusion(f32[32,78]{1,0:T(8,128)S(1)} %fusion.811, f32[]{:T(128)} %bitcast.216, f32[]{:T(128)} %bitcast.215, f32[]{:T(128)} %bitcast.214, f32[]{:T(128)} %bitcast.213, f32[]{:T(128)} %bitcast.212, f32[]{:T(128)} %bitcast.211, f32[]{:T(128)} %bitcast.210, f32[]{:T(128)} %bitcast.209, f32[]{:T(128)} %bitcast.208, ...), kind=kLoop, calls=%fused_computation.1447 | loop fusion | flops 59392 | bytes 131132 | tf_op jit(solution)/shard_map/add | solution.py:35
  75.1 9.5 %fusion.695 = f32[32,78]{1,0:T(8,128)S(1)} fusion(f32[1,46,78]{2,1,0:T(8,128)S(1)} %get-tuple-element.34, f32[]{:T(128)} %bitcast.385, f32[]{:T(128)} %bitcast.384, f32[]{:T(128)} %bitcast.383, f32[]{:T(128)} %bitcast.382, f32[]{:T(128)} %bitcast.381, f32[]{:T(128)} %bitcast.380, f32[]{:T(128)} %bitcast.379, f32[]{:T(128)} %bitcast.378, f32[]{:T(128)} %bitcast.377, ...), kind=kLoop, calls=%fused_computation.1241 | loop fusion | flops 72384 | bytes 159804 | tf_op jit(solution)/shard_map/add | solution.py:35
  84.6 9.7 %fusion.680 = f32[32,64]{1,0:T(8,128)S(1)} fusion(f32[32,78]{1,0:T(8,128)S(1)} %fusion.695, f32[]{:T(128)} %bitcast.400, f32[]{:T(128)} %bitcast.399, f32[]{:T(128)} %bitcast.398, f32[]{:T(128)} %bitcast.397, f32[]{:T(128)} %bitcast.396, f32[]{:T(128)} %bitcast.395, f32[]{:T(128)} %bitcast.394, f32[]{:T(128)} %bitcast.393, f32[]{:T(128)} %bitcast.392, ...), kind=kLoop, calls=%fused_computation.1211 | loop fusion | flops 59392 | bytes 131132 | tf_op jit(solution)/shard_map/add | solution.py:35
  94.3 9.4 %multiply_add_fusion.8 = f32[128]{0:T(128)S(1)} fusion(f32[]{:T(128)} %bitcast.369, f32[]{:T(128)} %bitcast.368, f32[]{:T(128)} %bitcast.367, f32[]{:T(128)} %bitcast.366, f32[]{:T(128)} %bitcast.365, f32[]{:T(128)} %bitcast.364, f32[]{:T(128)} %bitcast.363, f32[]{:T(128)} %bitcast.362, f32[]{:T(128)} %bitcast.361, f32[]{:T(128)} %bitcast.360, ...), kind=kLoop, calls=%fused_computation.1593 | loop fusion | flops 3584 | bytes 1084 | tf_op jit(solution)/shard_map/add | solution.py:35
  110.5 9.6 %multiply_add_fusion.7 = f32[128]{0:T(128)S(1)} fusion(f32[]{:T(128)} %bitcast.415, f32[]{:T(128)} %bitcast.414, f32[]{:T(128)} %bitcast.413, f32[]{:T(128)} %bitcast.412, f32[]{:T(128)} %bitcast.411, f32[]{:T(128)} %bitcast.410, f32[]{:T(128)} %bitcast.409, f32[]{:T(128)} %bitcast.408, f32[]{:T(128)} %bitcast.407, f32[]{:T(128)} %bitcast.406, ...), kind=kLoop, calls=%fused_computation.1592 | loop fusion | flops 3584 | bytes 1084 | tf_op jit(solution)/shard_map/add | solution.py:35
  120.4 11.3 %multiply_add_fusion.5 = f32[32,78,128]{2,1,0:T(8,128)S(1)} fusion(f32[46,78,128]{2,1,0:T(8,128)S(1)} %maximum_convert_fusion.2, f32[]{:T(128)} %bitcast.39, f32[]{:T(128)} %bitcast.38, f32[]{:T(128)} %bitcast.37, f32[]{:T(128)} %bitcast.36, f32[]{:T(128)} %bitcast.35, f32[]{:T(128)} %bitcast.34, f32[]{:T(128)} %bitcast.33, f32[]{:T(128)} %bitcast.32, ...), kind=kLoop, calls=%fused_computation.366 | loop fusion | flops 9265152 | bytes 20447292 | tf_op jit(solution)/shard_map/add | solution.py:35
  131.7 11.2 %multiply_add_fusion.4 = f32[32,78,128]{2,1,0:T(8,128)S(1)} fusion(f32[46,78,128]{2,1,0:T(8,128)S(1)} %maximum_convert_fusion.2, f32[]{:T(128)} %bitcast.96, f32[]{:T(128)} %bitcast.95, f32[]{:T(128)} %bitcast.94, f32[]{:T(128)} %bitcast.93, f32[]{:T(128)} %bitcast.92, f32[]{:T(128)} %bitcast.91, f32[]{:T(128)} %bitcast.90, f32[]{:T(128)} %bitcast.89, ...), kind=kLoop, calls=%fused_computation.365 | loop fusion | flops 9265152 | bytes 20447292 | tf_op jit(solution)/shard_map/add | solution.py:35
  142.9 11.0 %multiply_add_fusion.3 = f32[32,78,128]{2,1,0:T(8,128)S(1)} fusion(f32[46,78,128]{2,1,0:T(8,128)S(1)} %maximum_convert_fusion.2, f32[]{:T(128)} %bitcast.153, f32[]{:T(128)} %bitcast.152, f32[]{:T(128)} %bitcast.151, f32[]{:T(128)} %bitcast.150, f32[]{:T(128)} %bitcast.149, f32[]{:T(128)} %bitcast.148, f32[]{:T(128)} %bitcast.147, f32[]{:T(128)} %bitcast.146, ...), kind=kLoop, calls=%fused_computation.364 | loop fusion | flops 9265152 | bytes 20447292 | tf_op jit(solution)/shard_map/add | solution.py:35
  153.8 12.0 %fusion.600 = f32[32,64,128]{2,1,0:T(8,128)} fusion(f32[32,78,128]{2,1,0:T(8,128)S(1)} %multiply_add_fusion.5, f32[]{:T(128)} %bitcast.53, f32[]{:T(128)} %bitcast.52, f32[]{:T(128)} %bitcast.51, f32[]{:T(128)} %bitcast.50, f32[]{:T(128)} %bitcast.49, f32[]{:T(128)} %bitcast.48, f32[]{:T(128)} %bitcast.47, f32[]{:T(128)} %bitcast.46, f32[]{:T(128)} %bitcast.45, ...), kind=kLoop, calls=%fused_computation.1027 | loop fusion | flops 7602176 | bytes 16777276 | tf_op jit(solution)/shard_map/add | solution.py:35
  165.8 12.1 %fusion.572 = f32[32,64,128]{2,1,0:T(8,128)} fusion(f32[32,78,128]{2,1,0:T(8,128)S(1)} %multiply_add_fusion.3, f32[]{:T(128)} %bitcast.167, f32[]{:T(128)} %bitcast.166, f32[]{:T(128)} %bitcast.165, f32[]{:T(128)} %bitcast.164, f32[]{:T(128)} %bitcast.163, f32[]{:T(128)} %bitcast.162, f32[]{:T(128)} %bitcast.161, f32[]{:T(128)} %bitcast.160, f32[]{:T(128)} %bitcast.159, ...), kind=kLoop, calls=%fused_computation.969 | loop fusion | flops 7602176 | bytes 16777276 | tf_op jit(solution)/shard_map/add | solution.py:35
  177.9 11.7 %fusion.586 = f32[32,64,128]{2,1,0:T(8,128)} fusion(f32[32,78,128]{2,1,0:T(8,128)S(1)} %multiply_add_fusion.4, f32[]{:T(128)} %bitcast.110, f32[]{:T(128)} %bitcast.109, f32[]{:T(128)} %bitcast.108, f32[]{:T(128)} %bitcast.107, f32[]{:T(128)} %bitcast.106, f32[]{:T(128)} %bitcast.105, f32[]{:T(128)} %bitcast.104, f32[]{:T(128)} %bitcast.103, f32[]{:T(128)} %bitcast.102, ...), kind=kLoop, calls=%fused_computation.998 | loop fusion | flops 7602176 | bytes 16777276 | tf_op jit(solution)/shard_map/add | solution.py:35
  193.5 18.1 %multiply_divide_fusion.7 = (f32[32,64,128]{2,1,0:T(8,128)S(1)}, f32[32,64,128]{2,1,0:T(8,128)}) fusion(f32[32,64,128]{2,1,0:T(8,128)S(1)} %copy-done.7, f32[]{:T(128)} %bitcast.67, f32[]{:T(128)} %bitcast.66, f32[]{:T(128)} %bitcast.65, f32[]{:T(128)} %bitcast.64, f32[]{:T(128)} %bitcast.63, f32[]{:T(128)} %bitcast.62, f32[]{:T(128)} %bitcast.61, ...), kind=kOutput, calls=%fused_computation.1069 | convolution fusion | flops 276824064 | bytes 7487548 | tf_op jit(solution)/shard_map/skibz,skbj->ijz/dot_general | solution.py:146
  211.6 13.3 %fusion.623 = bf16[1,32,64,128]{3,2,1,0:T(8,128)(2,1)S(1)} fusion(f32[32,64,128]{2,1,0:T(8,128)S(1)} %get-tuple-element.447, f32[]{:T(128)} %bitcast.67, f32[]{:T(128)} %bitcast.66, f32[]{:T(128)} %bitcast.65, f32[]{:T(128)} %bitcast.64, f32[]{:T(128)} %bitcast.63, f32[]{:T(128)} %bitcast.62, f32[]{:T(128)} %bitcast.61, f32[]{:T(128)} %bitcast.60, ...), kind=kLoop, calls=%fused_computation.1080 | loop fusion | flops 7864320 | bytes 1572924 | tf_op jit(solution)/shard_map/stack | solution.py:162
  226.7 18.2 %multiply_divide_fusion.6 = (f32[32,64,128]{2,1,0:T(8,128)S(1)}, f32[32,64,128]{2,1,0:T(8,128)}) fusion(f32[32,64,128]{2,1,0:T(8,128)S(1)} %copy-done.6, f32[]{:T(128)} %bitcast.124, f32[]{:T(128)} %bitcast.123, f32[]{:T(128)} %bitcast.122, f32[]{:T(128)} %bitcast.121, f32[]{:T(128)} %bitcast.120, f32[]{:T(128)} %bitcast.119, f32[]{:T(128)} %bitcast.118, ...), kind=kOutput, calls=%fused_computation.1068 | convolution fusion | flops 276824064 | bytes 7487548 | tf_op jit(solution)/shard_map/skibz,skbj->ijz/dot_general | solution.py:146
  244.9 13.2 %fusion.624 = bf16[1,32,64,128]{3,2,1,0:T(8,128)(2,1)S(1)} fusion(f32[32,64,128]{2,1,0:T(8,128)S(1)} %get-tuple-element.445, f32[]{:T(128)} %bitcast.124, f32[]{:T(128)} %bitcast.123, f32[]{:T(128)} %bitcast.122, f32[]{:T(128)} %bitcast.121, f32[]{:T(128)} %bitcast.120, f32[]{:T(128)} %bitcast.119, f32[]{:T(128)} %bitcast.118, f32[]{:T(128)} %bitcast.117, ...), kind=kLoop, calls=%fused_computation.1081 | loop fusion | flops 7864320 | bytes 1572924 | tf_op jit(solution)/shard_map/stack | solution.py:162
  259.9 18.6 %multiply_divide_fusion.5 = (f32[32,64,128]{2,1,0:T(8,128)S(1)}, f32[32,64,128]{2,1,0:T(8,128)}) fusion(f32[32,64,128]{2,1,0:T(8,128)S(1)} %copy-done.5, f32[]{:T(128)} %bitcast.181, f32[]{:T(128)} %bitcast.180, f32[]{:T(128)} %bitcast.179, f32[]{:T(128)} %bitcast.178, f32[]{:T(128)} %bitcast.177, f32[]{:T(128)} %bitcast.176, f32[]{:T(128)} %bitcast.175, ...), kind=kOutput, calls=%fused_computation.1067 | convolution fusion | flops 276824064 | bytes 7487548 | tf_op jit(solution)/shard_map/skibz,skbj->ijz/dot_general | solution.py:146
  278.5 13.2 %fusion.625 = bf16[1,32,64,128]{3,2,1,0:T(8,128)(2,1)S(1)} fusion(f32[32,64,128]{2,1,0:T(8,128)S(1)} %get-tuple-element.443, f32[]{:T(128)} %bitcast.181, f32[]{:T(128)} %bitcast.180, f32[]{:T(128)} %bitcast.179, f32[]{:T(128)} %bitcast.178, f32[]{:T(128)} %bitcast.177, f32[]{:T(128)} %bitcast.176, f32[]{:T(128)} %bitcast.175, f32[]{:T(128)} %bitcast.174, ...), kind=kLoop, calls=%fused_computation.1082 | loop fusion | flops 7864320 | bytes 1572924 | tf_op jit(solution)/shard_map/stack | solution.py:162
  297.1 9.5 %multiply_add_fusion.11 = f32[128]{0:T(128)S(1)} fusion(f32[]{:T(128)} %bitcast.231, f32[]{:T(128)} %bitcast.230, f32[]{:T(128)} %bitcast.229, f32[]{:T(128)} %bitcast.228, f32[]{:T(128)} %bitcast.227, f32[]{:T(128)} %bitcast.226, f32[]{:T(128)} %bitcast.225, f32[]{:T(128)} %bitcast.224, f32[]{:T(128)} %bitcast.223, f32[]{:T(128)} %bitcast.222, ...), kind=kLoop, calls=%fused_computation.1596 | loop fusion | flops 3584 | bytes 1084 | tf_op jit(solution)/shard_map/add | solution.py:35
  307.4 9.5 %fusion.724 = f32[32,78]{1,0:T(8,128)S(1)} fusion(f32[1,46,78]{2,1,0:T(8,128)S(1)} %get-tuple-element.35, f32[]{:T(128)} %bitcast.339, f32[]{:T(128)} %bitcast.338, f32[]{:T(128)} %bitcast.337, f32[]{:T(128)} %bitcast.336, f32[]{:T(128)} %bitcast.335, f32[]{:T(128)} %bitcast.334, f32[]{:T(128)} %bitcast.333, f32[]{:T(128)} %bitcast.332, f32[]{:T(128)} %bitcast.331, ...), kind=kLoop, calls=%fused_computation.1300 | loop fusion | flops 72384 | bytes 159804 | tf_op jit(solution)/shard_map/add | solution.py:35
  322.9 9.4 %multiply_add_fusion.10 = f32[128]{0:T(128)S(1)} fusion(f32[]{:T(128)} %bitcast.277, f32[]{:T(128)} %bitcast.276, f32[]{:T(128)} %bitcast.275, f32[]{:T(128)} %bitcast.274, f32[]{:T(128)} %bitcast.273, f32[]{:T(128)} %bitcast.272, f32[]{:T(128)} %bitcast.271, f32[]{:T(128)} %bitcast.270, f32[]{:T(128)} %bitcast.269, f32[]{:T(128)} %bitcast.268, ...), kind=kLoop, calls=%fused_computation.1595 | loop fusion | flops 3584 | bytes 1084 | tf_op jit(solution)/shard_map/add | solution.py:35
  332.3 9.6 %fusion.709 = f32[32,64]{1,0:T(8,128)S(1)} fusion(f32[32,78]{1,0:T(8,128)S(1)} %fusion.724, f32[]{:T(128)} %bitcast.354, f32[]{:T(128)} %bitcast.353, f32[]{:T(128)} %bitcast.352, f32[]{:T(128)} %bitcast.351, f32[]{:T(128)} %bitcast.350, f32[]{:T(128)} %bitcast.349, f32[]{:T(128)} %bitcast.348, f32[]{:T(128)} %bitcast.347, f32[]{:T(128)} %bitcast.346, ...), kind=kLoop, calls=%fused_computation.1270 | loop fusion | flops 59392 | bytes 131132 | tf_op jit(solution)/shard_map/add | solution.py:35
  345.2 11.1 %fusion.92 = f32[32,78,128]{2,1,0:T(8,128)S(1)} fusion(f32[3,46,78,128]{3,2,1,0:T(8,128)S(1)} %maximum_convert_fusion, f32[]{:T(128)} %bitcast.39, f32[]{:T(128)} %bitcast.38, f32[]{:T(128)} %bitcast.37, f32[]{:T(128)} %bitcast.36, f32[]{:T(128)} %bitcast.35, f32[]{:T(128)} %bitcast.34, f32[]{:T(128)} %bitcast.33, f32[]{:T(128)} %bitcast.32, f32[]{:T(128)} %bitcast.31, ...), kind=kLoop, calls=%fused_computation.333 | loop fusion | flops 9265152 | bytes 20447292 | tf_op jit(solution)/shard_map/add | solution.py:35
  356.3 11.0 %fusion.62 = f32[32,78,128]{2,1,0:T(8,128)S(1)} fusion(f32[3,46,78,128]{3,2,1,0:T(8,128)S(1)} %maximum_convert_fusion, f32[]{:T(128)} %bitcast.153, f32[]{:T(128)} %bitcast.152, f32[]{:T(128)} %bitcast.151, f32[]{:T(128)} %bitcast.150, f32[]{:T(128)} %bitcast.149, f32[]{:T(128)} %bitcast.148, f32[]{:T(128)} %bitcast.147, f32[]{:T(128)} %bitcast.146, ...), kind=kLoop, calls=%fused_computation.273 | loop fusion | flops 9265152 | bytes 20447292 | tf_op jit(solution)/shard_map/add | solution.py:35
  367.3 12.1 %fusion.77 = f32[32,78,128]{2,1,0:T(8,128)} fusion(f32[3,46,78,128]{3,2,1,0:T(8,128)S(1)} %maximum_convert_fusion, f32[]{:T(128)} %bitcast.96, f32[]{:T(128)} %bitcast.95, f32[]{:T(128)} %bitcast.94, f32[]{:T(128)} %bitcast.93, f32[]{:T(128)} %bitcast.92, f32[]{:T(128)} %bitcast.91, f32[]{:T(128)} %bitcast.90, f32[]{:T(128)} %bitcast.89, f32[]{:T(128)} %bitcast.88, ...), kind=kLoop, calls=%fused_computation.303 | loop fusion | flops 9265152 | bytes 20447292 | tf_op jit(solution)/shard_map/add | solution.py:35
  379.4 40.4 %fusion.529 = f32[32,64,128]{2,1,0:T(8,128)} fusion(f32[32,78,128]{2,1,0:T(8,128)S(1)} %fusion.62, f32[32,78,128]{2,1,0:T(8,128)} %fusion.77, f32[32,78,128]{2,1,0:T(8,128)S(1)} %fusion.92, f32[]{:T(128)} %bitcast.167, f32[]{:T(128)} %bitcast.166, f32[]{:T(128)} %bitcast.165, f32[]{:T(128)} %bitcast.164, f32[]{:T(128)} %bitcast.163, f32[]{:T(128)} %bitcast.162, ...), kind=kLoop, calls=%fused_computation.881 | loop fusion | flops 23330816 | bytes 48234676 | tf_op jit(solution)/shard_map/add | solution.py:170
  419.8 9.6 %multiply_add_fusion.6 = f32[128]{0:T(128)S(1)} fusion(f32[]{:T(128)} %bitcast.461, f32[]{:T(128)} %bitcast.460, f32[]{:T(128)} %bitcast.459, f32[]{:T(128)} %bitcast.458, f32[]{:T(128)} %bitcast.457, f32[]{:T(128)} %bitcast.456, f32[]{:T(128)} %bitcast.455, f32[]{:T(128)} %bitcast.454, f32[]{:T(128)} %bitcast.453, f32[]{:T(128)} %bitcast.452, ...), kind=kLoop, calls=%fused_computation.1591 | loop fusion | flops 3584 | bytes 1084 | tf_op jit(solution)/shard_map/add | solution.py:35
  429.4 9.6 %multiply_add_fusion.9 = f32[128]{0:T(128)S(1)} fusion(f32[]{:T(128)} %bitcast.323, f32[]{:T(128)} %bitcast.322, f32[]{:T(128)} %bitcast.321, f32[]{:T(128)} %bitcast.320, f32[]{:T(128)} %bitcast.319, f32[]{:T(128)} %bitcast.318, f32[]{:T(128)} %bitcast.317, f32[]{:T(128)} %bitcast.316, f32[]{:T(128)} %bitcast.315, f32[]{:T(128)} %bitcast.314, ...), kind=kLoop, calls=%fused_computation.1594 | loop fusion | flops 3584 | bytes 1084 | tf_op jit(solution)/shard_map/add | solution.py:35
  439.0 9.6 %fusion.753 = f32[32,78]{1,0:T(8,128)S(1)} fusion(f32[1,46,78]{2,1,0:T(8,128)S(1)} %get-tuple-element.36, f32[]{:T(128)} %bitcast.293, f32[]{:T(128)} %bitcast.292, f32[]{:T(128)} %bitcast.291, f32[]{:T(128)} %bitcast.290, f32[]{:T(128)} %bitcast.289, f32[]{:T(128)} %bitcast.288, f32[]{:T(128)} %bitcast.287, f32[]{:T(128)} %bitcast.286, f32[]{:T(128)} %bitcast.285, ...), kind=kLoop, calls=%fused_computation.1359 | loop fusion | flops 72384 | bytes 159804 | tf_op jit(solution)/shard_map/add | solution.py:35
  448.6 9.5 %fusion.738 = f32[32,64]{1,0:T(8,128)S(1)} fusion(f32[32,78]{1,0:T(8,128)S(1)} %fusion.753, f32[]{:T(128)} %bitcast.308, f32[]{:T(128)} %bitcast.307, f32[]{:T(128)} %bitcast.306, f32[]{:T(128)} %bitcast.305, f32[]{:T(128)} %bitcast.304, f32[]{:T(128)} %bitcast.303, f32[]{:T(128)} %bitcast.302, f32[]{:T(128)} %bitcast.301, f32[]{:T(128)} %bitcast.300, ...), kind=kLoop, calls=%fused_computation.1329 | loop fusion | flops 59392 | bytes 131132 | tf_op jit(solution)/shard_map/add | solution.py:35
  467.4 9.3 %fusion.767 = f32[32,64]{1,0:T(8,128)S(1)} fusion(f32[32,78]{1,0:T(8,128)S(1)} %fusion.782, f32[]{:T(128)} %bitcast.262, f32[]{:T(128)} %bitcast.261, f32[]{:T(128)} %bitcast.260, f32[]{:T(128)} %bitcast.259, f32[]{:T(128)} %bitcast.258, f32[]{:T(128)} %bitcast.257, f32[]{:T(128)} %bitcast.256, f32[]{:T(128)} %bitcast.255, f32[]{:T(128)} %bitcast.254, ...), kind=kLoop, calls=%fused_computation.1388 | loop fusion | flops 59392 | bytes 131132 | tf_op jit(solution)/shard_map/add | solution.py:35
  503.7 11.3 %multiply_add_fusion.2 = f32[32,78,128]{2,1,0:T(8,128)S(1)} fusion(f32[46,78,128]{2,1,0:T(8,128)S(1)} %maximum_convert_fusion.3, f32[]{:T(128)} %bitcast.39, f32[]{:T(128)} %bitcast.38, f32[]{:T(128)} %bitcast.37, f32[]{:T(128)} %bitcast.36, f32[]{:T(128)} %bitcast.35, f32[]{:T(128)} %bitcast.34, f32[]{:T(128)} %bitcast.33, f32[]{:T(128)} %bitcast.32, ...), kind=kLoop, calls=%fused_computation.363 | loop fusion | flops 9265152 | bytes 20447292 | tf_op jit(solution)/shard_map/add | solution.py:35
  515.0 11.2 %multiply_add_fusion.1 = f32[32,78,128]{2,1,0:T(8,128)S(1)} fusion(f32[46,78,128]{2,1,0:T(8,128)S(1)} %maximum_convert_fusion.3, f32[]{:T(128)} %bitcast.96, f32[]{:T(128)} %bitcast.95, f32[]{:T(128)} %bitcast.94, f32[]{:T(128)} %bitcast.93, f32[]{:T(128)} %bitcast.92, f32[]{:T(128)} %bitcast.91, f32[]{:T(128)} %bitcast.90, f32[]{:T(128)} %bitcast.89, ...), kind=kLoop, calls=%fused_computation.362 | loop fusion | flops 9265152 | bytes 20447292 | tf_op jit(solution)/shard_map/add | solution.py:35
  526.2 11.0 %multiply_add_fusion = f32[32,78,128]{2,1,0:T(8,128)S(1)} fusion(f32[46,78,128]{2,1,0:T(8,128)S(1)} %maximum_convert_fusion.3, f32[]{:T(128)} %bitcast.153, f32[]{:T(128)} %bitcast.152, f32[]{:T(128)} %bitcast.151, f32[]{:T(128)} %bitcast.150, f32[]{:T(128)} %bitcast.149, f32[]{:T(128)} %bitcast.148, f32[]{:T(128)} %bitcast.147, f32[]{:T(128)} %bitcast.146, ...), kind=kLoop, calls=%fused_computation.361 | loop fusion | flops 9265152 | bytes 20447292 | tf_op jit(solution)/shard_map/add | solution.py:35
  537.2 11.3 %fusion.514 = f32[32,64,128]{2,1,0:T(8,128)S(1)} fusion(f32[32,78,128]{2,1,0:T(8,128)S(1)} %multiply_add_fusion.2, f32[]{:T(128)} %bitcast.53, f32[]{:T(128)} %bitcast.52, f32[]{:T(128)} %bitcast.51, f32[]{:T(128)} %bitcast.50, f32[]{:T(128)} %bitcast.49, f32[]{:T(128)} %bitcast.48, f32[]{:T(128)} %bitcast.47, f32[]{:T(128)} %bitcast.46, f32[]{:T(128)} %bitcast.45, ...), kind=kLoop, calls=%fused_computation.851 | loop fusion | flops 7602176 | bytes 16777276 | tf_op jit(solution)/shard_map/add | solution.py:35
  548.5 13.4 %multiply_divide_fusion.3 = f32[32,64,128]{2,1,0:T(8,128)S(1)} fusion(f32[32,64,128]{2,1,0:T(8,128)S(1)} %copy-done.10, f32[32,64,128]{2,1,0:T(8,128)S(1)} %fusion.514, f32[]{:T(128)} %bitcast.67, f32[]{:T(128)} %bitcast.66, f32[]{:T(128)} %bitcast.65, f32[]{:T(128)} %bitcast.64, f32[]{:T(128)} %bitcast.63, f32[]{:T(128)} %bitcast.62, f32[]{:T(128)} %bitcast.61, ...), kind=kLoop, calls=%fused_computation.1064 | loop fusion | flops 8388608 | bytes 3153980 | tf_op jit(solution)/shard_map/div | solution.py:160
  561.9 13.1 %fusion.626 = bf16[1,32,64,128]{3,2,1,0:T(8,128)(2,1)S(1)} fusion(f32[32,64,128]{2,1,0:T(8,128)S(1)} %multiply_divide_fusion.3, f32[]{:T(128)} %bitcast.67, f32[]{:T(128)} %bitcast.66, f32[]{:T(128)} %bitcast.65, f32[]{:T(128)} %bitcast.64, f32[]{:T(128)} %bitcast.63, f32[]{:T(128)} %bitcast.62, f32[]{:T(128)} %bitcast.61, f32[]{:T(128)} %bitcast.60, ...), kind=kLoop, calls=%fused_computation.1083 | loop fusion | flops 7864320 | bytes 1572924 | tf_op jit(solution)/shard_map/stack | solution.py:162
  575.0 11.4 %fusion.486 = f32[32,64,128]{2,1,0:T(8,128)S(1)} fusion(f32[32,78,128]{2,1,0:T(8,128)S(1)} %multiply_add_fusion, f32[]{:T(128)} %bitcast.167, f32[]{:T(128)} %bitcast.166, f32[]{:T(128)} %bitcast.165, f32[]{:T(128)} %bitcast.164, f32[]{:T(128)} %bitcast.163, f32[]{:T(128)} %bitcast.162, f32[]{:T(128)} %bitcast.161, f32[]{:T(128)} %bitcast.160, ...), kind=kLoop, calls=%fused_computation.793 | loop fusion | flops 7602176 | bytes 16777276 | tf_op jit(solution)/shard_map/add | solution.py:35
  586.4 13.5 %multiply_divide_fusion.1 = f32[32,64,128]{2,1,0:T(8,128)S(1)} fusion(f32[32,64,128]{2,1,0:T(8,128)S(1)} %copy-done.9, f32[32,64,128]{2,1,0:T(8,128)S(1)} %fusion.486, f32[]{:T(128)} %bitcast.181, f32[]{:T(128)} %bitcast.180, f32[]{:T(128)} %bitcast.179, f32[]{:T(128)} %bitcast.178, f32[]{:T(128)} %bitcast.177, f32[]{:T(128)} %bitcast.176, f32[]{:T(128)} %bitcast.175, ...), kind=kLoop, calls=%fused_computation.1062 | loop fusion | flops 8388608 | bytes 3153980 | tf_op jit(solution)/shard_map/div | solution.py:160
  599.9 13.5 %fusion.628 = bf16[1,32,64,128]{3,2,1,0:T(8,128)(2,1)S(1)} fusion(f32[32,64,128]{2,1,0:T(8,128)S(1)} %multiply_divide_fusion.1, f32[]{:T(128)} %bitcast.181, f32[]{:T(128)} %bitcast.180, f32[]{:T(128)} %bitcast.179, f32[]{:T(128)} %bitcast.178, f32[]{:T(128)} %bitcast.177, f32[]{:T(128)} %bitcast.176, f32[]{:T(128)} %bitcast.175, f32[]{:T(128)} %bitcast.174, ...), kind=kLoop, calls=%fused_computation.1085 | loop fusion | flops 7864320 | bytes 1572924 | tf_op jit(solution)/shard_map/stack | solution.py:162
  613.4 11.0 %fusion.500 = f32[32,64,128]{2,1,0:T(8,128)S(1)} fusion(f32[32,78,128]{2,1,0:T(8,128)S(1)} %multiply_add_fusion.1, f32[]{:T(128)} %bitcast.110, f32[]{:T(128)} %bitcast.109, f32[]{:T(128)} %bitcast.108, f32[]{:T(128)} %bitcast.107, f32[]{:T(128)} %bitcast.106, f32[]{:T(128)} %bitcast.105, f32[]{:T(128)} %bitcast.104, f32[]{:T(128)} %bitcast.103, ...), kind=kLoop, calls=%fused_computation.822 | loop fusion | flops 7602176 | bytes 16777276 | tf_op jit(solution)/shard_map/add | solution.py:35
  624.4 13.5 %multiply_divide_fusion.2 = f32[32,64,128]{2,1,0:T(8,128)S(1)} fusion(f32[32,64,128]{2,1,0:T(8,128)S(1)} %copy-done.8, f32[32,64,128]{2,1,0:T(8,128)S(1)} %fusion.500, f32[]{:T(128)} %bitcast.124, f32[]{:T(128)} %bitcast.123, f32[]{:T(128)} %bitcast.122, f32[]{:T(128)} %bitcast.121, f32[]{:T(128)} %bitcast.120, f32[]{:T(128)} %bitcast.119, f32[]{:T(128)} %bitcast.118, ...), kind=kLoop, calls=%fused_computation.1063 | loop fusion | flops 8388608 | bytes 3153980 | tf_op jit(solution)/shard_map/div | solution.py:160
  637.9 13.2 %fusion.627 = bf16[1,32,64,128]{3,2,1,0:T(8,128)(2,1)S(1)} fusion(f32[32,64,128]{2,1,0:T(8,128)S(1)} %multiply_divide_fusion.2, f32[]{:T(128)} %bitcast.124, f32[]{:T(128)} %bitcast.123, f32[]{:T(128)} %bitcast.122, f32[]{:T(128)} %bitcast.121, f32[]{:T(128)} %bitcast.120, f32[]{:T(128)} %bitcast.119, f32[]{:T(128)} %bitcast.118, f32[]{:T(128)} %bitcast.117, ...), kind=kLoop, calls=%fused_computation.1084 | loop fusion | flops 7864320 | bytes 1572924 | tf_op jit(solution)/shard_map/stack | solution.py:162
  677.3 11.1 %fusion.47 = f32[32,78,128]{2,1,0:T(8,128)S(1)} fusion(f32[3,46,78,128]{3,2,1,0:T(8,128)S(1)} %maximum_convert_fusion.1, f32[]{:T(128)} %bitcast.39, f32[]{:T(128)} %bitcast.38, f32[]{:T(128)} %bitcast.37, f32[]{:T(128)} %bitcast.36, f32[]{:T(128)} %bitcast.35, f32[]{:T(128)} %bitcast.34, f32[]{:T(128)} %bitcast.33, f32[]{:T(128)} %bitcast.32, f32[]{:T(128)} %bitcast.31, ...), kind=kLoop, calls=%fused_computation.243 | loop fusion | flops 9265152 | bytes 20447292 | tf_op jit(solution)/shard_map/add | solution.py:35
  688.4 11.0 %fusion.17 = f32[32,78,128]{2,1,0:T(8,128)S(1)} fusion(f32[3,46,78,128]{3,2,1,0:T(8,128)S(1)} %maximum_convert_fusion.1, f32[]{:T(128)} %bitcast.153, f32[]{:T(128)} %bitcast.152, f32[]{:T(128)} %bitcast.151, f32[]{:T(128)} %bitcast.150, f32[]{:T(128)} %bitcast.149, f32[]{:T(128)} %bitcast.148, f32[]{:T(128)} %bitcast.147, f32[]{:T(128)} %bitcast.146, ...), kind=kLoop, calls=%fused_computation.183 | loop fusion | flops 9265152 | bytes 20447292 | tf_op jit(solution)/shard_map/add | solution.py:35
  699.4 12.1 %fusion.32 = f32[32,78,128]{2,1,0:T(8,128)} fusion(f32[3,46,78,128]{3,2,1,0:T(8,128)S(1)} %maximum_convert_fusion.1, f32[]{:T(128)} %bitcast.96, f32[]{:T(128)} %bitcast.95, f32[]{:T(128)} %bitcast.94, f32[]{:T(128)} %bitcast.93, f32[]{:T(128)} %bitcast.92, f32[]{:T(128)} %bitcast.91, f32[]{:T(128)} %bitcast.90, f32[]{:T(128)} %bitcast.89, f32[]{:T(128)} %bitcast.88, ...), kind=kLoop, calls=%fused_computation.213 | loop fusion | flops 9265152 | bytes 20447292 | tf_op jit(solution)/shard_map/add | solution.py:35
  711.5 40.4 %fusion.443 = f32[32,64,128]{2,1,0:T(8,128)} fusion(f32[32,78,128]{2,1,0:T(8,128)S(1)} %fusion.17, f32[32,78,128]{2,1,0:T(8,128)} %fusion.32, f32[32,78,128]{2,1,0:T(8,128)S(1)} %fusion.47, f32[]{:T(128)} %bitcast.167, f32[]{:T(128)} %bitcast.166, f32[]{:T(128)} %bitcast.165, f32[]{:T(128)} %bitcast.164, f32[]{:T(128)} %bitcast.163, f32[]{:T(128)} %bitcast.162, ...), kind=kLoop, calls=%fused_computation.705 | loop fusion | flops 23330816 | bytes 48234676 | tf_op jit(solution)/shard_map/add | solution.py:170
  751.8 18.0 %all-reduce.18.cloned.1.call-done = f32[32,64,128]{2,1,0:T(8,128)} async-done(((f32[32,64,128]{2,1,0:T(8,128)}), f32[32,64,128]{2,1,0:T(8,128)}) %all-reduce.18.cloned.1.call-update) | async-done | bytes 1048592 | tf_op jit(solution)/shard_map/psum | solution.py:171
  (141 shorter events, 146.2 us)
Async XLA Ops:
  6.5 8.2 %copy-start = (bf16[3,1,16,8,16,128]{5,4,3,2,1,0:T(8,128)(2,1)S(1)}, bf16[3,1,16,8,16,128]{5,4,3,2,1,0:T(8,128)(2,1)}, u32[]{:S(2)}) copy-start(bf16[3,1,16,8,16,128]{5,4,3,2,1,0:T(8,128)(2,1)} %param.6) | copy-start | bytes 4718596
  6.5 7.7 copy-start.13
  8.0 97.7 %collective-permute-start = (bf16[7,64,128]{2,1,0:T(8,128)(2,1)S(1)}, bf16[7,64,128]{2,1,0:T(8,128)(2,1)S(1)}, u32[]{:S(2)}, u32[]{:S(2)}) collective-permute-start(bf16[7,64,128]{2,1,0:T(8,128)(2,1)S(1)} %get-tuple-element.27), channel_id=1, source_target_pairs={{0,4},{4,8},{8,12},{1,5},{5,9},{9,13},{2,6},{6,10},{10,14},{3,7},{... | collective-permute-start | bytes 344072 | tf_op jit(solution)/shard_map/ppermute | solution.py:18
  12.9 92.8 %collective-permute-start.1 = (bf16[7,64,128]{2,1,0:T(8,128)(2,1)S(1)}, bf16[7,64,128]{2,1,0:T(8,128)(2,1)S(1)}, u32[]{:S(2)}, u32[]{:S(2)}) collective-permute-start(bf16[7,64,128]{2,1,0:T(8,128)(2,1)S(1)} %get-tuple-element.28), channel_id=1, source_target_pairs={{4,0},{8,4},{12,8},{5,1},{9,5},{13,9},{6,2},{10,6},{14,10},{7,3},{... | collective-permute-start | bytes 344072 | tf_op jit(solution)/shard_map/ppermute | solution.py:21
  18.1 6.1 copy-start.4
  18.1 16.6 %copy-start.11 = (s32[6,2,64]{2,1,0:T(2,128)S(1)}, s32[6,2,64]{2,1,0:T(2,128)}, u32[]{:S(2)}) copy-start(s32[6,2,64]{2,1,0:T(2,128)} %param.9) | copy-start | bytes 9220
  18.1 16.6 %copy-start.12 = (s32[6,2,64]{2,1,0:T(2,128)S(1)}, s32[6,2,64]{2,1,0:T(2,128)}, u32[]{:S(2)}) copy-start(s32[6,2,64]{2,1,0:T(2,128)} %param.8) | copy-start | bytes 9220
  18.1 171.5 %all-to-all-start = ((bf16[4,3,8,8,16,128]{5,2,4,3,1,0:T(8,128)(2,1)}), bf16[4,3,8,8,16,128]{5,2,4,3,1,0:T(8,128)(2,1)}, u32[]{:S(2)}, u32[]{:S(2)}) async-start(bf16[4,3,8,8,16,128]{5,2,4,3,1,0:T(8,128)(2,1)} %copy.20), calls=%async_computation | async-start | bytes 6291456 | tf_op jit(solution)/shard_map/all_to_all | solution.py:86
  24.2 452.6 %all-reduce.16.cloned.1.call-start = ((), (), s32[]{:S(2)}) async-start(), calls=%async_computation.1 | async-start | bytes 2097152 | tf_op jit(solution)/shard_map/psum | solution.py:171
  105.8 14.3 %collective-permute-start.2 = (bf16[46,7,128]{2,1,0:T(8,128)(2,1)S(1)}, bf16[46,7,128]{2,1,0:T(8,128)(2,1)S(1)}, u32[]{:S(2)}, u32[]{:S(2)}) collective-permute-start(bf16[46,7,128]{2,1,0:T(8,128)(2,1)S(1)} %get-tuple-element.23), channel_id=1, source_target_pairs={{0,2},{1,3},{4,6},{5,7},{8,10},{9,11},{12,14},{13,15},{16,18},{17,... | collective-permute-start | bytes 247304 | tf_op jit(solution)/shard_map/ppermute | solution.py:18
  109.2 10.9 %collective-permute-start.3 = (bf16[46,7,128]{2,1,0:T(8,128)(2,1)S(1)}, bf16[46,7,128]{2,1,0:T(8,128)(2,1)S(1)}, u32[]{:S(2)}, u32[]{:S(2)}) collective-permute-start(bf16[46,7,128]{2,1,0:T(8,128)(2,1)S(1)} %get-tuple-element.24), channel_id=1, source_target_pairs={{2,0},{3,1},{6,4},{7,5},{10,8},{11,9},{14,12},{15,13},{18,16},{19,... | collective-permute-start | bytes 247304 | tf_op jit(solution)/shard_map/ppermute | solution.py:21
  191.7 1.8 copy-start.7
  224.9 1.8 copy-start.6
  258.1 1.8 copy-start.5
  291.9 25.0 %collective-permute-start.4 = (bf16[3,7,64,128]{3,2,1,0:T(8,128)(2,1)S(1)}, bf16[3,7,64,128]{3,2,1,0:T(8,128)(2,1)S(1)}, u32[]{:S(2)}, u32[]{:S(2)}) collective-permute-start(bf16[3,7,64,128]{3,2,1,0:T(8,128)(2,1)S(1)} %get-tuple-element.19), channel_id=1, source_target_pairs={{0,4},{4,8},{8,12},{1,5},{5,9},{9,13},{2,6},{6,10},{10,14},{3,7},{... | collective-permute-start | bytes 1032200 | tf_op jit(solution)/shard_map/ppermute | solution.py:18
  295.8 21.0 %collective-permute-start.5 = (bf16[3,7,64,128]{3,2,1,0:T(8,128)(2,1)S(1)}, bf16[3,7,64,128]{3,2,1,0:T(8,128)(2,1)S(1)}, u32[]{:S(2)}, u32[]{:S(2)}) collective-permute-start(bf16[3,7,64,128]{3,2,1,0:T(8,128)(2,1)S(1)} %get-tuple-element.20), channel_id=1, source_target_pairs={{4,0},{8,4},{12,8},{5,1},{9,5},{13,9},{6,2},{10,6},{14,10},{7,3},{... | collective-permute-start | bytes 1032200 | tf_op jit(solution)/shard_map/ppermute | solution.py:21
  317.0 24.9 %collective-permute-start.6 = (bf16[3,46,7,128]{3,2,1,0:T(8,128)(2,1)S(1)}, bf16[3,46,7,128]{3,2,1,0:T(8,128)(2,1)S(1)}, u32[]{:S(2)}, u32[]{:S(2)}) collective-permute-start(bf16[3,46,7,128]{3,2,1,0:T(8,128)(2,1)S(1)} %get-tuple-element.15), channel_id=1, source_target_pairs={{0,2},{1,3},{4,6},{5,7},{8,10},{9,11},{12,14},{13,15},{16,18},{17,... | collective-permute-start | bytes 741896 | tf_op jit(solution)/shard_map/ppermute | solution.py:18
  321.6 20.3 %collective-permute-start.7 = (bf16[3,46,7,128]{3,2,1,0:T(8,128)(2,1)S(1)}, bf16[3,46,7,128]{3,2,1,0:T(8,128)(2,1)S(1)}, u32[]{:S(2)}, u32[]{:S(2)}) collective-permute-start(bf16[3,46,7,128]{3,2,1,0:T(8,128)(2,1)S(1)} %get-tuple-element.16), channel_id=1, source_target_pairs={{2,0},{3,1},{6,4},{7,5},{10,8},{11,9},{14,12},{15,13},{18,16},{19,... | collective-permute-start | bytes 741896 | tf_op jit(solution)/shard_map/ppermute | solution.py:21
  419.7 57.0 %copy-start.2 = (f32[32,64,128]{2,1,0:T(8,128)S(1)}, f32[32,64,128]{2,1,0:T(8,128)}, u32[]{:S(2)}) copy-start(f32[32,64,128]{2,1,0:T(8,128)} %param.11) | copy-start | bytes 3145732
  419.8 350.0 %all-reduce.18.cloned.1.call-start = ((), (), s32[]{:S(2)}) async-start(), calls=%async_computation.2 | async-start | bytes 2097152 | tf_op jit(solution)/shard_map/psum | solution.py:171
  481.1 6.9 collective-permute-start.8
  485.6 6.7 collective-permute-start.9
  492.3 6.7 collective-permute-start.10
  496.9 6.5 collective-permute-start.11
  537.2 11.3 %copy-start.10 = (f32[32,64,128]{2,1,0:T(8,128)S(1)}, f32[32,64,128]{2,1,0:T(8,128)}, u32[]{:S(2)}) copy-start(f32[32,64,128]{2,1,0:T(8,128)} %get-tuple-element.448) | copy-start | bytes 3145732
  575.0 11.4 %copy-start.9 = (f32[32,64,128]{2,1,0:T(8,128)S(1)}, f32[32,64,128]{2,1,0:T(8,128)}, u32[]{:S(2)}) copy-start(f32[32,64,128]{2,1,0:T(8,128)} %get-tuple-element.444) | copy-start | bytes 3145732
  613.4 11.0 %copy-start.8 = (f32[32,64,128]{2,1,0:T(8,128)S(1)}, f32[32,64,128]{2,1,0:T(8,128)}, u32[]{:S(2)}) copy-start(f32[32,64,128]{2,1,0:T(8,128)} %get-tuple-element.446) | copy-start | bytes 3145732
  651.2 8.1 %collective-permute-start.12 = (bf16[3,7,64,128]{3,2,1,0:T(8,128)(2,1)S(1)}, bf16[3,7,64,128]{3,2,1,0:T(8,128)(2,1)S(1)}, u32[]{:S(2)}, u32[]{:S(2)}) collective-permute-start(bf16[3,7,64,128]{3,2,1,0:T(8,128)(2,1)S(1)} %get-tuple-element.17), channel_id=1, source_target_pairs={{0,4},{4,8},{8,12},{1,5},{5,9},{9,13},{2,6},{6,10},{10,14},{3,7},{... | collective-permute-start | bytes 1032200 | tf_op jit(solution)/shard_map/ppermute | solution.py:18
  654.6 9.1 %collective-permute-start.13 = (bf16[3,7,64,128]{3,2,1,0:T(8,128)(2,1)S(1)}, bf16[3,7,64,128]{3,2,1,0:T(8,128)(2,1)S(1)}, u32[]{:S(2)}, u32[]{:S(2)}) collective-permute-start(bf16[3,7,64,128]{3,2,1,0:T(8,128)(2,1)S(1)} %get-tuple-element.18), channel_id=1, source_target_pairs={{4,0},{8,4},{12,8},{5,1},{9,5},{13,9},{6,2},{10,6},{14,10},{7,3},{... | collective-permute-start | bytes 1032200 | tf_op jit(solution)/shard_map/ppermute | solution.py:21
  663.8 5.6 collective-permute-start.14
  665.4 8.5 %collective-permute-start.15 = (bf16[3,46,7,128]{3,2,1,0:T(8,128)(2,1)S(1)}, bf16[3,46,7,128]{3,2,1,0:T(8,128)(2,1)S(1)}, u32[]{:S(2)}, u32[]{:S(2)}) collective-permute-start(bf16[3,46,7,128]{3,2,1,0:T(8,128)(2,1)S(1)} %get-tuple-element.14), channel_id=1, source_target_pairs={{2,0},{3,1},{6,4},{7,5},{10,8},{11,9},{14,12},{15,13},{18,16},{19,... | collective-permute-start | bytes 741896 | tf_op jit(solution)/shard_map/ppermute | solution.py:21
  751.8 18.0 %copy-start.3 = (f32[32,64,128]{2,1,0:T(8,128)S(1)}, f32[32,64,128]{2,1,0:T(8,128)}, u32[]{:S(2)}) copy-start(f32[32,64,128]{2,1,0:T(8,128)} %get-tuple-element.9) | copy-start | bytes 3145732
  769.8 4.4 copy-start.1
Sparse Core Ops, SparseCore 0:
  419.9 22.8 all-reduce.15
  752.0 17.7 all-reduce.17
where the time goes:
time: 795 us; the launch traced here: 782 us
  other arithmetic  595 us (75%)
  matrix products  61.7 us (8%)
  starting transfers between devices  47.3 us (6%)
  waiting for transfers between devices  43.6 us (5%)
  local copies, waits for them, and re-layouts  18.8 us (2%)
  between operations  14.8 us (2%)
    add x36, other arithmetic, valid_pass(): summed = weighted if summed is None else summed + weighted  375 us
    add x2, other arithmetic, shards(): partial_value = spread if partial_value is None else partial_value + spread  80.7 us
    another operation x6, other arithmetic, shards(): stacked = jnp.stack(ratios)  79.5 us
    dot_general x3, matrix products, shards(): jnp.einsum('skibz,skbj->ijz', stretched, place_y[view_index], preferred_e...  54.9 us
    div x3, other arithmetic, shards(): quotient = observed[view_index] / (blurred + soft_floor)  40.4 us
    ppermute x8, starting transfers between devices, extended(): lax.ppermute(lax.slice_in_dim(block, block.shape[dim] - width, None, axis...  30.9 us
    psum x2, waiting for transfers between devices, shards(): combined = lax.psum(partial_value, 'vert')  18 us
    ppermute x8, waiting for transfers between devices, extended(): lax.ppermute(lax.slice_in_dim(block, 0, width, axis=dim), axis, backward)  17.5 us
  transfers between devices with their start and end apart: 19, of which 9 were waited for; matrix products, arithmetic and copies ran while one was open for 33% of the time, Pallas kernels for 0%

commit v1 on v0

v1 whole, which is shorter than its diff:
```python
import functools

import jax
import jax.numpy as jnp
from jax import lax
from jax.experimental import pallas as pl
from jax.experimental.pallas import tpu as pltpu
from jax.sharding import PartitionSpec as P

ITERS = 2
HALO_Y = 8

soft_floor = 0.01
damping = 0.5


def split_high_low(matrix):
    high = lax.reduce_precision(matrix, 8, 7)
    return high.astype(jnp.bfloat16), (matrix - high).astype(jnp.bfloat16)


def banded(taps, difference):
    summed = None
    for tap_index in range(taps.shape[-1]):
        term = jnp.where(difference == tap_index, taps[..., tap_index, None, None], 0.0)
        summed = term if summed is None else summed + term
    return summed


def place_kernel(filled, corner_x, corner_y, tiles, observed, summed, counted):
    view = pl.program_id(0)
    sources, _, capacity, wide, tall, _ = tiles.shape
    block_y = observed.shape[2]
    summed[...] = jnp.zeros_like(summed)
    counted[...] = jnp.zeros_like(counted)
    for source in range(sources):

        @pl.loop(0, capacity)
        def _(slot):
            at = source * capacity + slot

            @pl.when(filled[view, at] > 0)
            def _():
                x = corner_x[view, at]
                y = corner_y[view, at]
                where = (pl.ds(x, wide), pl.ds(y, tall), slice(None))
                summed[where] = summed[where] + tiles[source, 0, slot].astype(jnp.float32)
                counted[where] = counted[where] + 1.0

    @pl.loop(0, observed.shape[1])
    def _(x):
        observed[0, x] = summed[x, :block_y, :] / jnp.maximum(counted[x, :block_y, :], 1.0)


def place(filled, corner_x, corner_y, arrived, block_x, block_y):
    sources, views, capacity, wide, tall, depth = arrived.shape
    return pl.pallas_call(
        place_kernel,
        out_shape=jax.ShapeDtypeStruct((views, block_x, block_y, depth), jnp.float32),
        grid_spec=pltpu.PrefetchScalarGridSpec(
            num_scalar_prefetch=3,
            grid=(views,),
            in_specs=[
                pl.BlockSpec(
                    (sources, 1, capacity, wide, tall, depth), lambda v, *_: (0, v, 0, 0, 0, 0)
                )
            ],
            out_specs=pl.BlockSpec((1, block_x, block_y, depth), lambda v, *_: (v, 0, 0, 0)),
            scratch_shapes=[
                pltpu.VMEM((block_x, block_y, depth), jnp.float32),
                pltpu.VMEM((block_x, block_y, depth), jnp.float32),
            ],
        ),
        compiler_params=pltpu.CompilerParams(vmem_limit_bytes=32 << 20),
    )(filled, corner_x, corner_y, arrived)


def sweep_kernel(
    sizes,
    taps_x,
    observed,
    initial,
    inverse_norm,
    along_y,
    back_y,
    along_z,
    back_z,
    estimate,
    est_center,
    est_low,
    est_high,
    send_low,
    send_high,
    passed_y,
    passed_z,
    acc_center,
    out_x,
    out_y,
    in_x,
    in_y,
    vert_out,
    vert_in,
    est_send,
    est_recv,
    acc_send,
    acc_recv,
    vert_send,
    vert_recv,
):
    count_x, count_y = sizes
    views, block_x, block_y, depth = observed.shape
    tap_count = taps_x.shape[1]
    radius = tap_count // 2
    extended_x = block_x + 2 * radius
    me_x = lax.axis_index("gx")
    me_y = lax.axis_index("gy")
    me_v = lax.axis_index("vert")
    bf16 = jnp.bfloat16
    f32 = jnp.float32

    directions = [
        (dx, dy)
        for dx in (-1, 0, 1)
        for dy in (-1, 0, 1)
        if (dx, dy) != (0, 0)
    ]

    def exists(dx, dy):
        good = None
        for step, me, count in ((dx, me_x, count_x), (dy, me_y, count_y)):
            if step == -1:
                test = me > 0
            elif step == 1:
                test = me < count - 1
            else:
                continue
            good = test if good is None else jnp.logical_and(good, test)
        return good

    def device(dx, dy):
        return {"gx": me_x + dx, "gy": me_y + dy}

    def span(step):
        if step == 0:
            return pl.ds(radius, block_x)
        if step == -1:
            return pl.ds(radius, radius)
        return pl.ds(block_x, radius)

    def ghost(step):
        if step == 0:
            return pl.ds(radius, block_x)
        if step == -1:
            return pl.ds(0, radius)
        return pl.ds(block_x + radius, radius)

    def part(step, offset):
        if step == 0:
            return pl.ds(0, block_x)
        if step == -1:
            return pl.ds(0, radius)
        return pl.ds(block_x - radius, radius)

    def est_copy(sweep, index, dx, dy):
        if dy == 0:
            src = est_center.at[sweep, span(dx)]
            dst = est_center.at[sweep, ghost(-dx)]
        elif dy == -1:
            src = send_low.at[sweep, part(dx, 0)]
            dst = est_high.at[sweep, ghost(-dx)]
        else:
            src = send_high.at[sweep, part(dx, 0)]
            dst = est_low.at[sweep, ghost(-dx)]
        return src, dst

    def acc_copy(sweep, index, dx, dy):
        if dy == 0:
            side = 0 if dx == -1 else 1
            return out_x.at[sweep, side], in_x.at[sweep, 1 - side]
        side = 0 if dy == -1 else 1
        return out_y.at[sweep, side, ghost(dx)], in_y.at[sweep, 1 - side, ghost(-dx)]

    def exchange(make, send_sem, recv_sem, sweep):
        def copy(index, dx, dy):
            src, dst = make(sweep, index, dx, dy)
            opposite = directions.index((-dx, -dy))
            return pltpu.make_async_remote_copy(
                src_ref=src,
                dst_ref=dst,
                send_sem=send_sem.at[sweep, index],
                recv_sem=recv_sem.at[sweep, opposite],
                device_id=device(dx, dy),
                device_id_type=pl.DeviceIdType.MESH,
            )

        def start():
            for index, (dx, dy) in enumerate(directions):

                @pl.when(exists(dx, dy))
                def _():
                    copy(index, dx, dy).start()

        def finish():
            for index, (dx, dy) in enumerate(directions):

                @pl.when(exists(dx, dy))
                def _():
                    copy(index, dx, dy).wait_send()
                    opposite = directions.index((-dx, -dy))
                    src, dst = make(sweep, opposite, -dx, -dy)
                    pltpu.make_async_remote_copy(
                        src_ref=src,
                        dst_ref=dst,
                        send_sem=send_sem.at[sweep, opposite],
                        recv_sem=recv_sem.at[sweep, index],
                        device_id=device(dx, dy),
                        device_id_type=pl.DeviceIdType.MESH,
                    ).wait_recv()

        return start, finish

    barrier = pltpu.get_barrier_semaphore()
    for dx, dy in directions:

        @pl.when(exists(dx, dy))
        def _():
            pl.semaphore_signal(
                barrier, inc=1, device_id=device(dx, dy), device_id_type=pl.DeviceIdType.MESH
            )

    pl.semaphore_signal(
        barrier, inc=1, device_id={"vert": 1 - me_v}, device_id_type=pl.DeviceIdType.MESH
    )

    def publish(sweep, x, plane):
        est_center[sweep, radius + x] = plane.astype(bf16)
        send_low[sweep, x] = plane[:HALO_Y].astype(bf16)
        send_high[sweep, x] = plane[block_y - HALO_Y :].astype(bf16)

    @pl.loop(0, block_x)
    def _(x):
        publish(0, x, initial[x])

    for sweep in range(ITERS):
        for step in (-1, 1):

            @pl.when(jnp.logical_not(exists(step, 0)))
            def _():
                planes = ghost(step)
                est_center[sweep, planes] = jnp.zeros((radius, block_y, depth), bf16)
                est_low[sweep, planes] = jnp.zeros((radius, HALO_Y, depth), bf16)
                est_high[sweep, planes] = jnp.zeros((radius, HALO_Y, depth), bf16)
                in_x[sweep, 0 if step == -1 else 1] = jnp.zeros((radius, block_y, depth), bf16)
                in_y[sweep, 0, planes] = jnp.zeros((radius, HALO_Y, depth), bf16)
                in_y[sweep, 1, planes] = jnp.zeros((radius, HALO_Y, depth), bf16)

            @pl.when(jnp.logical_not(exists(0, step)))
            def _():
                rows = est_low if step == -1 else est_high
                rows[sweep] = jnp.zeros((extended_x, HALO_Y, depth), bf16)
                in_y[sweep, 0 if step == -1 else 1] = jnp.zeros((extended_x, HALO_Y, depth), bf16)

    passed_z[:, : 2 * radius] = jnp.zeros((views, 2 * radius, block_y, depth), f32)
    passed_z[:, 2 * radius + block_x :] = jnp.zeros((views, 2 * radius, block_y, depth), f32)

    peers = 1
    for dx, dy in directions:
        peers = peers + exists(dx, dy).astype(jnp.int32)
    pl.semaphore_wait(barrier, peers)

    group = 4
    while block_x % group:
        group //= 2

    for sweep in range(ITERS):
        start, finish = exchange(est_copy, est_send, est_recv, sweep)
        start()
        finish()

        @pl.loop(0, extended_x // 2)
        def _(pair):
            columns = []
            for x in (2 * pair, 2 * pair + 1):
                edges = jnp.concatenate(
                    [est_low[sweep, x].astype(f32), est_high[sweep, x].astype(f32)], axis=0
                ).astype(bf16)
                columns.append(jnp.concatenate([est_center[sweep, x], edges], axis=0))
            both = jnp.concatenate(columns, axis=1)
            both = jnp.concatenate([both, both], axis=0)
            result = jnp.dot(along_y[...], both, preferred_element_type=f32)
            for view in range(views):
                rows = slice(view * block_y, (view + 1) * block_y)
                passed_y[view, 2 * pair] = result[rows, :depth]
                passed_y[view, 2 * pair + 1] = result[rows, depth:]

        for view in range(views):

            @pl.loop(0, block_x // group)
            def _(step):
                planes = []
                for inner in range(group):
                    x = step * group + inner
                    value = taps_x[view, 0] * passed_y[view, x]
                    for tap in range(1, tap_count):
                        value = value + taps_x[view, tap] * passed_y[view, x + tap]
                    planes.append(value.astype(bf16))
                stacked = jnp.concatenate(planes, axis=0)
                stacked = jnp.concatenate([stacked, stacked], axis=1)
                blurred = jnp.dot(stacked, along_z[view], preferred_element_type=f32)
                measured = observed[view, pl.ds(step * group, group)].reshape(
                    group * block_y, depth
                )
                quotient = (measured / (blurred + soft_floor)).astype(bf16)
                quotient = jnp.concatenate([quotient, quotient], axis=1)
                spread = jnp.dot(quotient, back_z[view], preferred_element_type=f32)
                passed_z[view, pl.ds(2 * radius + step * group, group)] = spread.reshape(
                    group, block_y, depth
                )

        @pl.loop(0, extended_x // 2)
        def _(pair):
            columns = []
            for x in (2 * pair, 2 * pair + 1):
                stack = []
                for view in range(views):
                    value = taps_x[view, 0] * passed_z[view, x + 2 * radius]
                    for tap in range(1, tap_count):
                        value = value + taps_x[view, tap] * passed_z[view, x + 2 * radius - tap]
                    stack.append(value.astype(bf16))
                columns.append(jnp.concatenate(stack, axis=0))
            both = jnp.concatenate(columns, axis=1)
            result = jnp.dot(back_y[...], both, preferred_element_type=f32)
            rows = block_y + 2 * HALO_Y
            result = result[:rows] + result[rows:]
            for side in range(2):
                x = 2 * pair + side
                lanes = slice(side * depth, (side + 1) * depth)
                acc_center[x] = result[:block_y, lanes]
                out_y[sweep, 0, x] = result[block_y : block_y + HALO_Y, lanes].astype(bf16)
                out_y[sweep, 1, x] = result[block_y + HALO_Y :, lanes].astype(bf16)

        @pl.loop(0, radius)
        def _(x):
            out_x[sweep, 0, x] = acc_center[x].astype(bf16)
            out_x[sweep, 1, x] = acc_center[radius + block_x + x].astype(bf16)

        start, finish = exchange(acc_copy, acc_send, acc_recv, sweep)
        start()
        finish()

        @pl.loop(0, radius)
        def _(x):
            low = radius + x
            high = block_x + x
            acc_center[low] = acc_center[low] + in_x[sweep, 0, x].astype(f32)
            acc_center[high] = acc_center[high] + in_x[sweep, 1, x].astype(f32)
            for side in range(2):
                rows = slice(0, HALO_Y) if side == 0 else slice(block_y - HALO_Y, block_y)
                acc_center[low, rows] = acc_center[low, rows] + in_y[sweep, side, x].astype(f32)
                acc_center[high, rows] = acc_center[high, rows] + in_y[
                    sweep, side, radius + block_x + x
                ].astype(f32)

        @pl.loop(0, block_x)
        def _(x):
            plane = acc_center[radius + x]
            low = plane[:HALO_Y] + in_y[sweep, 0, radius + x].astype(f32)
            high = plane[block_y - HALO_Y :] + in_y[sweep, 1, radius + x].astype(f32)
            vert_out[sweep, x] = jnp.concatenate(
                [low, plane[HALO_Y : block_y - HALO_Y], high], axis=0
            )

        vert = pltpu.make_async_remote_copy(
            src_ref=vert_out.at[sweep],
            dst_ref=vert_in.at[sweep],
            send_sem=vert_send.at[sweep],
            recv_sem=vert_recv.at[sweep],
            device_id={"vert": 1 - me_v},
            device_id_type=pl.DeviceIdType.MESH,
        )
        vert.start()
        vert.wait()

        @pl.loop(0, block_x)
        def _(x):
            before = initial[x] if sweep == 0 else estimate[x]
            combined = vert_out[sweep, x] + vert_in[sweep, x]
            after = before * (combined + damping) * inverse_norm[x]
            estimate[x] = after
            if sweep + 1 < ITERS:
                publish(sweep + 1, x, after)


def sweeps(sizes, taps_x, observed, initial, inverse_norm, along_y, back_y, along_z, back_z):
    views, block_x, block_y, depth = observed.shape
    radius = taps_x.shape[1] // 2
    extended_x = block_x + 2 * radius
    vmem = pl.BlockSpec(memory_space=pltpu.VMEM)
    bf16 = jnp.bfloat16
    f32 = jnp.float32
    return pl.pallas_call(
        functools.partial(sweep_kernel, sizes),
        out_shape=jax.ShapeDtypeStruct(initial.shape, f32),
        in_specs=[pl.BlockSpec(memory_space=pltpu.SMEM)] + [vmem] * 7,
        out_specs=vmem,
        scratch_shapes=[
            pltpu.VMEM((ITERS, extended_x, block_y, depth), bf16),
            pltpu.VMEM((ITERS, extended_x, HALO_Y, depth), bf16),
            pltpu.VMEM((ITERS, extended_x, HALO_Y, depth), bf16),
            pltpu.VMEM((ITERS, block_x, HALO_Y, depth), bf16),
            pltpu.VMEM((ITERS, block_x, HALO_Y, depth), bf16),
            pltpu.VMEM((views, extended_x, block_y, depth), f32),
            pltpu.VMEM((views, block_x + 4 * radius, block_y, depth), f32),
            pltpu.VMEM((extended_x, block_y, depth), f32),
            pltpu.VMEM((ITERS, 2, radius, block_y, depth), bf16),
            pltpu.VMEM((ITERS, 2, extended_x, HALO_Y, depth), bf16),
            pltpu.VMEM((ITERS, 2, radius, block_y, depth), bf16),
            pltpu.VMEM((ITERS, 2, extended_x, HALO_Y, depth), bf16),
            pltpu.VMEM((ITERS, block_x, block_y, depth), f32),
            pltpu.VMEM((ITERS, block_x, block_y, depth), f32),
            pltpu.SemaphoreType.DMA((ITERS, 8)),
            pltpu.SemaphoreType.DMA((ITERS, 8)),
            pltpu.SemaphoreType.DMA((ITERS, 8)),
            pltpu.SemaphoreType.DMA((ITERS, 8)),
            pltpu.SemaphoreType.DMA((ITERS,)),
            pltpu.SemaphoreType.DMA((ITERS,)),
        ],
        compiler_params=pltpu.CompilerParams(
            collective_id=0, has_side_effects=True, vmem_limit_bytes=48 << 20
        ),
    )(taps_x, observed, initial, inverse_norm, along_y, back_y, along_z, back_z)


def shards(tiles, tile_block, tile_x, tile_y, psf, initial):
    column_count = lax.axis_size("gx")
    column_index = lax.axis_index("gx")
    row_index = lax.axis_index("gy")
    core_index = lax.axis_index("vert")
    local_views = tiles.shape[0]
    all_views = psf.shape[0]
    per_device = tiles.shape[2]
    tile_wide = tiles.shape[3]
    tile_tall = tiles.shape[4]
    block_x, block_y, depth = initial.shape
    capacity = max(2, 2 * per_device // column_count)
    radius = psf.shape[2] // 2
    first_view = core_index * local_views
    mine_psf = lax.dynamic_slice_in_dim(psf, first_view, local_views, 0)

    def my_rows(table):
        chosen = lax.dynamic_slice_in_dim(table, first_view, local_views, 0)
        chosen = lax.dynamic_slice_in_dim(chosen, row_index, 1, 1)[:, 0]
        return chosen.reshape(local_views, column_count, per_device)

    targets = my_rows(tile_block[:, :, :, 0])
    offsets_x = my_rows(tile_x)
    offsets_y = my_rows(tile_y)
    columns_iota = jnp.arange(column_count, dtype=jnp.int32)
    hits = (targets[..., None] == columns_iota).astype(jnp.int32)
    ranks = jnp.cumsum(hits, axis=2, dtype=jnp.int32)
    slot_ids = jnp.arange(capacity, dtype=jnp.int32) + 1
    sent_hits = jnp.swapaxes(lax.dynamic_slice_in_dim(hits, column_index, 1, 1)[:, 0], 1, 2)
    sent_ranks = jnp.swapaxes(lax.dynamic_slice_in_dim(ranks, column_index, 1, 1)[:, 0], 1, 2)
    chooser = sent_hits[:, :, None, :] * (
        sent_ranks[:, :, None, :] == slot_ids[None, None, :, None]
    ).astype(jnp.int32)
    outgoing = jnp.einsum(
        "vgkj,vjabz->gvkabz",
        chooser.astype(jnp.bfloat16),
        tiles[:, 0],
        preferred_element_type=jnp.bfloat16,
    )
    arrived = lax.all_to_all(outgoing, "gx", split_axis=0, concat_axis=0, tiled=True)
    from_hits = lax.dynamic_slice_in_dim(hits, column_index, 1, 3)[..., 0]
    from_ranks = lax.dynamic_slice_in_dim(ranks, column_index, 1, 3)[..., 0]
    picks = from_hits[:, :, None, :] * (
        from_ranks[:, :, None, :] == slot_ids[None, None, :, None]
    ).astype(jnp.int32)
    filled = jnp.sum(picks, axis=3).reshape(local_views, -1)
    corner_x = jnp.sum(picks * offsets_x[:, :, None, :], axis=3).reshape(local_views, -1)
    corner_y = jnp.sum(picks * offsets_y[:, :, None, :], axis=3).reshape(local_views, -1)
    observed = place(filled, corner_x, corner_y, arrived, block_x, block_y)

    row_iota = jnp.arange(tile_block.shape[1], dtype=jnp.int32)
    global_x = (tile_block[..., 0] * block_x + tile_x).reshape(all_views, -1)
    global_y = (row_iota[None, :, None] * block_y + tile_y).reshape(all_views, -1)
    near_x = jnp.arange(block_x + 2 * radius, dtype=jnp.int32) - radius
    near_y = jnp.arange(block_y + 2 * radius, dtype=jnp.int32) - radius
    cells_x = column_index * block_x + near_x
    cells_y = row_index * block_y + near_y
    cover_x = (
        (cells_x >= global_x[..., None]) & (cells_x < global_x[..., None] + tile_wide)
    ).astype(jnp.bfloat16)
    cover_y = (
        (cells_y >= global_y[..., None]) & (cells_y < global_y[..., None] + tile_tall)
    ).astype(jnp.bfloat16)
    counts = jnp.einsum("vti,vtj->vij", cover_x, cover_y, preferred_element_type=jnp.float32)
    coverage = jnp.minimum(counts, 1.0)
    iota_x = jnp.arange(block_x, dtype=jnp.int32)
    iota_y = jnp.arange(block_y, dtype=jnp.int32)
    iota_z = jnp.arange(depth, dtype=jnp.int32)
    adjoint_x = banded(psf[:, 0], iota_x[:, None] - near_x[None, :] + radius)
    adjoint_y = banded(psf[:, 1], iota_y[:, None] - near_y[None, :] + radius)
    exact = lax.Precision.HIGHEST
    spread = jnp.einsum("vij,vyj->viy", coverage, adjoint_y, precision=exact)
    spread = jnp.einsum("vxi,viy->vxy", adjoint_x, spread, precision=exact)
    profile = jnp.sum(banded(psf[:, 2], iota_z[:, None] - iota_z[None, :] + radius), axis=2)
    norm_field = jnp.einsum("vxy,vz->xyz", spread, profile, precision=exact)
    inverse_norm = 1.0 / (norm_field + damping)

    places_y = jnp.concatenate(
        [
            iota_y,
            jnp.arange(HALO_Y, dtype=jnp.int32) - HALO_Y,
            jnp.arange(HALO_Y, dtype=jnp.int32) + block_y,
        ]
    )
    band_y = banded(mine_psf[:, 1], places_y[None, :] - iota_y[:, None] + radius)
    high, low = split_high_low(band_y)
    flat = (local_views * block_y, places_y.shape[0])
    along_y = jnp.concatenate([high.reshape(flat), low.reshape(flat)], axis=1)
    back_y = jnp.concatenate([high.reshape(flat).T, low.reshape(flat).T], axis=0)
    band_z = banded(mine_psf[:, 2], iota_z[:, None] - iota_z[None, :] + radius)
    along_z = jnp.concatenate(split_high_low(band_z), axis=1)
    back_z = jnp.concatenate(split_high_low(jnp.swapaxes(band_z, 1, 2)), axis=1)
    return sweeps(
        (column_count, lax.axis_size("gy")),
        mine_psf[:, 0],
        observed,
        initial,
        inverse_norm,
        along_y,
        back_y,
        along_z,
        back_z,
    )


def solution(mesh):
    in_specs = (
        P("vert", "gy", ("groups", "gx"), None, None, None),
        P(None, None, "groups", None),
        P(None, None, "groups"),
        P(None, None, "groups"),
        P(),
        P(("groups", "gx"), "gy", None),
    )
    out_specs = P(("groups", "gx"), "gy", None)
    return jax.shard_map(shards, mesh=mesh, in_specs=in_specs, out_specs=out_specs, check_vma=False)
```

time: 795 us -> 161 us (0.20); the launches traced: 782 us -> 161 us
  other arithmetic: 595 us -> 3.71 us
  Pallas kernels: 0 us -> 75.4 us
  matrix products: 61.7 us -> 5.5 us
  starting transfers between devices: 47.3 us -> 6.46 us
  between operations: 14.8 us -> 0.63 us
  waiting for transfers between devices: 43.6 us -> 55.2 us
    add x42 -> x3, other arithmetic: 456 us -> 0.02 us  [the longest x1 0.01 us: shards(): cells_x = column_index * block_x + near_x]
    another operation x6 -> x0, other arithmetic: 79.5 us -> none  [shards(): stacked = jnp.stack(ratios)]
    pallas_call x0 -> x2, Pallas kernels: none -> 75.4 us  [the longest x1 69.8 us: sweeps(): pl.pallas_call(functools.partial(sweep_kernel, sizes), out_shape=jax.Shap...]
    dot_general x6 -> x3, matrix products: 60.2 us -> 4.05 us  [the longest x1 2.81 us: shards(): norm_field = jnp.einsum('vxy,vz->xyz', spread, profile, precision=exact)]
    all_to_all x1, waiting for transfers between devices: 0.01 us -> 55.2 us  [shards(): lax.all_to_all(outgoing, 'gx', split_axis=0, concat_axis=0, tiled=True)]
    div x4 -> x0, other arithmetic: 44.8 us -> none  [the longest x3 40.4 us: shards(): quotient = observed[view_index] / (blurred + soft_floor)]
    ppermute x16 -> x0, starting transfers between devices: 41.2 us -> none  [the longest x8 30.9 us: extended(): lax.ppermute(lax.slice_in_dim(block, block.shape[dim] - width, None, axis...]
    ppermute x16 -> x0, waiting for transfers between devices: 25.6 us -> none  [the longest x8 17.5 us: extended(): lax.ppermute(lax.slice_in_dim(block, 0, width, axis=dim), axis, backward)]
  transfers between devices with their start and end apart: 19 -> 1, of which waited for: 9 -> 1; matrix products, arithmetic and copies ran while one was open for 33% -> 9% of each run, Pallas kernels for 0% -> 0%
where the time goes in v1:
time: 161 us
  Pallas kernels  75.4 us (47%)
  waiting for transfers between devices  55.2 us (34%)
  local copies, waits for them, and re-layouts  13.6 us (8%)
  starting transfers between devices  6.46 us (4%)
  matrix products  5.5 us (3%)
  other arithmetic  3.71 us (2%)
    pallas_call x1, Pallas kernels, sweeps(): pl.pallas_call(functools.partial(sweep_kernel, sizes), out_shape=jax.Shap...  69.8 us
    all_to_all x1, waiting for transfers between devices, shards(): lax.all_to_all(outgoing, 'gx', split_axis=0, concat_axis=0, tiled=True)  55.2 us
    all_to_all x1, starting transfers between devices, shards(): lax.all_to_all(outgoing, 'gx', split_axis=0, concat_axis=0, tiled=True)  6.46 us
    pallas_call x1, Pallas kernels, place(): pl.pallas_call(place_kernel, out_shape=jax.ShapeDtypeStruct((views, block...  5.59 us
    broadcast_in_dim x60, local copies, waits for them, and re-layouts, banded(): jnp.where(difference == tap_index, taps[..., tap_index, None, None], 0.0)  3.97 us
  transfers between devices with their start and end apart: 1, of which 1 were waited for; matrix products, arithmetic and copies ran while one was open for 9% of the time, Pallas kernels for 0%

profile of v1, /device:TPU:0, one launch (start us, length us, event | category | flops | bytes accessed | tf_op | source)
XLA Modules:
  0.0 160.5 jit_solution(4790191701253314833)
XLA Ops:
  0.0 0.8 fusion.227
  0.8 0.1 eq.439
  0.9 0.1 copy.38
  1.1 0.1 reduce_window_sum.11
  1.2 0.1 copy.39
  1.3 0.1 copy-done
  1.4 1.2 fusion
  2.6 2.6 %copy.84 = bf16[3,4,8,8,16,128]{5,4,3,2,0,1:T(8,128)(2,1)} copy(bf16[3,4,8,8,16,128]{5,2,4,3,1,0:T(8,128)(2,1)S(1)} %fusion) | data formatting | bytes 6291456 | tf_op jit(solution)/shard_map/vgkj,vjabz->gvkabz/dot_general | solution.py:467
  5.2 6.5 %all-to-all-start = ((bf16[4,3,8,8,16,128]{5,4,3,2,1,0:T(8,128)(2,1)}), bf16[4,3,8,8,16,128]{5,4,3,2,1,0:T(8,128)(2,1)}, u32[]{:S(2)}, u32[]{:S(2)}) async-start(bf16[4,3,8,8,16,128]{5,4,3,2,1,0:T(8,128)(2,1)} %bitcast.61), calls=%async_computation | async-start | bytes 6291456 | tf_op jit(solution)/shard_map/all_to_all | solution.py:473
  11.7 0.4 dynamic-slice_reduce_fusion
  12.6 0.8 fusion.141
  13.4 0.1 reshape.204.filled
  13.7 0.4 slice_reduce_fusion.74
  14.4 0.1 broadcast_in_dim.1149
  14.7 0.1 broadcast_in_dim.1161
  16.6 0.1 copy.47
  16.8 0.1 copy.48
  16.9 0.1 copy.49
  17.0 0.1 copy.50
  17.1 0.1 copy.51
  17.3 0.1 copy.52
  17.4 0.1 copy.53
  17.5 0.1 copy.54
  17.6 0.1 copy.55
  17.7 0.1 copy.56
  17.9 0.1 copy.57
  18.0 0.1 copy.58
  18.1 0.1 copy.59
  18.2 0.1 copy.60
  18.4 0.1 copy.61
  18.5 0.2 reduce-precision_convert_fusion.2
  18.7 0.1 copy.62.along_y
  19.1 0.4 slice_reduce_fusion.59
  19.7 0.4 slice_reduce_fusion.29
  20.1 0.4 slice_reduce_fusion.44
  20.5 0.4 slice_reduce_fusion.14
  21.0 0.4 reduce-precision_convert_fusion.1
  21.5 0.4 reduce-precision_convert_fusion
  22.1 0.3 convolution_minimum_fusion
  22.4 0.8 fusion.8
  23.1 0.5 fusion.61
  23.6 0.8 add_reduce_fusion
  24.4 2.8 %fusion.2.inverse_norm = f32[32,64,128]{2,1,0:T(8,128)} fusion(f32[6,32,64]{2,1,0:T(8,128)S(1)} %fusion.61, f32[6,128]{1,0:T(8,128)S(1)} %add_reduce_fusion), kind=kOutput, calls=%fused_computation.4 | convolution fusion | flops 19398656 | bytes 1100800 | tf_op jit(solution)/shard_map/vxy,vz->xyz/dot_general | solution.py:508
  27.3 55.2 %all-to-all-done.tiles = bf16[4,3,8,8,16,128]{5,4,3,2,1,0:T(8,128)(2,1)} async-done(((bf16[4,3,8,8,16,128]{5,4,3,2,1,0:T(8,128)(2,1)}), bf16[4,3,8,8,16,128]{5,4,3,2,1,0:T(8,128)(2,1)}, u32[]{:S(2)}, u32[]{:S(2)}) %all-to-all-start) | async-done | bytes 3145760 | tf_op jit(solution)/shard_map/all_to_all | solution.py:473
  82.4 5.6 %shard_map.64.observed = f32[3,32,64,128]{3,2,1,0:T(8,128)S(1)} custom-call(s32[3,32]{1,0:T(4,128)S(1)} %reshape.204.filled, s32[3,32]{1,0:T(4,128)S(1)} %reshape.205.corner_x, s32[3,32]{1,0:T(4,128)S(1)} %reshape.206.corner_y, bf16[4,3,8,8,16,128]{5,4,3,2,1,0:T(8,128)(2,1)} %all-to-all-done.tiles), custom_call_target="tpu_custom_call" | custom-call | tf_op jit(solution)/shard_map/pallas_call | solution.py:57
  88.0 1.7 %copy-done.1 = f32[3,32,64,128]{3,2,1,0:T(8,128)} copy-done((f32[3,32,64,128]{3,2,1,0:T(8,128)}, f32[3,32,64,128]{3,2,1,0:T(8,128)S(1)}, u32[]{:S(2)}) %copy-start.1) | copy-done | bytes 3145752
  89.7 69.8 %shard_map.65 = f32[32,64,128]{2,1,0:T(8,128)S(1)} custom-call(f32[3,15]{1,0:T(4,128)S(1)} %bitcast.60, f32[3,32,64,128]{3,2,1,0:T(8,128)} %copy-done.1, f32[32,64,128]{2,1,0:T(8,128)S(1)} %copy-done.2, f32[32,64,128]{2,1,0:T(8,128)S(1)} %copy-done.3, bf16[192,160]{1,0:T(8,128)(2,1)S(1)} %copy.62.along_y, bf16[160,192]{1,0:T(8,128)(2,1)S(1)} %pad_maximum_fusion.3.back_y, ...), custom_call_target="tpu_custom_call" | custom-call | tf_op jit(solution)/shard_map/pallas_call | solution.py:401
  159.5 1.0 copy.88
  (113 shorter events, 3.9 us)
Async XLA Ops:
  0.0 1.4 copy-start
  5.2 7.2 %copy-start.5 = (s32[6,2,64]{2,1,0:T(2,128)S(1)}, s32[6,2,64]{2,1,0:T(2,128)}, u32[]{:S(2)}) copy-start(s32[6,2,64]{2,1,0:T(2,128)} %param.9) | copy-start | bytes 9220
  5.2 7.2 %copy-start.6 = (s32[6,2,64]{2,1,0:T(2,128)S(1)}, s32[6,2,64]{2,1,0:T(2,128)}, u32[]{:S(2)}) copy-start(s32[6,2,64]{2,1,0:T(2,128)} %param.8) | copy-start | bytes 9220
  5.2 8.5 %copy-start.4 = (f32[6,3,15]{2,1,0:T(4,128)S(1)}, f32[6,3,15]{2,1,0:T(4,128)}, u32[]{:S(2)}) copy-start(f32[6,3,15]{2,1,0:T(4,128)} %param.10) | copy-start | bytes 3244
  5.2 13.8 %copy-start.7 = (s32[6,2,64,1]{2,3,1,0:T(1,128)S(1)}, s32[6,2,64,1]{2,3,1,0:T(1,128)}, u32[]{:S(2)}) copy-start(s32[6,2,64,1]{2,3,1,0:T(1,128)} %param.7) | copy-start | bytes 9220
  5.2 77.2 %all-to-all-start = ((bf16[4,3,8,8,16,128]{5,4,3,2,1,0:T(8,128)(2,1)}), bf16[4,3,8,8,16,128]{5,4,3,2,1,0:T(8,128)(2,1)}, u32[]{:S(2)}, u32[]{:S(2)}) async-start(bf16[4,3,8,8,16,128]{5,4,3,2,1,0:T(8,128)(2,1)} %bitcast.61), calls=%async_computation | async-start | bytes 6291456 | tf_op jit(solution)/shard_map/all_to_all | solution.py:473
  27.3 62.4 %copy-start.2 = (f32[32,64,128]{2,1,0:T(8,128)S(1)}, f32[32,64,128]{2,1,0:T(8,128)}, u32[]{:S(2)}) copy-start(f32[32,64,128]{2,1,0:T(8,128)} %initial.1) | copy-start | bytes 3145732
  82.4 7.3 %copy-start.3 = (f32[32,64,128]{2,1,0:T(8,128)S(1)}, f32[32,64,128]{2,1,0:T(8,128)}, u32[]{:S(2)}) copy-start(f32[32,64,128]{2,1,0:T(8,128)} %fusion.2.inverse_norm) | copy-start | bytes 3145732
  88.0 1.7 %copy-start.1 = (f32[3,32,64,128]{3,2,1,0:T(8,128)}, f32[3,32,64,128]{3,2,1,0:T(8,128)S(1)}, u32[]{:S(2)}) copy-start(f32[3,32,64,128]{3,2,1,0:T(8,128)S(1)} %shard_map.64.observed) | copy-start | bytes 9437188

commit v2 on v0

v2 whole, which is shorter than its diff:
```python
import functools

import jax
import jax.numpy as jnp
from jax import lax
from jax.experimental import pallas as pl
from jax.experimental.pallas import tpu as pltpu
from jax.sharding import PartitionSpec as P

ITERS = 2
HALO_Y = 8

soft_floor = 0.01
damping = 0.5


def split_high_low(matrix):
    high = lax.reduce_precision(matrix, 8, 7)
    return high.astype(jnp.bfloat16), (matrix - high).astype(jnp.bfloat16)


def banded(taps, difference):
    summed = None
    for tap_index in range(taps.shape[-1]):
        term = jnp.where(difference == tap_index, taps[..., tap_index, None, None], 0.0)
        summed = term if summed is None else summed + term
    return summed


class Links:
    def __init__(self, sizes, radius, block_x):
        self.radius = radius
        self.block_x = block_x
        self.me = (lax.axis_index("gx"), lax.axis_index("gy"))
        self.sizes = sizes
        self.directions = [
            (dx, dy) for dx in (-1, 0, 1) for dy in (-1, 0, 1) if (dx, dy) != (0, 0)
        ]

    def exists(self, dx, dy):
        good = None
        for step, me, count in zip((dx, dy), self.me, self.sizes):
            if step == 0:
                continue
            test = me > 0 if step == -1 else me < count - 1
            good = test if good is None else jnp.logical_and(good, test)
        return good

    def device(self, dx, dy):
        return {"gx": self.me[0] + dx, "gy": self.me[1] + dy}

    def greet(self, others=()):
        barrier = pltpu.get_barrier_semaphore()
        for dx, dy in self.directions:

            @pl.when(self.exists(dx, dy))
            def _():
                pl.semaphore_signal(
                    barrier,
                    inc=1,
                    device_id=self.device(dx, dy),
                    device_id_type=pl.DeviceIdType.MESH,
                )

        for other in others:
            pl.semaphore_signal(
                barrier, inc=1, device_id=other, device_id_type=pl.DeviceIdType.MESH
            )

    def await_greetings(self, others=0):
        peers = others
        for dx, dy in self.directions:
            peers = peers + self.exists(dx, dy).astype(jnp.int32)
        pl.semaphore_wait(pltpu.get_barrier_semaphore(), peers)

    def span(self, step):
        if step == 0:
            return pl.ds(self.radius, self.block_x)
        return pl.ds(self.radius if step == -1 else self.block_x, self.radius)

    def ghost(self, step):
        if step == 0:
            return pl.ds(self.radius, self.block_x)
        return pl.ds(0 if step == -1 else self.block_x + self.radius, self.radius)

    def part(self, step):
        if step == 0:
            return pl.ds(0, self.block_x)
        return pl.ds(0 if step == -1 else self.block_x - self.radius, self.radius)

    def exchange(self, make, send_sem, recv_sem):
        def copy(index, dx, dy):
            src, dst = make(dx, dy)
            return pltpu.make_async_remote_copy(
                src_ref=src,
                dst_ref=dst,
                send_sem=send_sem.at[index],
                recv_sem=recv_sem.at[index],
                device_id=self.device(dx, dy),
                device_id_type=pl.DeviceIdType.MESH,
            )

        for index, (dx, dy) in enumerate(self.directions):

            @pl.when(self.exists(dx, dy))
            def _():
                copy(index, dx, dy).start()

        for index, (dx, dy) in enumerate(self.directions):

            @pl.when(self.exists(dx, dy))
            def _():
                copy(index, dx, dy).wait_send()

            @pl.when(self.exists(-dx, -dy))
            def _():
                copy(index, dx, dy).wait_recv()


def ghosts_of_estimate(links, center, low, high, send_low, send_high):
    def make(dx, dy):
        if dy == 0:
            return center.at[links.span(dx)], center.at[links.ghost(-dx)]
        if dy == -1:
            return send_low.at[links.part(dx)], high.at[links.ghost(-dx)]
        return send_high.at[links.part(dx)], low.at[links.ghost(-dx)]

    return make


def ghosts_of_sums(links, out_x, out_y, in_x, in_y):
    def make(dx, dy):
        if dy == 0:
            side = 0 if dx == -1 else 1
            return out_x.at[side], in_x.at[1 - side]
        side = 0 if dy == -1 else 1
        return out_y.at[side, links.ghost(dx)], in_y.at[1 - side, links.ghost(-dx)]

    return make


def clear_missing(links, center, low, high):
    radius = links.radius
    for step in (-1, 1):

        @pl.when(jnp.logical_not(links.exists(step, 0)))
        def _():
            for rows in (center, low, high):
                rows[links.ghost(step)] = jnp.zeros((radius,) + rows.shape[1:], rows.dtype)

        @pl.when(jnp.logical_not(links.exists(0, step)))
        def _():
            rows = low if step == -1 else high
            rows[...] = jnp.zeros(rows.shape, rows.dtype)

    tail = links.block_x + 2 * radius
    for rows in (center, low, high):
        rows[tail:] = jnp.zeros((rows.shape[0] - tail,) + rows.shape[1:], rows.dtype)


def publish(links, center, send_low, send_high, x, plane):
    center[links.radius + x] = plane.astype(jnp.bfloat16)
    send_low[x] = plane[:HALO_Y].astype(jnp.bfloat16)
    send_high[x] = plane[plane.shape[0] - HALO_Y :].astype(jnp.bfloat16)


def pass_along_y(center, low, high, along_y, passed_y, views):
    block_y, depth = center.shape[1:]

    @pl.loop(0, center.shape[0] // 4)
    def _(step):
        for first in (4 * step, 4 * step + 2):
            columns = []
            for x in (first, first + 1):
                edges = jnp.concatenate(
                    [low[x].astype(jnp.float32), high[x].astype(jnp.float32)], axis=0
                ).astype(jnp.bfloat16)
                columns.append(jnp.concatenate([center[x], edges], axis=0))
            both = jnp.concatenate(columns, axis=1)
            both = jnp.concatenate([both, both], axis=0)
            result = jnp.dot(along_y[...], both, preferred_element_type=jnp.float32)
            for view in range(views):
                rows = slice(view * block_y, (view + 1) * block_y)
                passed_y[view, first] = result[rows, :depth]
                passed_y[view, first + 1] = result[rows, depth:]


def pass_along_xz(taps_x, passed_y, along_z, view, first, group):
    planes = []
    for inner in range(group):
        x = first + inner
        value = taps_x[view, 0] * passed_y[view, x]
        for tap in range(1, taps_x.shape[1]):
            value = value + taps_x[view, tap] * passed_y[view, x + tap]
        planes.append(value.astype(jnp.bfloat16))
    stacked = jnp.concatenate(planes, axis=0)
    stacked = jnp.concatenate([stacked, stacked], axis=1)
    return jnp.dot(stacked, along_z, preferred_element_type=jnp.float32)


def spread_quotient(measured, blurred, back_z):
    quotient = (measured / (blurred + soft_floor)).astype(jnp.bfloat16)
    quotient = jnp.concatenate([quotient, quotient], axis=1)
    return jnp.dot(quotient, back_z, preferred_element_type=jnp.float32)


def group_of(block_x):
    group = 4
    while block_x % group:
        group //= 2
    return group


def blur_kernel(
    sizes,
    taps_x,
    initial,
    along_y,
    along_z,
    blurred,
    center,
    low,
    high,
    send_low,
    send_high,
    passed_y,
    send_sem,
    recv_sem,
):
    views, block_x, block_y, depth = blurred.shape
    links = Links(sizes, taps_x.shape[1] // 2, block_x)
    links.greet()

    @pl.loop(0, block_x)
    def _(x):
        publish(links, center, send_low, send_high, x, initial[x])

    clear_missing(links, center, low, high)
    links.await_greetings()
    links.exchange(
        ghosts_of_estimate(links, center, low, high, send_low, send_high), send_sem, recv_sem
    )
    pass_along_y(center, low, high, along_y, passed_y, views)
    group = group_of(block_x)

    @pl.loop(0, block_x // group)
    def _(step):
        for view in range(views):
            value = pass_along_xz(taps_x, passed_y, along_z[view], view, step * group, group)
            blurred[view, pl.ds(step * group, group)] = value.reshape(group, block_y, depth)


def estimate_scratch(planes, block_x, block_y, depth):
    return [
        pltpu.VMEM((planes, block_y, depth), jnp.bfloat16),
        pltpu.VMEM((planes, HALO_Y, depth), jnp.bfloat16),
        pltpu.VMEM((planes, HALO_Y, depth), jnp.bfloat16),
        pltpu.VMEM((block_x, HALO_Y, depth), jnp.bfloat16),
        pltpu.VMEM((block_x, HALO_Y, depth), jnp.bfloat16),
    ]


def planes_of(block_x, radius):
    return -(-(block_x + 2 * radius) // 4) * 4


def first_blur(sizes, taps_x, initial, along_y, along_z):
    block_x, block_y, depth = initial.shape
    views = taps_x.shape[0]
    planes = planes_of(block_x, taps_x.shape[1] // 2)
    vmem = pl.BlockSpec(memory_space=pltpu.VMEM)
    shape = (views, block_x, block_y, depth)
    return pl.pallas_call(
        functools.partial(blur_kernel, sizes),
        out_shape=jax.ShapeDtypeStruct(shape, jnp.float32),
        in_specs=[pl.BlockSpec(memory_space=pltpu.SMEM)] + [vmem] * 3,
        out_specs=vmem,
        scratch_shapes=estimate_scratch(planes, block_x, block_y, depth)
        + [
            pltpu.VMEM((views, planes, block_y, depth), jnp.float32),
            pltpu.SemaphoreType.DMA((8,)),
            pltpu.SemaphoreType.DMA((8,)),
        ],
        cost_estimate=pl.CostEstimate(
            flops=20_000_000_000, bytes_accessed=40_000_000, transcendentals=0
        ),
        compiler_params=pltpu.CompilerParams(
            collective_id=0, has_side_effects=True, vmem_limit_bytes=32 << 20
        ),
    )(taps_x, initial, along_y, along_z)


def place_kernel(
    filled, corner_x, corner_y, tiles, blurred, back_z, observed, spread, summed, counted
):
    sources, capacity, wide, tall, depth = tiles.shape
    block_x, block_y = observed.shape[:2]
    summed[...] = jnp.zeros_like(summed)
    counted[...] = jnp.zeros_like(counted)

    @pl.loop(0, sources)
    def _(source):
        @pl.loop(0, capacity)
        def _(slot):
            at = source * capacity + slot

            @pl.when(filled[at] > 0)
            def _():
                x = corner_x[at]
                y = corner_y[at]
                where = (pl.ds(x, wide), pl.ds(y, tall), slice(None))
                summed[where] = summed[where] + tiles[source, slot].astype(jnp.float32)
                counted[where] = counted[where] + 1.0

    group = group_of(block_x)

    @pl.loop(0, block_x // group)
    def _(step):
        planes = pl.ds(step * group, group)
        measured = summed[planes] / jnp.maximum(counted[planes], 1.0)
        observed[planes] = measured
        flat = (group * block_y, depth)
        result = spread_quotient(
            measured.reshape(flat), blurred[0, planes].reshape(flat), back_z[0]
        )
        spread[planes] = result.reshape(group, block_y, depth)


def place(view, filled, corner_x, corner_y, arrived, blurred, back_z):
    _, block_x, block_y, depth = blurred.shape
    shape = (block_x, block_y, depth)

    def whole(shape):
        return pl.BlockSpec(shape, lambda i, *_: (0,) * len(shape))

    return pl.pallas_call(
        place_kernel,
        out_shape=[jax.ShapeDtypeStruct(shape, jnp.float32)] * 2,
        grid_spec=pltpu.PrefetchScalarGridSpec(
            num_scalar_prefetch=3,
            grid=(1,),
            in_specs=[
                whole(arrived.shape),
                pl.BlockSpec((1,) + shape, lambda i, *_: (view, 0, 0, 0)),
                pl.BlockSpec((1,) + back_z.shape[1:], lambda i, *_: (view, 0, 0)),
            ],
            out_specs=[whole(shape)] * 2,
            scratch_shapes=[pltpu.VMEM(shape, jnp.float32)] * 2,
        ),
        cost_estimate=pl.CostEstimate(
            flops=1_000_000_000, bytes_accessed=8_000_000, transcendentals=0
        ),
        compiler_params=pltpu.CompilerParams(vmem_limit_bytes=24 << 20),
    )(filled, corner_x, corner_y, arrived, blurred, back_z)


def sweep_kernel(sizes, views, *refs):
    taps_x = refs[0]
    observed = refs[1 : 1 + views]
    spreads = refs[1 + views : 1 + 2 * views]
    initial, inverse_norm, along_y, back_y, along_z, back_z, estimate = refs[
        1 + 2 * views : 8 + 2 * views
    ]
    (
        center,
        low,
        high,
        send_low,
        send_high,
        passed_y,
        passed_z,
        acc,
        out_x,
        out_y,
        in_x,
        in_y,
        vert_out,
        vert_in,
        est_send,
        est_recv,
        acc_send,
        acc_recv,
        vert_send,
        vert_recv,
    ) = refs[8 + 2 * views :]
    block_x, block_y, depth = initial.shape
    tap_count = taps_x.shape[1]
    radius = tap_count // 2
    planes = center.shape[1]
    bf16 = jnp.bfloat16
    f32 = jnp.float32
    links = Links(sizes, radius, block_x)
    partner = {"vert": 1 - lax.axis_index("vert")}
    links.greet((partner,))
    for sweep in range(ITERS):
        if sweep > 0:
            at = sweep - 1
            clear_missing(links, center.at[at], low.at[at], high.at[at])
        for step in (-1, 1):
            side = 0 if step == -1 else 1

            @pl.when(jnp.logical_not(links.exists(step, 0)))
            def _():
                in_x[sweep, side] = jnp.zeros(in_x.shape[2:], bf16)
                for other in range(2):
                    in_y[sweep, other, links.ghost(step)] = jnp.zeros(
                        (radius,) + in_y.shape[3:], bf16
                    )

            @pl.when(jnp.logical_not(links.exists(0, step)))
            def _():
                in_y[sweep, side] = jnp.zeros(in_y.shape[2:], bf16)

    below = 2 * radius
    beyond = passed_z.shape[1] - below - block_x
    passed_z[:, :below] = jnp.zeros((views, below, block_y, depth), f32)
    passed_z[:, below + block_x :] = jnp.zeros((views, beyond, block_y, depth), f32)
    group = group_of(block_x)

    @pl.loop(0, block_x)
    def _(x):
        for view in range(views):
            passed_z[view, below + x] = spreads[view][x]

    for sweep in range(ITERS):
        if sweep > 0:
            at = sweep - 1
            links.exchange(
                ghosts_of_estimate(
                    links, center.at[at], low.at[at], high.at[at], send_low.at[at], send_high.at[at]
                ),
                est_send.at[at],
                est_recv.at[at],
            )
            pass_along_y(center.at[at], low.at[at], high.at[at], along_y, passed_y, views)

            @pl.loop(0, block_x // group)
            def _(step):
                first = step * group
                for view in range(views):
                    blurred = pass_along_xz(taps_x, passed_y, along_z[view], view, first, group)
                    measured = observed[view][pl.ds(first, group)].reshape(blurred.shape)
                    result = spread_quotient(measured, blurred, back_z[view])
                    passed_z[view, pl.ds(below + first, group)] = result.reshape(
                        group, block_y, depth
                    )

        @pl.loop(0, planes // 4)
        def _(step):
            for first in (4 * step, 4 * step + 2):
                columns = []
                for x in (first, first + 1):
                    stack = []
                    for view in range(views):
                        value = taps_x[view, 0] * passed_z[view, x + below]
                        for tap in range(1, tap_count):
                            value = value + taps_x[view, tap] * passed_z[view, x + below - tap]
                        stack.append(value.astype(bf16))
                    columns.append(jnp.concatenate(stack, axis=0))
                both = jnp.concatenate(columns, axis=1)
                result = jnp.dot(back_y[...], both, preferred_element_type=f32)
                rows = block_y + 2 * HALO_Y
                result = result[:rows] + result[rows:]
                for side in range(2):
                    x = first + side
                    lanes = slice(side * depth, (side + 1) * depth)
                    acc[x] = result[:block_y, lanes]
                    out_y[sweep, 0, x] = result[block_y : block_y + HALO_Y, lanes].astype(bf16)
                    out_y[sweep, 1, x] = result[block_y + HALO_Y :, lanes].astype(bf16)

        @pl.loop(0, radius)
        def _(x):
            out_x[sweep, 0, x] = acc[x].astype(bf16)
            out_x[sweep, 1, x] = acc[radius + block_x + x].astype(bf16)

        if sweep == 0:
            links.await_greetings(1)
        links.exchange(
            ghosts_of_sums(
                links, out_x.at[sweep], out_y.at[sweep], in_x.at[sweep], in_y.at[sweep]
            ),
            acc_send.at[sweep],
            acc_recv.at[sweep],
        )

        @pl.loop(0, radius)
        def _(x):
            for side, at, beside in ((0, radius + x, x), (1, block_x + x, radius + block_x + x)):
                plane = acc[at] + in_x[sweep, side, x].astype(f32)
                first = plane[:HALO_Y] + in_y[sweep, 0, beside].astype(f32)
                last = plane[block_y - HALO_Y :] + in_y[sweep, 1, beside].astype(f32)
                acc[at] = jnp.concatenate(
                    [first, plane[HALO_Y : block_y - HALO_Y], last], axis=0
                )

        @pl.loop(0, block_x)
        def _(x):
            plane = acc[radius + x]
            first = plane[:HALO_Y] + in_y[sweep, 0, radius + x].astype(f32)
            last = plane[block_y - HALO_Y :] + in_y[sweep, 1, radius + x].astype(f32)
            vert_out[sweep, x] = jnp.concatenate(
                [first, plane[HALO_Y : block_y - HALO_Y], last], axis=0
            )

        vert = pltpu.make_async_remote_copy(
            src_ref=vert_out.at[sweep],
            dst_ref=vert_in.at[sweep],
            send_sem=vert_send.at[sweep],
            recv_sem=vert_recv.at[sweep],
            device_id=partner,
            device_id_type=pl.DeviceIdType.MESH,
        )
        vert.start()
        vert.wait()

        @pl.loop(0, block_x)
        def _(x):
            before = initial[x] if sweep == 0 else estimate[x]
            combined = vert_out[sweep, x] + vert_in[sweep, x]
            after = before * (combined + damping) * inverse_norm[x]
            estimate[x] = after
            if sweep + 1 < ITERS:
                publish(
                    links, center.at[sweep], send_low.at[sweep], send_high.at[sweep], x, after
                )


def sweeps(
    sizes, taps_x, observed, spreads, initial, inverse_norm, along_y, back_y, along_z, back_z
):
    block_x, block_y, depth = initial.shape
    views = len(observed)
    radius = taps_x.shape[1] // 2
    planes = planes_of(block_x, radius)
    vmem = pl.BlockSpec(memory_space=pltpu.VMEM)
    bf16 = jnp.bfloat16
    f32 = jnp.float32
    repeats = ITERS - 1
    return pl.pallas_call(
        functools.partial(sweep_kernel, sizes, views),
        out_shape=jax.ShapeDtypeStruct(initial.shape, f32),
        in_specs=[pl.BlockSpec(memory_space=pltpu.SMEM)] + [vmem] * (6 + 2 * views),
        out_specs=vmem,
        scratch_shapes=[
            pltpu.VMEM((repeats,) + scratch.shape, scratch.dtype)
            for scratch in estimate_scratch(planes, block_x, block_y, depth)
        ]
        + [
            pltpu.VMEM((views, planes, block_y, depth), f32),
            pltpu.VMEM((views, planes + 2 * radius, block_y, depth), f32),
            pltpu.VMEM((planes, block_y, depth), f32),
            pltpu.VMEM((ITERS, 2, radius, block_y, depth), bf16),
            pltpu.VMEM((ITERS, 2, planes, HALO_Y, depth), bf16),
            pltpu.VMEM((ITERS, 2, radius, block_y, depth), bf16),
            pltpu.VMEM((ITERS, 2, planes, HALO_Y, depth), bf16),
            pltpu.VMEM((ITERS, block_x, block_y, depth), f32),
            pltpu.VMEM((ITERS, block_x, block_y, depth), f32),
            pltpu.SemaphoreType.DMA((repeats, 8)),
            pltpu.SemaphoreType.DMA((repeats, 8)),
            pltpu.SemaphoreType.DMA((ITERS, 8)),
            pltpu.SemaphoreType.DMA((ITERS, 8)),
            pltpu.SemaphoreType.DMA((ITERS,)),
            pltpu.SemaphoreType.DMA((ITERS,)),
        ],
        compiler_params=pltpu.CompilerParams(
            collective_id=1, has_side_effects=True, vmem_limit_bytes=52 << 20
        ),
    )(taps_x, *observed, *spreads, initial, inverse_norm, along_y, back_y, along_z, back_z)


def shards(tiles, tile_block, tile_x, tile_y, psf, initial):
    column_count = lax.axis_size("gx")
    column_index = lax.axis_index("gx")
    row_index = lax.axis_index("gy")
    core_index = lax.axis_index("vert")
    local_views = tiles.shape[0]
    all_views = psf.shape[0]
    per_device = tiles.shape[2]
    tile_wide = tiles.shape[3]
    tile_tall = tiles.shape[4]
    block_x, block_y, depth = initial.shape
    capacity = max(2, 2 * per_device // column_count)
    radius = psf.shape[2] // 2
    first_view = core_index * local_views
    mine_psf = lax.dynamic_slice_in_dim(psf, first_view, local_views, 0)

    def my_rows(table):
        chosen = lax.dynamic_slice_in_dim(table, first_view, local_views, 0)
        chosen = lax.dynamic_slice_in_dim(chosen, row_index, 1, 1)[:, 0]
        return chosen.reshape(local_views, column_count, per_device)

    targets = my_rows(tile_block[:, :, :, 0])
    offsets_x = my_rows(tile_x)
    offsets_y = my_rows(tile_y)
    columns_iota = jnp.arange(column_count, dtype=jnp.int32)
    hits = (targets[..., None] == columns_iota).astype(jnp.int32)
    ranks = jnp.cumsum(hits, axis=2, dtype=jnp.int32)
    slot_ids = jnp.arange(capacity, dtype=jnp.int32) + 1
    sent_hits = jnp.swapaxes(lax.dynamic_slice_in_dim(hits, column_index, 1, 1)[:, 0], 1, 2)
    sent_ranks = jnp.swapaxes(lax.dynamic_slice_in_dim(ranks, column_index, 1, 1)[:, 0], 1, 2)
    chooser = sent_hits[:, :, None, :] * (
        sent_ranks[:, :, None, :] == slot_ids[None, None, :, None]
    ).astype(jnp.int32)
    chooser = chooser.astype(jnp.bfloat16)
    arrived = []
    for view in range(local_views):
        outgoing = jnp.einsum(
            "gkj,jabz->gkabz",
            chooser[view],
            tiles[view, 0],
            preferred_element_type=jnp.bfloat16,
        )
        arrived.append(lax.all_to_all(outgoing, "gx", split_axis=0, concat_axis=0, tiled=True))
    from_hits = lax.dynamic_slice_in_dim(hits, column_index, 1, 3)[..., 0]
    from_ranks = lax.dynamic_slice_in_dim(ranks, column_index, 1, 3)[..., 0]
    picks = from_hits[:, :, None, :] * (
        from_ranks[:, :, None, :] == slot_ids[None, None, :, None]
    ).astype(jnp.int32)
    filled = jnp.sum(picks, axis=3).reshape(local_views, -1)
    corner_x = jnp.sum(picks * offsets_x[:, :, None, :], axis=3).reshape(local_views, -1)
    corner_y = jnp.sum(picks * offsets_y[:, :, None, :], axis=3).reshape(local_views, -1)

    row_iota = jnp.arange(tile_block.shape[1], dtype=jnp.int32)
    global_x = (tile_block[..., 0] * block_x + tile_x).reshape(all_views, -1)
    global_y = (row_iota[None, :, None] * block_y + tile_y).reshape(all_views, -1)
    near_x = jnp.arange(block_x + 2 * radius, dtype=jnp.int32) - radius
    near_y = jnp.arange(block_y + 2 * radius, dtype=jnp.int32) - radius
    cells_x = column_index * block_x + near_x
    cells_y = row_index * block_y + near_y
    cover_x = (
        (cells_x >= global_x[..., None]) & (cells_x < global_x[..., None] + tile_wide)
    ).astype(jnp.bfloat16)
    cover_y = (
        (cells_y >= global_y[..., None]) & (cells_y < global_y[..., None] + tile_tall)
    ).astype(jnp.bfloat16)
    counts = jnp.einsum("vti,vtj->vij", cover_x, cover_y, preferred_element_type=jnp.float32)
    coverage = jnp.minimum(counts, 1.0)
    iota_x = jnp.arange(block_x, dtype=jnp.int32)
    iota_y = jnp.arange(block_y, dtype=jnp.int32)
    iota_z = jnp.arange(depth, dtype=jnp.int32)
    adjoint_x = banded(psf[:, 0], iota_x[:, None] - near_x[None, :] + radius)
    adjoint_y = banded(psf[:, 1], iota_y[:, None] - near_y[None, :] + radius)
    exact = lax.Precision.HIGHEST
    spread = jnp.einsum("vij,vyj->viy", coverage, adjoint_y, precision=exact)
    spread = jnp.einsum("vxi,viy->vxy", adjoint_x, spread, precision=exact)
    profile = jnp.sum(banded(psf[:, 2], iota_z[:, None] - iota_z[None, :] + radius), axis=2)
    norm_field = jnp.einsum("vxy,vz->xyz", spread, profile, precision=exact)
    inverse_norm = 1.0 / (norm_field + damping)

    places_y = jnp.concatenate(
        [
            iota_y,
            jnp.arange(HALO_Y, dtype=jnp.int32) - HALO_Y,
            jnp.arange(HALO_Y, dtype=jnp.int32) + block_y,
        ]
    )
    band_y = banded(mine_psf[:, 1], places_y[None, :] - iota_y[:, None] + radius)
    high, low = split_high_low(band_y)
    flat = (local_views * block_y, places_y.shape[0])
    along_y = jnp.concatenate([high.reshape(flat), low.reshape(flat)], axis=1)
    back_y = jnp.concatenate([high.reshape(flat).T, low.reshape(flat).T], axis=0)
    band_z = banded(mine_psf[:, 2], iota_z[:, None] - iota_z[None, :] + radius)
    along_z = jnp.concatenate(split_high_low(band_z), axis=1)
    back_z = jnp.concatenate(split_high_low(jnp.swapaxes(band_z, 1, 2)), axis=1)
    sizes = (column_count, lax.axis_size("gy"))
    taps_x = mine_psf[:, 0]
    blurred = first_blur(sizes, taps_x, initial, along_y, along_z)
    placed = [
        place(
            view, filled[view], corner_x[view], corner_y[view], arrived[view], blurred, back_z
        )
        for view in range(local_views)
    ]
    observed, spreads = zip(*placed)
    return sweeps(
        sizes,
        taps_x,
        observed,
        spreads,
        initial,
        inverse_norm,
        along_y,
        back_y,
        along_z,
        back_z,
    )


def solution(mesh):
    in_specs = (
        P("vert", "gy", ("groups", "gx"), None, None, None),
        P(None, None, "groups", None),
        P(None, None, "groups"),
        P(None, None, "groups"),
        P(),
        P(("groups", "gx"), "gy", None),
    )
    out_specs = P(("groups", "gx"), "gy", None)
    return jax.shard_map(shards, mesh=mesh, in_specs=in_specs, out_specs=out_specs, check_vma=False)
```

time: 795 us -> 169 us (0.21); the launches traced: 782 us -> 169 us
  other arithmetic: 595 us -> 11.4 us
  Pallas kernels: 0 us -> 86.2 us
  matrix products: 61.7 us -> 7.95 us
  starting transfers between devices: 47.3 us -> 14.4 us
  waiting for transfers between devices: 43.6 us -> 13.7 us
  local copies, waits for them, and re-layouts: 18.8 us -> 33.1 us
  between operations: 14.8 us -> 2 us
    add x42 -> x3, other arithmetic: 456 us -> 1.11 us  [the longest x1 0.59 us: shards(): cells_y = row_index * block_y + near_y]
    pallas_call x0 -> x5, Pallas kernels: none -> 86.2 us  [the longest x1 53.1 us: sweeps(): pl.pallas_call(functools.partial(sweep_kernel, sizes, views), out_shape=j...]
    another operation x6 -> x0, other arithmetic: 79.5 us -> none  [shards(): stacked = jnp.stack(ratios)]
    dot_general x7 -> x6, matrix products: 61.4 us -> 6.99 us  [the longest x1 2.83 us: shards(): norm_field = jnp.einsum('vxy,vz->xyz', spread, profile, precision=exact)]
    div x4 -> x0, other arithmetic: 44.8 us -> none  [the longest x3 40.4 us: shards(): quotient = observed[view_index] / (blurred + soft_floor)]
    ppermute x16 -> x0, starting transfers between devices: 41.2 us -> none  [the longest x8 30.9 us: extended(): lax.ppermute(lax.slice_in_dim(block, block.shape[dim] - width, None, axis...]
    ppermute x16 -> x0, waiting for transfers between devices: 25.6 us -> none  [the longest x8 17.5 us: extended(): lax.ppermute(lax.slice_in_dim(block, 0, width, axis=dim), axis, backward)]
    psum x2 -> x0, waiting for transfers between devices: 18 us -> none  [shards(): combined = lax.psum(partial_value, 'vert')]
  transfers between devices with their start and end apart: 19 -> 3, of which waited for: 9 -> 2; matrix products, arithmetic and copies ran while one was open for 33% -> 21% of each run, Pallas kernels for 0% -> 17%
where the time goes in v2:
time: 169 us
  Pallas kernels  86.2 us (51%)
  local copies, waits for them, and re-layouts  33.1 us (20%)
  starting transfers between devices  14.4 us (9%)
  waiting for transfers between devices  13.7 us (8%)
  other arithmetic  11.4 us (7%)
  matrix products  7.95 us (5%)
  between operations  2 us (1%)
    pallas_call x1, Pallas kernels, sweeps(): pl.pallas_call(functools.partial(sweep_kernel, sizes, views), out_shape=j...  53.1 us
    pallas_call x1, Pallas kernels, first_blur(): pl.pallas_call(functools.partial(blur_kernel, sizes), out_shape=jax.Shape...  23.9 us
    all_to_all x3, starting transfers between devices, shards(): lax.all_to_all(outgoing, 'gx', split_axis=0, concat_axis=0, tiled=True)  14.4 us
    all_to_all x3, waiting for transfers between devices, shards(): lax.all_to_all(outgoing, 'gx', split_axis=0, concat_axis=0, tiled=True)  13.7 us
    unnamed x236, local copies, waits for them, and re-layouts  10.1 us
    pallas_call x3, Pallas kernels, place(): pl.pallas_call(place_kernel, out_shape=[jax.ShapeDtypeStruct(shape, jnp.f...  9.22 us
    broadcast_in_dim x60, local copies, waits for them, and re-layouts, banded(): jnp.where(difference == tap_index, taps[..., tap_index, None, None], 0.0)  3.97 us
    slice x5, local copies, waits for them, and re-layouts, banded(): taps[..., tap_index, None, None]  3.78 us
  transfers between devices with their start and end apart: 3, of which 2 were waited for; matrix products, arithmetic and copies ran while one was open for 21% of the time, Pallas kernels for 17%

profile of v2, /device:TPU:0, one launch (start us, length us, event | category | flops | bytes accessed | tf_op | source)
XLA Modules:
  0.0 168.6 jit_solution(12795766825350501667)
XLA Ops:
  0.0 0.7 fusion.221
  1.6 0.7 fusion.222
  2.5 2.5 %fusion.226 = (bf16[1,1,16,8,16,128]{5,4,3,2,1,0:T(8,128)(2,1)S(1)}, bf16[1,1,16,8,16,128]{5,4,3,2,1,0:T(8,128)(2,1)S(1)}, bf16[1,1,16,8,16,128]{5,4,3,2,1,0:T(8,128)(2,1)}) fusion(bf16[3,1,16,8,16,128]{5,4,3,2,1,0:T(8,128)(2,1)} %param.6), kind=kLoop, calls=%fused_computation.362 | loop fusion | bytes 3145728 | tf_op jit(solution)/shard_map/slice | solution.py:610
  5.0 0.8 fusion.142
  6.2 1.2 copy.71
  7.5 6.5 %all-to-all-start.2 = ((bf16[4,8,8,16,128]{4,3,2,1,0:T(8,128)(2,1)}), bf16[4,8,8,16,128]{4,3,2,1,0:T(8,128)(2,1)S(1)}, u32[]{:S(2)}, u32[]{:S(2)}) async-start(bf16[4,8,8,16,128]{4,3,2,1,0:T(8,128)(2,1)} %copy.71), calls=%async_computation.2 | async-start | bytes 2097152 | tf_op jit(solution)/shard_map/all_to_all | solution.py:613
  23.6 1.0 slice_reduce_fusion.29
  24.7 1.0 slice_reduce_fusion.44
  25.7 1.0 slice_reduce_fusion.14
  26.9 0.6 pad_maximum_fusion.3.refs_10_
  28.1 1.2 copy.69
  29.5 0.6 fusion.228
  30.7 0.7 fusion.219
  31.5 1.1 reduce-precision_convert_fusion
  32.6 0.7 fusion.8
  33.8 5.8 %all-to-all-done.2.tiles = bf16[4,8,8,16,128]{4,3,2,1,0:T(8,128)(2,1)S(1)} async-done(((bf16[4,8,8,16,128]{4,3,2,1,0:T(8,128)(2,1)}), bf16[4,8,8,16,128]{4,3,2,1,0:T(8,128)(2,1)S(1)}, u32[]{:S(2)}, u32[]{:S(2)}) %all-to-all-start.2) | async-done | bytes 1048608 | tf_op jit(solution)/shard_map/all_to_all | solution.py:613
  39.6 3.7 %all-to-all-start.1 = ((bf16[4,8,8,16,128]{4,3,2,1,0:T(8,128)(2,1)}), bf16[4,8,8,16,128]{4,3,2,1,0:T(8,128)(2,1)S(1)}, u32[]{:S(2)}, u32[]{:S(2)}) async-start(bf16[4,8,8,16,128]{4,3,2,1,0:T(8,128)(2,1)} %copy.69), calls=%async_computation.1 | async-start | bytes 2097152 | tf_op jit(solution)/shard_map/all_to_all | solution.py:613
  43.9 0.7 copy.67.along_y.refs_9_
  45.2 0.7 squeeze.87.corner_x
  45.9 0.7 squeeze.88.corner_y
  46.6 0.6 squeeze.82.corner_x
  47.2 0.7 squeeze.83.corner_y
  47.9 1.2 copy.51
  49.3 0.6 squeeze.74.corner_y
  50.0 1.0 pad_maximum_fusion.1.back_z.refs_12_
  51.0 0.7 fusion.188
  51.7 1.0 convolution_minimum_fusion
  52.9 1.5 fusion.9
  54.7 1.2 fusion.62
  56.1 1.5 add_reduce_fusion
  57.7 2.8 %fusion.refs_8_ = f32[32,64,128]{2,1,0:T(8,128)} fusion(f32[6,32,64]{2,1,0:T(8,128)S(1)} %fusion.62, f32[6,128]{1,0:T(8,128)S(1)} %add_reduce_fusion), kind=kOutput, calls=%fused_computation.1 | convolution fusion | flops 19398656 | bytes 1100800 | tf_op jit(solution)/shard_map/vxy,vz->xyz/dot_general | solution.py:647
  60.5 7.8 %all-to-all-done.1.tiles = bf16[4,8,8,16,128]{4,3,2,1,0:T(8,128)(2,1)S(1)} async-done(((bf16[4,8,8,16,128]{4,3,2,1,0:T(8,128)(2,1)}), bf16[4,8,8,16,128]{4,3,2,1,0:T(8,128)(2,1)S(1)}, u32[]{:S(2)}, u32[]{:S(2)}) %all-to-all-start.1) | async-done | bytes 1048608 | tf_op jit(solution)/shard_map/all_to_all | solution.py:613
  68.4 4.2 %all-to-all-start = ((bf16[4,8,8,16,128]{4,3,2,1,0:T(8,128)(2,1)}), bf16[4,8,8,16,128]{4,3,2,1,0:T(8,128)(2,1)}, u32[]{:S(2)}, u32[]{:S(2)}) async-start(bf16[4,8,8,16,128]{4,3,2,1,0:T(8,128)(2,1)} %copy.51), calls=%async_computation | async-start | bytes 2097152 | tf_op jit(solution)/shard_map/all_to_all | solution.py:613
  72.6 1.2 copy-done.4
  73.8 0.9 copy-done.11
  74.7 23.9 %shard_map.64.blurred = f32[3,32,64,128]{3,2,1,0:T(8,128)S(1)} custom-call(f32[3,15]{1,0:T(4,128)S(1)} %bitcast.84, f32[32,64,128]{2,1,0:T(8,128)S(1)} %copy-done.4, bf16[192,160]{1,0:T(8,128)(2,1)S(1)} %copy-done.11, bf16[3,256,128]{2,1,0:T(8,128)(2,1)S(1)} %pad_maximum_fusion.along_z.refs_11_), custom_call_target="tpu_custom_call" | custom-call | flops 20000000000 | bytes 40000000 | tf_op jit(solution)/shard_map/pallas_call | solution.py:273
  98.7 2.7 %shard_map.67 = (f32[32,64,128]{2,1,0:T(8,128)S(1)}, f32[32,64,128]{2,1,0:T(8,128)S(1)}) custom-call(s32[32]{0:T(128)S(1)} %copy-done.14, s32[32]{0:T(128)S(1)} %copy-done.16, s32[32]{0:T(128)S(1)} %copy-done.19, bf16[4,8,8,16,128]{4,3,2,1,0:T(8,128)(2,1)S(1)} %copy-done.1, f32[3,32,64,128]{3,2,1,0:T(8,128)S(1)} %shard_map.64.blurred, ...), custom_call_target="tpu_custom_call" | custom-call | flops 1000000000 | bytes 8000000 | tf_op jit(solution)/shard_map/pallas_call | solution.py:336
  101.4 1.0 copy-done.5
  102.4 1.0 copy-done.6
  103.4 2.7 %shard_map.66 = (f32[32,64,128]{2,1,0:T(8,128)S(1)}, f32[32,64,128]{2,1,0:T(8,128)S(1)}) custom-call(s32[32]{0:T(128)S(1)} %squeeze.81.filled, s32[32]{0:T(128)S(1)} %copy-done.15, s32[32]{0:T(128)S(1)} %copy-done.17, bf16[4,8,8,16,128]{4,3,2,1,0:T(8,128)(2,1)S(1)} %copy-done.3, f32[3,32,64,128]{3,2,1,0:T(8,128)S(1)} %shard_map.64.blurred, ...), custom_call_target="tpu_custom_call" | custom-call | flops 1000000000 | bytes 8000000 | tf_op jit(solution)/shard_map/pallas_call | solution.py:336
  106.1 1.0 copy-done.7
  107.0 1.0 copy-done.8
  108.1 0.6 copy-done.18
  108.7 3.9 %shard_map.65 = (f32[32,64,128]{2,1,0:T(8,128)S(1)}, f32[32,64,128]{2,1,0:T(8,128)S(1)}) custom-call(s32[32]{0:T(128)S(1)} %squeeze.72.filled, s32[32]{0:T(128)S(1)} %squeeze.73.corner_x, s32[32]{0:T(128)S(1)} %copy-done.18, bf16[4,8,8,16,128]{4,3,2,1,0:T(8,128)(2,1)} %all-to-all-done.tiles, f32[3,32,64,128]{3,2,1,0:T(8,128)S(1)} %shard_map.64.blurred, ...), custom_call_target="tpu_custom_call" | custom-call | flops 1000000000 | bytes 8000000 | tf_op jit(solution)/shard_map/pallas_call | solution.py:336
  112.6 1.0 copy-done.9
  113.6 1.0 copy-done.10
  114.5 53.1 %shard_map.68 = f32[32,64,128]{2,1,0:T(8,128)S(1)} custom-call(f32[3,15]{1,0:T(4,128)S(1)} %bitcast.85, f32[32,64,128]{2,1,0:T(8,128)} %copy-done.9, f32[32,64,128]{2,1,0:T(8,128)} %copy-done.7, f32[32,64,128]{2,1,0:T(8,128)} %copy-done.5, f32[32,64,128]{2,1,0:T(8,128)} %copy-done.10, f32[32,64,128]{2,1,0:T(8,128)} %copy-done.8, f32[32,64,128]{2,1,0:T(8,128)} %copy-done.6, ...), custom_call_target="tpu_custom_call" | custom-call | tf_op jit(solution)/shard_map/pallas_call | solution.py:539
  167.6 1.0 copy.107
  (350 shorter events, 14.0 us)
Async XLA Ops:
  7.4 7.2 %copy-start.53 = (f32[6,3,15]{2,1,0:T(4,128)S(1)}, f32[6,3,15]{2,1,0:T(4,128)}, u32[]{:S(2)}) copy-start(f32[6,3,15]{2,1,0:T(4,128)} %param.10) | copy-start | bytes 3244
  7.5 32.2 %all-to-all-start.2 = ((bf16[4,8,8,16,128]{4,3,2,1,0:T(8,128)(2,1)}), bf16[4,8,8,16,128]{4,3,2,1,0:T(8,128)(2,1)S(1)}, u32[]{:S(2)}, u32[]{:S(2)}) async-start(bf16[4,8,8,16,128]{4,3,2,1,0:T(8,128)(2,1)} %copy.71), calls=%async_computation.2 | async-start | bytes 2097152 | tf_op jit(solution)/shard_map/all_to_all | solution.py:613
  13.9 8.3 %copy-start.21 = (pred[128,128]{1,0:T(8,128)(4,1)}, pred[128,128]{1,0:T(8,128)(4,1)S(1)}, u32[]{:S(2)}) copy-start(pred[128,128]{1,0:T(8,128)(4,1)S(1)} %get-tuple-element.171) | copy-start | bytes 49156
  13.9 8.3 %copy-start.23 = (pred[128,128]{1,0:T(8,128)(4,1)}, pred[128,128]{1,0:T(8,128)(4,1)S(1)}, u32[]{:S(2)}) copy-start(pred[128,128]{1,0:T(8,128)(4,1)S(1)} %get-tuple-element.172) | copy-start | bytes 49156
  14.0 8.3 %copy-start.25 = (pred[128,128]{1,0:T(8,128)(4,1)}, pred[128,128]{1,0:T(8,128)(4,1)S(1)}, u32[]{:S(2)}) copy-start(pred[128,128]{1,0:T(8,128)(4,1)S(1)} %get-tuple-element.173) | copy-start | bytes 49156
  14.0 8.3 %copy-start.27 = (pred[128,128]{1,0:T(8,128)(4,1)}, pred[128,128]{1,0:T(8,128)(4,1)S(1)}, u32[]{:S(2)}) copy-start(pred[128,128]{1,0:T(8,128)(4,1)S(1)} %get-tuple-element.174) | copy-start | bytes 49156
  14.0 8.3 %copy-start.29 = (pred[128,128]{1,0:T(8,128)(4,1)}, pred[128,128]{1,0:T(8,128)(4,1)S(1)}, u32[]{:S(2)}) copy-start(pred[128,128]{1,0:T(8,128)(4,1)S(1)} %get-tuple-element.175) | copy-start | bytes 49156
  14.1 8.3 %copy-start.31 = (pred[128,128]{1,0:T(8,128)(4,1)}, pred[128,128]{1,0:T(8,128)(4,1)S(1)}, u32[]{:S(2)}) copy-start(pred[128,128]{1,0:T(8,128)(4,1)S(1)} %get-tuple-element.176) | copy-start | bytes 49156
  14.1 8.2 %copy-start.33 = (pred[128,128]{1,0:T(8,128)(4,1)}, pred[128,128]{1,0:T(8,128)(4,1)S(1)}, u32[]{:S(2)}) copy-start(pred[128,128]{1,0:T(8,128)(4,1)S(1)} %get-tuple-element.177) | copy-start | bytes 49156
  14.1 8.2 %copy-start.35 = (pred[128,128]{1,0:T(8,128)(4,1)}, pred[128,128]{1,0:T(8,128)(4,1)S(1)}, u32[]{:S(2)}) copy-start(pred[128,128]{1,0:T(8,128)(4,1)S(1)} %get-tuple-element.178) | copy-start | bytes 49156
  14.2 8.2 %copy-start.37 = (pred[128,128]{1,0:T(8,128)(4,1)}, pred[128,128]{1,0:T(8,128)(4,1)S(1)}, u32[]{:S(2)}) copy-start(pred[128,128]{1,0:T(8,128)(4,1)S(1)} %get-tuple-element.179) | copy-start | bytes 49156
  14.2 8.2 %copy-start.39 = (pred[128,128]{1,0:T(8,128)(4,1)}, pred[128,128]{1,0:T(8,128)(4,1)S(1)}, u32[]{:S(2)}) copy-start(pred[128,128]{1,0:T(8,128)(4,1)S(1)} %get-tuple-element.180) | copy-start | bytes 49156
  14.2 8.2 %copy-start.41 = (pred[128,128]{1,0:T(8,128)(4,1)}, pred[128,128]{1,0:T(8,128)(4,1)S(1)}, u32[]{:S(2)}) copy-start(pred[128,128]{1,0:T(8,128)(4,1)S(1)} %get-tuple-element.181) | copy-start | bytes 49156
  14.2 8.2 %copy-start.43 = (pred[128,128]{1,0:T(8,128)(4,1)}, pred[128,128]{1,0:T(8,128)(4,1)S(1)}, u32[]{:S(2)}) copy-start(pred[128,128]{1,0:T(8,128)(4,1)S(1)} %get-tuple-element.182) | copy-start | bytes 49156
  14.3 8.1 %copy-start.45 = (pred[128,128]{1,0:T(8,128)(4,1)}, pred[128,128]{1,0:T(8,128)(4,1)S(1)}, u32[]{:S(2)}) copy-start(pred[128,128]{1,0:T(8,128)(4,1)S(1)} %get-tuple-element.183) | copy-start | bytes 49156
  14.3 8.1 %copy-start.47 = (pred[128,128]{1,0:T(8,128)(4,1)}, pred[128,128]{1,0:T(8,128)(4,1)S(1)}, u32[]{:S(2)}) copy-start(pred[128,128]{1,0:T(8,128)(4,1)S(1)} %get-tuple-element.184) | copy-start | bytes 49156
  14.3 8.1 %copy-start.49 = (pred[128,128]{1,0:T(8,128)(4,1)}, pred[128,128]{1,0:T(8,128)(4,1)S(1)}, u32[]{:S(2)}) copy-start(pred[128,128]{1,0:T(8,128)(4,1)S(1)} %fusion.140) | copy-start | bytes 49156
  21.7 4.9 %copy-start.68 = (f32[3]{0:T(128)}, f32[3]{0:T(128)S(1)}, u32[]{:S(2)}) copy-start(f32[3]{0:T(128)S(1)} %get-tuple-element.69) | copy-start | bytes 40
  21.8 4.9 %copy-start.70 = (f32[3]{0:T(128)}, f32[3]{0:T(128)S(1)}, u32[]{:S(2)}) copy-start(f32[3]{0:T(128)S(1)} %get-tuple-element.70) | copy-start | bytes 40
  21.8 4.9 %copy-start.72 = (f32[3]{0:T(128)}, f32[3]{0:T(128)S(1)}, u32[]{:S(2)}) copy-start(f32[3]{0:T(128)S(1)} %get-tuple-element.71) | copy-start | bytes 40
  21.8 4.9 %copy-start.74 = (f32[3]{0:T(128)}, f32[3]{0:T(128)S(1)}, u32[]{:S(2)}) copy-start(f32[3]{0:T(128)S(1)} %get-tuple-element.72) | copy-start | bytes 40
  21.8 4.9 %copy-start.76 = (f32[3]{0:T(128)}, f32[3]{0:T(128)S(1)}, u32[]{:S(2)}) copy-start(f32[3]{0:T(128)S(1)} %get-tuple-element.73) | copy-start | bytes 40
  21.8 4.9 %copy-start.78 = (f32[3]{0:T(128)}, f32[3]{0:T(128)S(1)}, u32[]{:S(2)}) copy-start(f32[3]{0:T(128)S(1)} %get-tuple-element.74) | copy-start | bytes 40
  21.8 4.9 %copy-start.80 = (f32[3]{0:T(128)}, f32[3]{0:T(128)S(1)}, u32[]{:S(2)}) copy-start(f32[3]{0:T(128)S(1)} %get-tuple-element.75) | copy-start | bytes 40
  21.8 4.9 %copy-start.82 = (f32[3]{0:T(128)}, f32[3]{0:T(128)S(1)}, u32[]{:S(2)}) copy-start(f32[3]{0:T(128)S(1)} %get-tuple-element.76) | copy-start | bytes 40
  21.8 4.9 %copy-start.84 = (f32[3]{0:T(128)}, f32[3]{0:T(128)S(1)}, u32[]{:S(2)}) copy-start(f32[3]{0:T(128)S(1)} %get-tuple-element.77) | copy-start | bytes 40
  21.8 4.9 %copy-start.86 = (f32[3]{0:T(128)}, f32[3]{0:T(128)S(1)}, u32[]{:S(2)}) copy-start(f32[3]{0:T(128)S(1)} %get-tuple-element.78) | copy-start | bytes 40
  21.8 4.9 %copy-start.88 = (f32[3]{0:T(128)}, f32[3]{0:T(128)S(1)}, u32[]{:S(2)}) copy-start(f32[3]{0:T(128)S(1)} %get-tuple-element.79) | copy-start | bytes 40
  23.5 7.2 %copy-start.115 = (s32[46]{0:T(128)S(1)}, s32[46]{0:T(128)}, u32[]{:S(2)}) copy-start(s32[46]{0:T(128)} %iota_add_fusion.1) | copy-start | bytes 556
  24.6 6.8 %copy-start.65 = (f32[3]{0:T(128)S(1)}, f32[3]{0:T(128)}, u32[]{:S(2)}) copy-start(f32[3]{0:T(128)} %copy-done.64) | copy-start | bytes 40
  24.7 6.8 %copy-start.67 = (f32[3]{0:T(128)S(1)}, f32[3]{0:T(128)}, u32[]{:S(2)}) copy-start(f32[3]{0:T(128)} %copy-done.66) | copy-start | bytes 40
  33.3 11.3 %copy-start.63 = (f32[3,1,15]{2,1,0:T(1,128)S(1)}, f32[3,1,15]{2,1,0:T(1,128)}, u32[]{:S(2)}) copy-start(f32[3,1,15]{2,1,0:T(1,128)} %get-tuple-element.109) | copy-start | bytes 544
  33.3 11.9 %copy-start.59 = (s32[1,4,8]{2,1,0:T(4,128)S(1)}, s32[1,4,8]{2,1,0:T(4,128)}, u32[]{:S(2)}) copy-start(s32[1,4,8]{2,1,0:T(4,128)} %get-tuple-element.113) | copy-start | bytes 388
  33.3 12.6 %copy-start.62 = (s32[1,4,8]{2,1,0:T(4,128)S(1)}, s32[1,4,8]{2,1,0:T(4,128)}, u32[]{:S(2)}) copy-start(s32[1,4,8]{2,1,0:T(4,128)} %get-tuple-element.110) | copy-start | bytes 388
  33.3 13.3 %copy-start.58 = (s32[1,4,8]{2,1,0:T(4,128)S(1)}, s32[1,4,8]{2,1,0:T(4,128)}, u32[]{:S(2)}) copy-start(s32[1,4,8]{2,1,0:T(4,128)} %get-tuple-element.114) | copy-start | bytes 388
  33.3 13.9 %copy-start.61 = (s32[1,4,8]{2,1,0:T(4,128)S(1)}, s32[1,4,8]{2,1,0:T(4,128)}, u32[]{:S(2)}) copy-start(s32[1,4,8]{2,1,0:T(4,128)} %get-tuple-element.111) | copy-start | bytes 388
  39.6 9.5 %copy-start = (bf16[4,8,8,16,128]{4,3,2,1,0:T(8,128)(2,1)}, bf16[4,8,8,16,128]{4,3,2,1,0:T(8,128)(2,1)S(1)}, u32[]{:S(2)}) copy-start(bf16[4,8,8,16,128]{4,3,2,1,0:T(8,128)(2,1)S(1)} %all-to-all-done.2.tiles) | copy-start | bytes 3145732
  39.6 28.7 %all-to-all-start.1 = ((bf16[4,8,8,16,128]{4,3,2,1,0:T(8,128)(2,1)}), bf16[4,8,8,16,128]{4,3,2,1,0:T(8,128)(2,1)S(1)}, u32[]{:S(2)}, u32[]{:S(2)}) async-start(bf16[4,8,8,16,128]{4,3,2,1,0:T(8,128)(2,1)} %copy.69), calls=%async_computation.1 | async-start | bytes 2097152 | tf_op jit(solution)/shard_map/all_to_all | solution.py:613
  43.3 5.9 %copy-start.57 = (s32[1,4,8]{2,1,0:T(4,128)S(1)}, s32[1,4,8]{2,1,0:T(4,128)}, u32[]{:S(2)}) copy-start(s32[1,4,8]{2,1,0:T(4,128)} %get-tuple-element.115) | copy-start | bytes 388
  43.3 5.9 %copy-start.60 = (s32[1,4,8]{2,1,0:T(4,128)S(1)}, s32[1,4,8]{2,1,0:T(4,128)}, u32[]{:S(2)}) copy-start(s32[1,4,8]{2,1,0:T(4,128)} %get-tuple-element.112) | copy-start | bytes 388
  68.4 39.7 %all-to-all-start = ((bf16[4,8,8,16,128]{4,3,2,1,0:T(8,128)(2,1)}), bf16[4,8,8,16,128]{4,3,2,1,0:T(8,128)(2,1)}, u32[]{:S(2)}, u32[]{:S(2)}) async-start(bf16[4,8,8,16,128]{4,3,2,1,0:T(8,128)(2,1)} %copy.51), calls=%async_computation | async-start | bytes 2097152 | tf_op jit(solution)/shard_map/all_to_all | solution.py:613
  74.7 23.9 %copy-start.1 = (bf16[4,8,8,16,128]{4,3,2,1,0:T(8,128)(2,1)S(1)}, bf16[4,8,8,16,128]{4,3,2,1,0:T(8,128)(2,1)}, u32[]{:S(2)}) copy-start(bf16[4,8,8,16,128]{4,3,2,1,0:T(8,128)(2,1)} %copy-done) | copy-start | bytes 3145732
  74.7 23.9 %copy-start.14 = (s32[32]{0:T(128)S(1)}, s32[32]{0:T(128)}, u32[]{:S(2)}) copy-start(s32[32]{0:T(128)} %squeeze.86.filled) | copy-start | bytes 388
  74.7 23.9 %copy-start.16 = (s32[32]{0:T(128)S(1)}, s32[32]{0:T(128)}, u32[]{:S(2)}) copy-start(s32[32]{0:T(128)} %squeeze.87.corner_x) | copy-start | bytes 388
  74.7 23.9 %copy-start.19 = (s32[32]{0:T(128)S(1)}, s32[32]{0:T(128)}, u32[]{:S(2)}) copy-start(s32[32]{0:T(128)} %squeeze.88.corner_y) | copy-start | bytes 388
  98.7 4.7 %copy-start.3 = (bf16[4,8,8,16,128]{4,3,2,1,0:T(8,128)(2,1)S(1)}, bf16[4,8,8,16,128]{4,3,2,1,0:T(8,128)(2,1)}, u32[]{:S(2)}) copy-start(bf16[4,8,8,16,128]{4,3,2,1,0:T(8,128)(2,1)} %copy-done.2) | copy-start | bytes 3145732
  108.7 5.9 %copy-start.12 = (bf16[192,160]{1,0:T(8,128)(2,1)S(1)}, bf16[192,160]{1,0:T(8,128)(2,1)}, u32[]{:S(2)}) copy-start(bf16[192,160]{1,0:T(8,128)(2,1)} %copy.67.along_y.refs_9_) | copy-start | bytes 184324
  108.7 5.9 %copy-start.13 = (bf16[160,192]{1,0:T(8,128)(2,1)S(1)}, bf16[160,192]{1,0:T(8,128)(2,1)}, u32[]{:S(2)}) copy-start(bf16[160,192]{1,0:T(8,128)(2,1)} %pad_maximum_fusion.3.refs_10_) | copy-start | bytes 184324
  (71 other events, 253.8 us)

commit v3 on v2

--- a/solution.py
+++ b/solution.py
@@ -211,35 +211,35 @@
     return group
 
 
-def blur_kernel(
-    sizes,
-    taps_x,
-    initial,
-    along_y,
-    along_z,
-    blurred,
-    center,
-    low,
-    high,
-    send_low,
-    send_high,
-    passed_y,
-    send_sem,
-    recv_sem,
+def halo_kernel(
+    sizes, radius, initial, center, low, high, all_center, all_low, all_high, *scratch
 ):
-    views, block_x, block_y, depth = blurred.shape
-    links = Links(sizes, taps_x.shape[1] // 2, block_x)
+    send_low, send_high, send_sem, recv_sem = scratch
+    block_x = initial.shape[0]
+    links = Links(sizes, radius, block_x)
     links.greet()
 
     @pl.loop(0, block_x)
     def _(x):
-        publish(links, center, send_low, send_high, x, initial[x])
-
-    clear_missing(links, center, low, high)
+        publish(links, all_center, send_low, send_high, x, initial[x])
+
+    clear_missing(links, all_center, all_low, all_high)
     links.await_greetings()
     links.exchange(
-        ghosts_of_estimate(links, center, low, high, send_low, send_high), send_sem, recv_sem
+        ghosts_of_estimate(links, all_center, all_low, all_high, send_low, send_high),
+        send_sem,
+        recv_sem,
     )
+
+    @pl.loop(0, center.shape[0])
+    def _(x):
+        center[x] = all_center[x]
+        low[x] = all_low[x]
+        high[x] = all_high[x]
+
+
+def blur_kernel(taps_x, center, low, high, along_y, along_z, blurred, passed_y):
+    views, block_x, block_y, depth = blurred.shape
     pass_along_y(center, low, high, along_y, passed_y, views)
     group = group_of(block_x)
 
@@ -264,37 +264,47 @@
     return -(-(block_x + 2 * radius) // 4) * 4
 
 
-def first_blur(sizes, taps_x, initial, along_y, along_z):
+def first_halos(sizes, radius, initial):
     block_x, block_y, depth = initial.shape
+    vmem = pl.BlockSpec(memory_space=pltpu.VMEM)
+    scratch = estimate_scratch(planes_of(block_x, radius), block_x, block_y, depth)
+    return pl.pallas_call(
+        functools.partial(halo_kernel, sizes, radius),
+        out_shape=[jax.ShapeDtypeStruct(one.shape, one.dtype) for one in scratch[:3]],
+        in_specs=[vmem],
+        out_specs=[vmem] * 3,
+        scratch_shapes=scratch
+        + [pltpu.SemaphoreType.DMA((8,)), pltpu.SemaphoreType.DMA((8,))],
+        compiler_params=pltpu.CompilerParams(
+            collective_id=0, has_side_effects=True, vmem_limit_bytes=12 << 20
+        ),
+    )(initial)
+
+
+def first_blur(taps_x, halos, along_y, along_z, block_x):
+    planes, block_y, depth = halos[0].shape
     views = taps_x.shape[0]
-    planes = planes_of(block_x, taps_x.shape[1] // 2)
     vmem = pl.BlockSpec(memory_space=pltpu.VMEM)
     shape = (views, block_x, block_y, depth)
     return pl.pallas_call(
-        functools.partial(blur_kernel, sizes),
+        blur_kernel,
         out_shape=jax.ShapeDtypeStruct(shape, jnp.float32),
-        in_specs=[pl.BlockSpec(memory_space=pltpu.SMEM)] + [vmem] * 3,
+        in_specs=[pl.BlockSpec(memory_space=pltpu.SMEM)] + [vmem] * 5,
         out_specs=vmem,
-        scratch_shapes=estimate_scratch(planes, block_x, block_y, depth)
-        + [
-            pltpu.VMEM((views, planes, block_y, depth), jnp.float32),
-            pltpu.SemaphoreType.DMA((8,)),
-            pltpu.SemaphoreType.DMA((8,)),
-        ],
+        scratch_shapes=[pltpu.VMEM((views, planes, block_y, depth), jnp.float32)],
         cost_estimate=pl.CostEstimate(
-            flops=20_000_000_000, bytes_accessed=40_000_000, transcendentals=0
+            flops=10_000_000_000, bytes_accessed=40_000_000, transcendentals=0
         ),
-        compiler_params=pltpu.CompilerParams(
-            collective_id=0, has_side_effects=True, vmem_limit_bytes=32 << 20
-        ),
-    )(taps_x, initial, along_y, along_z)
+        compiler_params=pltpu.CompilerParams(vmem_limit_bytes=20 << 20),
+    )(taps_x, *halos, along_y, along_z)
 
 
 def place_kernel(
     filled, corner_x, corner_y, tiles, blurred, back_z, observed, spread, summed, counted
 ):
-    sources, capacity, wide, tall, depth = tiles.shape
-    block_x, block_y = observed.shape[:2]
+    view = pl.program_id(0)
+    sources, _, capacity, wide, tall, depth = tiles.shape
+    _, block_x, block_y, _ = observed.shape
     summed[...] = jnp.zeros_like(summed)
     counted[...] = jnp.zeros_like(counted)
 
@@ -304,12 +314,12 @@
         def _(slot):
             at = source * capacity + slot
 
-            @pl.when(filled[at] > 0)
+            @pl.when(filled[view, at] > 0)
             def _():
-                x = corner_x[at]
-                y = corner_y[at]
+                x = corner_x[view, at]
+                y = corner_y[view, at]
                 where = (pl.ds(x, wide), pl.ds(y, tall), slice(None))
-                summed[where] = summed[where] + tiles[source, slot].astype(jnp.float32)
+                summed[where] = summed[where] + tiles[source, 0, slot].astype(jnp.float32)
                 counted[where] = counted[where] + 1.0
 
     group = group_of(block_x)
@@ -318,50 +328,50 @@
     def _(step):
         planes = pl.ds(step * group, group)
         measured = summed[planes] / jnp.maximum(counted[planes], 1.0)
-        observed[planes] = measured
+        observed[0, planes] = measured
         flat = (group * block_y, depth)
         result = spread_quotient(
             measured.reshape(flat), blurred[0, planes].reshape(flat), back_z[0]
         )
-        spread[planes] = result.reshape(group, block_y, depth)
-
-
-def place(view, filled, corner_x, corner_y, arrived, blurred, back_z):
-    _, block_x, block_y, depth = blurred.shape
-    shape = (block_x, block_y, depth)
-
-    def whole(shape):
-        return pl.BlockSpec(shape, lambda i, *_: (0,) * len(shape))
-
+        spread[0, planes] = result.reshape(group, block_y, depth)
+
+
+def place(filled, corner_x, corner_y, arrived, blurred, back_z):
+    sources, views, capacity, wide, tall, depth = arrived.shape
+    shape = blurred.shape
+    volume = pl.BlockSpec((1,) + shape[1:], lambda v, *_: (v, 0, 0, 0))
     return pl.pallas_call(
         place_kernel,
         out_shape=[jax.ShapeDtypeStruct(shape, jnp.float32)] * 2,
         grid_spec=pltpu.PrefetchScalarGridSpec(
             num_scalar_prefetch=3,
-            grid=(1,),
+            grid=(views,),
             in_specs=[
-                whole(arrived.shape),
-                pl.BlockSpec((1,) + shape, lambda i, *_: (view, 0, 0, 0)),
-                pl.BlockSpec((1,) + back_z.shape[1:], lambda i, *_: (view, 0, 0)),
+                pl.BlockSpec(
+                    (sources, 1, capacity, wide, tall, depth), lambda v, *_: (0, v, 0, 0, 0, 0)
+                ),
+                volume,
+                pl.BlockSpec((1,) + back_z.shape[1:], lambda v, *_: (v, 0, 0)),
             ],
-            out_specs=[whole(shape)] * 2,
-            scratch_shapes=[pltpu.VMEM(shape, jnp.float32)] * 2,
+            out_specs=[volume] * 2,
+            scratch_shapes=[pltpu.VMEM(shape[1:], jnp.float32)] * 2,
         ),
-        cost_estimate=pl.CostEstimate(
-            flops=1_000_000_000, bytes_accessed=8_000_000, transcendentals=0
-        ),
-        compiler_params=pltpu.CompilerParams(vmem_limit_bytes=24 << 20),
+        compiler_params=pltpu.CompilerParams(vmem_limit_bytes=20 << 20),
     )(filled, corner_x, corner_y, arrived, blurred, back_z)
 
 
-def sweep_kernel(sizes, views, *refs):
-    taps_x = refs[0]
-    observed = refs[1 : 1 + views]
-    spreads = refs[1 + views : 1 + 2 * views]
-    initial, inverse_norm, along_y, back_y, along_z, back_z, estimate = refs[
-        1 + 2 * views : 8 + 2 * views
-    ]
+def sweep_kernel(sizes, *refs):
     (
+        taps_x,
+        observed,
+        spreads,
+        initial,
+        inverse_norm,
+        along_y,
+        back_y,
+        along_z,
+        back_z,
+        estimate,
         center,
         low,
         high,
@@ -374,7 +384,8 @@
         out_y,
         in_x,
         in_y,
-        vert_out,
+        far_x,
+        far_y,
         vert_in,
         est_send,
         est_recv,
@@ -382,8 +393,10 @@
         acc_recv,
         vert_send,
         vert_recv,
-    ) = refs[8 + 2 * views :]
-    block_x, block_y, depth = initial.shape
+        far_send,
+        far_recv,
+    ) = refs
+    views, block_x, block_y, depth = observed.shape
     tap_count = taps_x.shape[1]
     radius = tap_count // 2
     planes = center.shape[1]
@@ -420,7 +433,7 @@
     @pl.loop(0, block_x)
     def _(x):
         for view in range(views):
-            passed_z[view, below + x] = spreads[view][x]
+            passed_z[view, below + x] = spreads[view, x]
 
     for sweep in range(ITERS):
         if sweep > 0:
@@ -439,11 +452,28 @@
                 first = step * group
                 for view in range(views):
                     blurred = pass_along_xz(taps_x, passed_y, along_z[view], view, first, group)
-                    measured = observed[view][pl.ds(first, group)].reshape(blurred.shape)
+                    measured = observed[view, pl.ds(first, group)].reshape(blurred.shape)
                     result = spread_quotient(measured, blurred, back_z[view])
                     passed_z[view, pl.ds(below + first, group)] = result.reshape(
                         group, block_y, depth
                     )
+
+        if sweep == 0:
+            links.await_greetings(1)
+
+        def vert(start, size):
+            chunk = pl.ds(start, size)
+            return pltpu.make_async_remote_copy(
+                src_ref=acc.at[sweep, chunk],
+                dst_ref=vert_in.at[sweep, chunk],
+                send_sem=vert_send.at[sweep],
+                recv_sem=vert_recv.at[sweep],
+                device_id=partner,
+                device_id_type=pl.DeviceIdType.MESH,
+            )
+
+        first_chunk = radius // 4
+        last_chunk = (radius + block_x - 1) // 4
 
         @pl.loop(0, planes // 4)
         def _(step):
@@ -464,17 +494,19 @@
                 for side in range(2):
                     x = first + side
                     lanes = slice(side * depth, (side + 1) * depth)
-                    acc[x] = result[:block_y, lanes]
+                    acc[sweep, x] = result[:block_y, lanes]
                     out_y[sweep, 0, x] = result[block_y : block_y + HALO_Y, lanes].astype(bf16)
                     out_y[sweep, 1, x] = result[block_y + HALO_Y :, lanes].astype(bf16)
 
+            @pl.when(jnp.logical_and(step >= first_chunk, step <= last_chunk))
+            def _():
+                vert(4 * step, 4).start()
+
         @pl.loop(0, radius)
         def _(x):
-            out_x[sweep, 0, x] = acc[x].astype(bf16)
-            out_x[sweep, 1, x] = acc[radius + block_x + x].astype(bf16)
-
-        if sweep == 0:
-            links.await_greetings(1)
+            out_x[sweep, 0, x] = acc[sweep, x].astype(bf16)
+            out_x[sweep, 1, x] = acc[sweep, radius + block_x + x].astype(bf16)
+
         links.exchange(
             ghosts_of_sums(
                 links, out_x.at[sweep], out_y.at[sweep], in_x.at[sweep], in_y.at[sweep]
@@ -482,41 +514,50 @@
             acc_send.at[sweep],
             acc_recv.at[sweep],
         )
+        forwards = [
+            pltpu.make_async_remote_copy(
+                src_ref=near.at[sweep],
+                dst_ref=far.at[sweep],
+                send_sem=far_send.at[sweep, index],
+                recv_sem=far_recv.at[sweep, index],
+                device_id=partner,
+                device_id_type=pl.DeviceIdType.MESH,
+            )
+            for index, (near, far) in enumerate(((in_x, far_x), (in_y, far_y)))
+        ]
+        for forward in forwards:
+            forward.start()
+        vert(4 * first_chunk, 4 * (last_chunk - first_chunk + 1)).wait()
+
+        @pl.loop(0, block_x)
+        def _(x):
+            acc[sweep, radius + x] = acc[sweep, radius + x] + vert_in[sweep, radius + x]
+
+        for forward in forwards:
+            forward.wait()
+
+        def beyond_y(side, plane):
+            return in_y[sweep, side, plane].astype(f32) + far_y[sweep, side, plane].astype(f32)
 
         @pl.loop(0, radius)
         def _(x):
             for side, at, beside in ((0, radius + x, x), (1, block_x + x, radius + block_x + x)):
-                plane = acc[at] + in_x[sweep, side, x].astype(f32)
-                first = plane[:HALO_Y] + in_y[sweep, 0, beside].astype(f32)
-                last = plane[block_y - HALO_Y :] + in_y[sweep, 1, beside].astype(f32)
-                acc[at] = jnp.concatenate(
+                plane = acc[sweep, at] + (
+                    in_x[sweep, side, x].astype(f32) + far_x[sweep, side, x].astype(f32)
+                )
+                first = plane[:HALO_Y] + beyond_y(0, beside)
+                last = plane[block_y - HALO_Y :] + beyond_y(1, beside)
+                acc[sweep, at] = jnp.concatenate(
                     [first, plane[HALO_Y : block_y - HALO_Y], last], axis=0
                 )
 
         @pl.loop(0, block_x)
         def _(x):
-            plane = acc[radius + x]
-            first = plane[:HALO_Y] + in_y[sweep, 0, radius + x].astype(f32)
-            last = plane[block_y - HALO_Y :] + in_y[sweep, 1, radius + x].astype(f32)
-            vert_out[sweep, x] = jnp.concatenate(
-                [first, plane[HALO_Y : block_y - HALO_Y], last], axis=0
-            )
-
-        vert = pltpu.make_async_remote_copy(
-            src_ref=vert_out.at[sweep],
-            dst_ref=vert_in.at[sweep],
-            send_sem=vert_send.at[sweep],
-            recv_sem=vert_recv.at[sweep],
-            device_id=partner,
-            device_id_type=pl.DeviceIdType.MESH,
-        )
-        vert.start()
-        vert.wait()
-
-        @pl.loop(0, block_x)
-        def _(x):
+            plane = acc[sweep, radius + x]
+            first = plane[:HALO_Y] + beyond_y(0, radius + x)
+            last = plane[block_y - HALO_Y :] + beyond_y(1, radius + x)
+            combined = jnp.concatenate([first, plane[HALO_Y : block_y - HALO_Y], last], axis=0)
             before = initial[x] if sweep == 0 else estimate[x]
-            combined = vert_out[sweep, x] + vert_in[sweep, x]
             after = before * (combined + damping) * inverse_norm[x]
             estimate[x] = after
             if sweep + 1 < ITERS:
@@ -529,17 +570,18 @@
     sizes, taps_x, observed, spreads, initial, inverse_norm, along_y, back_y, along_z, back_z
 ):
     block_x, block_y, depth = initial.shape
-    views = len(observed)
+    views = observed.shape[0]
     radius = taps_x.shape[1] // 2
     planes = planes_of(block_x, radius)
+    extended_x = block_x + 2 * radius
     vmem = pl.BlockSpec(memory_space=pltpu.VMEM)
     bf16 = jnp.bfloat16
     f32 = jnp.float32
     repeats = ITERS - 1
     return pl.pallas_call(
-        functools.partial(sweep_kernel, sizes, views),
+        functools.partial(sweep_kernel, sizes),
         out_shape=jax.ShapeDtypeStruct(initial.shape, f32),
-        in_specs=[pl.BlockSpec(memory_space=pltpu.SMEM)] + [vmem] * (6 + 2 * views),
+        in_specs=[pl.BlockSpec(memory_space=pltpu.SMEM)] + [vmem] * 8,
         out_specs=vmem,
         scratch_shapes=[
             pltpu.VMEM((repeats,) + scratch.shape, scratch.dtype)
@@ -548,24 +590,27 @@
         + [
             pltpu.VMEM((views, planes, block_y, depth), f32),
             pltpu.VMEM((views, planes + 2 * radius, block_y, depth), f32),
-            pltpu.VMEM((planes, block_y, depth), f32),
+            pltpu.VMEM((ITERS, planes, block_y, depth), f32),
             pltpu.VMEM((ITERS, 2, radius, block_y, depth), bf16),
             pltpu.VMEM((ITERS, 2, planes, HALO_Y, depth), bf16),
             pltpu.VMEM((ITERS, 2, radius, block_y, depth), bf16),
-            pltpu.VMEM((ITERS, 2, planes, HALO_Y, depth), bf16),
-            pltpu.VMEM((ITERS, block_x, block_y, depth), f32),
-            pltpu.VMEM((ITERS, block_x, block_y, depth), f32),
+            pltpu.VMEM((ITERS, 2, extended_x, HALO_Y, depth), bf16),
+            pltpu.VMEM((ITERS, 2, radius, block_y, depth), bf16),
+            pltpu.VMEM((ITERS, 2, extended_x, HALO_Y, depth), bf16),
+            pltpu.VMEM((ITERS, planes, block_y, depth), f32),
             pltpu.SemaphoreType.DMA((repeats, 8)),
             pltpu.SemaphoreType.DMA((repeats, 8)),
             pltpu.SemaphoreType.DMA((ITERS, 8)),
             pltpu.SemaphoreType.DMA((ITERS, 8)),
             pltpu.SemaphoreType.DMA((ITERS,)),
             pltpu.SemaphoreType.DMA((ITERS,)),
+            pltpu.SemaphoreType.DMA((ITERS, 2)),
+            pltpu.SemaphoreType.DMA((ITERS, 2)),
         ],
         compiler_params=pltpu.CompilerParams(
-            collective_id=1, has_side_effects=True, vmem_limit_bytes=52 << 20
+            collective_id=1, has_side_effects=True, vmem_limit_bytes=40 << 20
         ),
-    )(taps_x, *observed, *spreads, initial, inverse_norm, along_y, back_y, along_z, back_z)
+    )(taps_x, observed, spreads, initial, inverse_norm, along_y, back_y, along_z, back_z)
 
 
 def shards(tiles, tile_block, tile_x, tile_y, psf, initial):
@@ -601,16 +646,16 @@
     chooser = sent_hits[:, :, None, :] * (
         sent_ranks[:, :, None, :] == slot_ids[None, None, :, None]
     ).astype(jnp.int32)
-    chooser = chooser.astype(jnp.bfloat16)
-    arrived = []
-    for view in range(local_views):
-        outgoing = jnp.einsum(
-            "gkj,jabz->gkabz",
-            chooser[view],
-            tiles[view, 0],
-            preferred_element_type=jnp.bfloat16,
-        )
-        arrived.append(lax.all_to_all(outgoing, "gx", split_axis=0, concat_axis=0, tiled=True))
+    outgoing = jnp.einsum(
+        "vgkj,vjabz->gvkabz",
+        chooser.astype(jnp.bfloat16),
+        tiles[:, 0],
+        preferred_element_type=jnp.bfloat16,
+    )
+    sizes = (column_count, lax.axis_size("gy"))
+    halos = first_halos(sizes, radius, initial)
+    outgoing, halos = lax.optimization_barrier((outgoing, halos))
+    arrived = lax.all_to_all(outgoing, "gx", split_axis=0, concat_axis=0, tiled=True)
     from_hits = lax.dynamic_slice_in_dim(hits, column_index, 1, 3)[..., 0]
     from_ranks = lax.dynamic_slice_in_dim(ranks, column_index, 1, 3)[..., 0]
     picks = from_hits[:, :, None, :] * (
@@ -662,16 +707,9 @@
     band_z = banded(mine_psf[:, 2], iota_z[:, None] - iota_z[None, :] + radius)
     along_z = jnp.concatenate(split_high_low(band_z), axis=1)
     back_z = jnp.concatenate(split_high_low(jnp.swapaxes(band_z, 1, 2)), axis=1)
-    sizes = (column_count, lax.axis_size("gy"))
     taps_x = mine_psf[:, 0]
-    blurred = first_blur(sizes, taps_x, initial, along_y, along_z)
-    placed = [
-        place(
-            view, filled[view], corner_x[view], corner_y[view], arrived[view], blurred, back_z
-        )
-        for view in range(local_views)
-    ]
-    observed, spreads = zip(*placed)
+    blurred = first_blur(taps_x, halos, along_y, along_z, block_x)
+    observed, spreads = place(filled, corner_x, corner_y, arrived, blurred, back_z)
     return sweeps(
         sizes,
         taps_x,

time: 169 us -> 143 us (0.85)
  Pallas kernels: 86.2 us -> 65.7 us
  starting transfers between devices: 14.4 us -> 4.95 us
  waiting for transfers between devices: 13.7 us -> 22 us
  local copies, waits for them, and re-layouts: 33.1 us -> 27.7 us
  other arithmetic: 11.4 us -> 15.7 us
  matrix products: 7.95 us -> 5.5 us
    pallas_call x2 -> x3, Pallas kernels: 76.9 us -> 57 us  [the longest x1 40.9 us: sweeps(): pl.pallas_call(functools.partial(sweep_kernel, sizes), out_shape=jax.Shap...]
    all_to_all x3 -> x1, starting transfers between devices: 14.4 us -> 4.95 us  [shards(): lax.all_to_all(outgoing, 'gx', split_axis=0, concat_axis=0, tiled=True)]
    all_to_all x3 -> x1, waiting for transfers between devices: 13.7 us -> 22 us  [shards(): lax.all_to_all(outgoing, 'gx', split_axis=0, concat_axis=0, tiled=True)]
    broadcast_in_dim x60, local copies, waits for them, and re-layouts: 3.97 us -> 10.8 us  [banded(): jnp.where(difference == tap_index, taps[..., tap_index, None, None], 0.0)]
    eq x19, other arithmetic: 1.92 us -> 6.11 us  [banded(): difference == tap_index]
    squeeze x9 -> x0, local copies, waits for them, and re-layouts: 4.06 us -> none  [the longest x3 1.94 us: shards(): corner_y[view]]
    slice x4 -> x0, local copies, waits for them, and re-layouts: 3.74 us -> none  [the longest x1 2.54 us: shards(): tiles[view, 0]]
    unnamed x236 -> x54, local copies, waits for them, and re-layouts: 10.1 us -> 6.36 us
  transfers between devices with their start and end apart: 3 -> 1, of which waited for: 2 -> 1; matrix products, arithmetic and copies ran while one was open for 21% -> 27% of each run, Pallas kernels for 17% -> 5%
where the time goes in v3:
time: 143 us; the launch traced here: 142 us
  Pallas kernels  65.7 us (46%)
  local copies, waits for them, and re-layouts  27.7 us (19%)
  waiting for transfers between devices  22 us (15%)
  other arithmetic  15.7 us (11%)
  matrix products  5.5 us (4%)
  starting transfers between devices  4.95 us (3%)
    pallas_call x1, Pallas kernels, sweeps(): pl.pallas_call(functools.partial(sweep_kernel, sizes), out_shape=jax.Shap...  40.9 us
    all_to_all x1, waiting for transfers between devices, shards(): lax.all_to_all(outgoing, 'gx', split_axis=0, concat_axis=0, tiled=True)  22 us
    broadcast_in_dim x60, local copies, waits for them, and re-layouts, banded(): jnp.where(difference == tap_index, taps[..., tap_index, None, None], 0.0)  10.8 us
    pallas_call x1, Pallas kernels, first_halos(): pl.pallas_call(functools.partial(halo_kernel, sizes, radius), out_shape=[...  9.03 us
    pallas_call x1, Pallas kernels, place(): pl.pallas_call(place_kernel, out_shape=[jax.ShapeDtypeStruct(shape, jnp.f...  8.67 us
    pallas_call x1, Pallas kernels, first_blur(): pl.pallas_call(blur_kernel, out_shape=jax.ShapeDtypeStruct(shape, jnp.flo...  7.15 us
    unnamed x54, local copies, waits for them, and re-layouts  6.36 us
    eq x19, other arithmetic, banded(): difference == tap_index  6.11 us
  transfers between devices with their start and end apart: 1, of which 1 were waited for; matrix products, arithmetic and copies ran while one was open for 27% of the time, Pallas kernels for 5%

profile of v3, /device:TPU:0, one launch (start us, length us, event | category | flops | bytes accessed | tf_op | source)
XLA Modules:
  0.0 142.3 jit_solution(2914052004071549126)
XLA Ops:
  0.0 0.8 fusion.227
  1.4 1.2 fusion
  2.6 2.6 %copy.87 = bf16[3,4,8,8,16,128]{5,4,3,2,0,1:T(8,128)(2,1)} copy(bf16[3,4,8,8,16,128]{5,2,4,3,1,0:T(8,128)(2,1)S(1)} %fusion) | data formatting | bytes 6291456 | tf_op jit(solution)/shard_map/vgkj,vjabz->gvkabz/dot_general | solution.py:649
  5.2 9.0 %shard_map.64 = (bf16[48,64,128]{2,1,0:T(8,128)(2,1)S(1)}, bf16[48,8,128]{2,1,0:T(8,128)(2,1)S(1)}, bf16[48,8,128]{2,1,0:T(8,128)(2,1)S(1)}) custom-call(f32[32,64,128]{2,1,0:T(8,128)S(1)} %copy-done.1), custom_call_target="tpu_custom_call" | custom-call | tf_op jit(solution)/shard_map/pallas_call | solution.py:271
  14.3 0.9 copy-done.5
  15.1 4.9 %all-to-all-start = ((bf16[4,3,8,8,16,128]{5,4,3,2,1,0:T(8,128)(2,1)}), bf16[4,3,8,8,16,128]{5,4,3,2,1,0:T(8,128)(2,1)}, u32[]{:S(2)}, u32[]{:S(2)}) async-start(bf16[4,3,8,8,16,128]{5,4,3,2,1,0:T(8,128)(2,1)} %bitcast.62), calls=%async_computation | async-start | bytes 6291456 | tf_op jit(solution)/shard_map/all_to_all | solution.py:658
  20.4 0.6 fusion.110
  21.1 0.6 fusion.112
  21.7 0.6 fusion.114
  22.4 0.6 fusion.116
  23.0 0.6 fusion.118
  23.6 0.7 fusion.120
  24.3 0.6 fusion.122
  24.9 0.6 fusion.124
  29.7 0.6 broadcast_in_dim.1023
  30.4 0.6 broadcast_in_dim.1029
  31.1 0.7 broadcast_in_dim.1035
  31.8 0.7 broadcast_in_dim.1041
  32.6 0.7 broadcast_in_dim.1047
  33.3 0.7 broadcast_in_dim.1053
  34.0 0.7 broadcast_in_dim.1059
  34.8 0.7 broadcast_in_dim.1065
  35.5 0.6 broadcast_in_dim.1071
  36.2 0.7 broadcast_in_dim.1077
  36.9 0.6 broadcast_in_dim.1083
  37.6 0.6 broadcast_in_dim.1089
  40.3 0.9 reduce-precision_convert_fusion.2
  41.8 0.7 fusion.228
  42.7 1.4 %fusion.141 = (s32[3,4,8]{2,1,0:T(4,128)S(1)}, s32[3,4,8]{2,1,0:T(4,128)S(1)}, s32[3,4,8]{2,1,0:T(4,128)S(1)}) fusion(s32[3,4,16]{2,1,0:T(4,128)S(1)} %mul.71, s32[3,4,16]{2,1,0:T(4,128)} %bitcast.81, s32[3,4,16]{2,1,0:T(4,128)S(1)} %dynamic-slice_reduce_fusion, s32[8]{0:T(128)} %copy-done.22, s32[3,4,16]{2,1,0:T(4,128)S(1)} %mul.68), kind=kLoop, calls=%fused_computation.164 | loop fusion | flops 10464 | bytes 4256 | tf_op jit(solution)/shard_map/reduce_sum | solution.py:666
  44.9 0.8 broadcast_add_fusion
  45.7 0.7 ge.35
  46.3 0.7 bitcast_add_fusion
  47.1 0.7 ge.31
  47.7 0.7 copy.88
  48.4 0.7 copy_bitcast_fusion.1
  50.9 1.3 reduce-precision_convert_fusion
  52.3 0.7 broadcast_add_fusion.1
  53.0 0.6 fusion.224
  54.1 0.8 fusion.8
  55.4 0.8 add_reduce_fusion
  56.2 2.8 %fusion.2.refs_4_ = f32[32,64,128]{2,1,0:T(8,128)} fusion(f32[6,32,64]{2,1,0:T(8,128)S(1)} %fusion.61, f32[6,128]{1,0:T(8,128)S(1)} %add_reduce_fusion), kind=kOutput, calls=%fused_computation.4 | convolution fusion | flops 19398656 | bytes 1100800 | tf_op jit(solution)/shard_map/vxy,vz->xyz/dot_general | solution.py:692
  59.0 7.2 %shard_map.65.blurred = f32[3,32,64,128]{3,2,1,0:T(8,128)S(1)} custom-call(f32[3,15]{1,0:T(4,128)S(1)} %bitcast.60, bf16[48,64,128]{2,1,0:T(8,128)(2,1)S(1)} %copy-done.6, bf16[48,8,128]{2,1,0:T(8,128)(2,1)S(1)} %get-tuple-element.19.low, bf16[48,8,128]{2,1,0:T(8,128)(2,1)S(1)} %get-tuple-element.20.high, bf16[192,160]{1,0:T(8,128)(2,1)S(1)} %copy.59.along_y.refs_5_, ...), custom_call_target="tpu_custom_call" | custom-call | flops 10000000000 | bytes 40000000 | tf_op jit(solution)/shard_map/pallas_call | solution.py:289
  66.2 1.7 %copy-done.2 = f32[3,32,64,128]{3,2,1,0:T(8,128)} copy-done((f32[3,32,64,128]{3,2,1,0:T(8,128)}, f32[3,32,64,128]{3,2,1,0:T(8,128)S(1)}, u32[]{:S(2)}) %copy-start.2) | copy-done | bytes 3145752
  67.9 22.0 %all-to-all-done.tiles = bf16[4,3,8,8,16,128]{5,4,3,2,1,0:T(8,128)(2,1)} async-done(((bf16[4,3,8,8,16,128]{5,4,3,2,1,0:T(8,128)(2,1)}), bf16[4,3,8,8,16,128]{5,4,3,2,1,0:T(8,128)(2,1)}, u32[]{:S(2)}, u32[]{:S(2)}) %all-to-all-start) | async-done | bytes 3145760 | tf_op jit(solution)/shard_map/all_to_all | solution.py:658
  89.9 1.9 %copy-done.3 = f32[3,32,64,128]{3,2,1,0:T(8,128)S(1)} copy-done((f32[3,32,64,128]{3,2,1,0:T(8,128)S(1)}, f32[3,32,64,128]{3,2,1,0:T(8,128)}, u32[]{:S(2)}) %copy-start.3) | copy-done | bytes 3145752
  91.8 8.7 %shard_map.66 = (f32[3,32,64,128]{3,2,1,0:T(8,128)S(1)}, f32[3,32,64,128]{3,2,1,0:T(8,128)S(1)}) custom-call(s32[3,32]{1,0:T(4,128)S(1)} %reshape.204.filled, s32[3,32]{1,0:T(4,128)S(1)} %reshape.205.corner_x, s32[3,32]{1,0:T(4,128)S(1)} %reshape.206.corner_y, bf16[4,3,8,8,16,128]{5,4,3,2,1,0:T(8,128)(2,1)} %all-to-all-done.tiles, ...), custom_call_target="tpu_custom_call" | custom-call | tf_op jit(solution)/shard_map/pallas_call | solution.py:343
  100.5 40.9 %shard_map.67 = f32[32,64,128]{2,1,0:T(8,128)S(1)} custom-call(f32[3,15]{1,0:T(4,128)S(1)} %bitcast.61, f32[3,32,64,128]{3,2,1,0:T(8,128)S(1)} %get-tuple-element.21.refs_1_, f32[3,32,64,128]{3,2,1,0:T(8,128)S(1)} %get-tuple-element.22.refs_2_, f32[32,64,128]{2,1,0:T(8,128)S(1)} %copy-done.1, f32[32,64,128]{2,1,0:T(8,128)S(1)} %copy-done.4, ...), custom_call_target="tpu_custom_call" | custom-call | tf_op jit(solution)/shard_map/pallas_call | solution.py:581
  141.3 1.0 copy.91
  (149 shorter events, 11.6 us)
Async XLA Ops:
  0.0 1.4 %copy-start = (bf16[3,1,16,8,16,128]{5,4,3,2,1,0:T(8,128)(2,1)S(1)}, bf16[3,1,16,8,16,128]{5,4,3,2,1,0:T(8,128)(2,1)}, u32[]{:S(2)}) copy-start(bf16[3,1,16,8,16,128]{5,4,3,2,1,0:T(8,128)(2,1)} %param.6) | copy-start | bytes 4718596
  0.0 1.4 copy-start.22
  2.6 2.6 %copy-start.1 = (f32[32,64,128]{2,1,0:T(8,128)S(1)}, f32[32,64,128]{2,1,0:T(8,128)}, u32[]{:S(2)}) copy-start(f32[32,64,128]{2,1,0:T(8,128)} %refs_3_.1) | copy-start | bytes 3145732
  14.2 0.9 copy-start.5
  15.1 13.0 %copy-start.21 = (f32[6,3,15]{2,1,0:T(4,128)S(1)}, f32[6,3,15]{2,1,0:T(4,128)}, u32[]{:S(2)}) copy-start(f32[6,3,15]{2,1,0:T(4,128)} %param.10) | copy-start | bytes 3244
  15.1 74.8 %all-to-all-start = ((bf16[4,3,8,8,16,128]{5,4,3,2,1,0:T(8,128)(2,1)}), bf16[4,3,8,8,16,128]{5,4,3,2,1,0:T(8,128)(2,1)}, u32[]{:S(2)}, u32[]{:S(2)}) async-start(bf16[4,3,8,8,16,128]{5,4,3,2,1,0:T(8,128)(2,1)} %bitcast.62), calls=%async_computation | async-start | bytes 6291456 | tf_op jit(solution)/shard_map/all_to_all | solution.py:658
  20.3 30.5 %copy-start.7 = (pred[128,128]{1,0:T(8,128)(4,1)}, pred[128,128]{1,0:T(8,128)(4,1)S(1)}, u32[]{:S(2)}) copy-start(pred[128,128]{1,0:T(8,128)(4,1)S(1)} %get-tuple-element.173) | copy-start | bytes 49156
  20.3 30.5 %copy-start.9 = (pred[128,128]{1,0:T(8,128)(4,1)}, pred[128,128]{1,0:T(8,128)(4,1)S(1)}, u32[]{:S(2)}) copy-start(pred[128,128]{1,0:T(8,128)(4,1)S(1)} %get-tuple-element.174) | copy-start | bytes 49156
  20.3 30.5 %copy-start.11 = (pred[128,128]{1,0:T(8,128)(4,1)}, pred[128,128]{1,0:T(8,128)(4,1)S(1)}, u32[]{:S(2)}) copy-start(pred[128,128]{1,0:T(8,128)(4,1)S(1)} %get-tuple-element.175) | copy-start | bytes 49156
  20.4 30.5 %copy-start.13 = (pred[128,128]{1,0:T(8,128)(4,1)}, pred[128,128]{1,0:T(8,128)(4,1)S(1)}, u32[]{:S(2)}) copy-start(pred[128,128]{1,0:T(8,128)(4,1)S(1)} %get-tuple-element.176) | copy-start | bytes 49156
  20.4 30.5 %copy-start.15 = (pred[128,128]{1,0:T(8,128)(4,1)}, pred[128,128]{1,0:T(8,128)(4,1)S(1)}, u32[]{:S(2)}) copy-start(pred[128,128]{1,0:T(8,128)(4,1)S(1)} %get-tuple-element.177) | copy-start | bytes 49156
  20.4 31.9 %copy-start.17 = (pred[128,128]{1,0:T(8,128)(4,1)}, pred[128,128]{1,0:T(8,128)(4,1)S(1)}, u32[]{:S(2)}) copy-start(pred[128,128]{1,0:T(8,128)(4,1)S(1)} %fusion.139) | copy-start | bytes 49156
  47.7 6.0 %copy-start.23 = (s32[78]{0:T(128)S(1)}, s32[78]{0:T(128)}, u32[]{:S(2)}) copy-start(s32[78]{0:T(128)} %iota_add_fusion) | copy-start | bytes 940
  47.7 6.1 %copy-start.19 = (s32[6,128]{1,0:T(8,128)S(1)}, s32[6,128]{1,0:T(8,128)}, u32[]{:S(2)}) copy-start(s32[6,128]{1,0:T(8,128)} %ge.35) | copy-start | bytes 9220
  47.7 6.1 %copy-start.20 = (s32[6,128]{1,0:T(8,128)S(1)}, s32[6,128]{1,0:T(8,128)}, u32[]{:S(2)}) copy-start(s32[6,128]{1,0:T(8,128)} %ge.31) | copy-start | bytes 9220
  47.7 6.1 %copy-start.24 = (s32[78]{0:T(128)S(1)}, s32[78]{0:T(128)}, u32[]{:S(2)}) copy-start(s32[78]{0:T(128)} %broadcast_add_fusion.3) | copy-start | bytes 940
  50.9 4.5 %copy-start.8 = (pred[128,128]{1,0:T(8,128)(4,1)S(1)}, pred[128,128]{1,0:T(8,128)(4,1)}, u32[]{:S(2)}) copy-start(pred[128,128]{1,0:T(8,128)(4,1)} %copy-done.7) | copy-start | bytes 49156
  50.9 4.5 %copy-start.10 = (pred[128,128]{1,0:T(8,128)(4,1)S(1)}, pred[128,128]{1,0:T(8,128)(4,1)}, u32[]{:S(2)}) copy-start(pred[128,128]{1,0:T(8,128)(4,1)} %copy-done.9) | copy-start | bytes 49156
  50.9 4.5 %copy-start.12 = (pred[128,128]{1,0:T(8,128)(4,1)S(1)}, pred[128,128]{1,0:T(8,128)(4,1)}, u32[]{:S(2)}) copy-start(pred[128,128]{1,0:T(8,128)(4,1)} %copy-done.11) | copy-start | bytes 49156
  50.9 4.5 %copy-start.14 = (pred[128,128]{1,0:T(8,128)(4,1)S(1)}, pred[128,128]{1,0:T(8,128)(4,1)}, u32[]{:S(2)}) copy-start(pred[128,128]{1,0:T(8,128)(4,1)} %copy-done.13) | copy-start | bytes 49156
  50.9 4.5 %copy-start.16 = (pred[128,128]{1,0:T(8,128)(4,1)S(1)}, pred[128,128]{1,0:T(8,128)(4,1)}, u32[]{:S(2)}) copy-start(pred[128,128]{1,0:T(8,128)(4,1)} %copy-done.15) | copy-start | bytes 49156
  52.3 3.1 %copy-start.18 = (pred[128,128]{1,0:T(8,128)(4,1)S(1)}, pred[128,128]{1,0:T(8,128)(4,1)}, u32[]{:S(2)}) copy-start(pred[128,128]{1,0:T(8,128)(4,1)} %copy-done.17) | copy-start | bytes 49156
  54.8 4.2 %copy-start.6 = (bf16[48,64,128]{2,1,0:T(8,128)(2,1)S(1)}, bf16[48,64,128]{2,1,0:T(8,128)(2,1)}, u32[]{:S(2)}) copy-start(bf16[48,64,128]{2,1,0:T(8,128)(2,1)} %copy-done.5) | copy-start | bytes 2359300
  66.2 1.7 %copy-start.2 = (f32[3,32,64,128]{3,2,1,0:T(8,128)}, f32[3,32,64,128]{3,2,1,0:T(8,128)S(1)}, u32[]{:S(2)}) copy-start(f32[3,32,64,128]{3,2,1,0:T(8,128)S(1)} %shard_map.65.blurred) | copy-start | bytes 9437188
  89.9 1.9 %copy-start.3 = (f32[3,32,64,128]{3,2,1,0:T(8,128)S(1)}, f32[3,32,64,128]{3,2,1,0:T(8,128)}, u32[]{:S(2)}) copy-start(f32[3,32,64,128]{3,2,1,0:T(8,128)} %copy-done.2) | copy-start | bytes 9437188
  91.8 8.7 %copy-start.4 = (f32[32,64,128]{2,1,0:T(8,128)S(1)}, f32[32,64,128]{2,1,0:T(8,128)}, u32[]{:S(2)}) copy-start(f32[32,64,128]{2,1,0:T(8,128)} %fusion.2.refs_4_) | copy-start | bytes 3145732

commit v4 on v3

--- a/solution.py
+++ b/solution.py
@@ -89,32 +89,44 @@
         return pl.ds(0 if step == -1 else self.block_x - self.radius, self.radius)
 
     def exchange(self, make, send_sem, recv_sem):
-        def copy(index, dx, dy):
-            src, dst = make(dx, dy)
-            return pltpu.make_async_remote_copy(
-                src_ref=src,
-                dst_ref=dst,
-                send_sem=send_sem.at[index],
-                recv_sem=recv_sem.at[index],
-                device_id=self.device(dx, dy),
-                device_id_type=pl.DeviceIdType.MESH,
-            )
-
-        for index, (dx, dy) in enumerate(self.directions):
+        self.start(make, send_sem, recv_sem, self.directions)
+        self.finish(make, send_sem, recv_sem, self.directions)
+
+    def across_x(self):
+        return [one for one in self.directions if one[0] != 0]
+
+    def along_y_only(self):
+        return [one for one in self.directions if one[0] == 0]
+
+    def copy(self, make, send_sem, recv_sem, dx, dy):
+        index = self.directions.index((dx, dy))
+        src, dst = make(dx, dy)
+        return pltpu.make_async_remote_copy(
+            src_ref=src,
+            dst_ref=dst,
+            send_sem=send_sem.at[index],
+            recv_sem=recv_sem.at[index],
+            device_id=self.device(dx, dy),
+            device_id_type=pl.DeviceIdType.MESH,
+        )
+
+    def start(self, make, send_sem, recv_sem, directions):
+        for dx, dy in directions:
 
             @pl.when(self.exists(dx, dy))
             def _():
-                copy(index, dx, dy).start()
-
-        for index, (dx, dy) in enumerate(self.directions):
+                self.copy(make, send_sem, recv_sem, dx, dy).start()
+
+    def finish(self, make, send_sem, recv_sem, directions):
+        for dx, dy in directions:
 
             @pl.when(self.exists(dx, dy))
             def _():
-                copy(index, dx, dy).wait_send()
+                self.copy(make, send_sem, recv_sem, dx, dy).wait_send()
 
             @pl.when(self.exists(-dx, -dy))
             def _():
-                copy(index, dx, dy).wait_recv()
+                self.copy(make, send_sem, recv_sem, dx, dy).wait_recv()
 
 
 def ghosts_of_estimate(links, center, low, high, send_low, send_high):
@@ -300,7 +312,7 @@
 
 
 def place_kernel(
-    filled, corner_x, corner_y, tiles, blurred, back_z, observed, spread, summed, counted
+    below, filled, corner_x, corner_y, tiles, blurred, back_z, observed, spread, summed, counted
 ):
     view = pl.program_id(0)
     sources, _, capacity, wide, tall, depth = tiles.shape
@@ -323,6 +335,9 @@
                 counted[where] = counted[where] + 1.0
 
     group = group_of(block_x)
+    beyond = spread.shape[1] - below - block_x
+    spread[0, :below] = jnp.zeros((below, block_y, depth), jnp.float32)
+    spread[0, below + block_x :] = jnp.zeros((beyond, block_y, depth), jnp.float32)
 
     @pl.loop(0, block_x // group)
     def _(step):
@@ -333,16 +348,20 @@
         result = spread_quotient(
             measured.reshape(flat), blurred[0, planes].reshape(flat), back_z[0]
         )
-        spread[0, planes] = result.reshape(group, block_y, depth)
-
-
-def place(filled, corner_x, corner_y, arrived, blurred, back_z):
+        spread[0, pl.ds(below + step * group, group)] = result.reshape(group, block_y, depth)
+
+
+def place(filled, corner_x, corner_y, arrived, blurred, back_z, radius):
     sources, views, capacity, wide, tall, depth = arrived.shape
     shape = blurred.shape
     volume = pl.BlockSpec((1,) + shape[1:], lambda v, *_: (v, 0, 0, 0))
+    padded = (views, planes_of(shape[1], radius) + 2 * radius) + shape[2:]
     return pl.pallas_call(
-        place_kernel,
-        out_shape=[jax.ShapeDtypeStruct(shape, jnp.float32)] * 2,
+        functools.partial(place_kernel, 2 * radius),
+        out_shape=[
+            jax.ShapeDtypeStruct(shape, jnp.float32),
+            jax.ShapeDtypeStruct(padded, jnp.float32),
+        ],
         grid_spec=pltpu.PrefetchScalarGridSpec(
             num_scalar_prefetch=3,
             grid=(views,),
@@ -353,7 +372,10 @@
                 volume,
                 pl.BlockSpec((1,) + back_z.shape[1:], lambda v, *_: (v, 0, 0)),
             ],
-            out_specs=[volume] * 2,
+            out_specs=[
+                volume,
+                pl.BlockSpec((1,) + padded[1:], lambda v, *_: (v, 0, 0, 0)),
+            ],
             scratch_shapes=[pltpu.VMEM(shape[1:], jnp.float32)] * 2,
         ),
         compiler_params=pltpu.CompilerParams(vmem_limit_bytes=20 << 20),
@@ -430,21 +452,9 @@
     passed_z[:, below + block_x :] = jnp.zeros((views, beyond, block_y, depth), f32)
     group = group_of(block_x)
 
-    @pl.loop(0, block_x)
-    def _(x):
-        for view in range(views):
-            passed_z[view, below + x] = spreads[view, x]
-
     for sweep in range(ITERS):
         if sweep > 0:
             at = sweep - 1
-            links.exchange(
-                ghosts_of_estimate(
-                    links, center.at[at], low.at[at], high.at[at], send_low.at[at], send_high.at[at]
-                ),
-                est_send.at[at],
-                est_recv.at[at],
-            )
             pass_along_y(center.at[at], low.at[at], high.at[at], along_y, passed_y, views)
 
             @pl.loop(0, block_x // group)
@@ -475,16 +485,19 @@
         first_chunk = radius // 4
         last_chunk = (radius + block_x - 1) // 4
 
-        @pl.loop(0, planes // 4)
-        def _(step):
+        source = spreads if sweep == 0 else passed_z
+        far_chunk = (radius + block_x) // 4
+        edge_turns = planes // 4 - far_chunk + -(-radius // 4)
+        def adjoint(turn):
+            step = lax.rem(turn + far_chunk, planes // 4)
             for first in (4 * step, 4 * step + 2):
                 columns = []
                 for x in (first, first + 1):
                     stack = []
                     for view in range(views):
-                        value = taps_x[view, 0] * passed_z[view, x + below]
+                        value = taps_x[view, 0] * source[view, x + below]
                         for tap in range(1, tap_count):
-                            value = value + taps_x[view, tap] * passed_z[view, x + below - tap]
+                            value = value + taps_x[view, tap] * source[view, x + below - tap]
                         stack.append(value.astype(bf16))
                     columns.append(jnp.concatenate(stack, axis=0))
                 both = jnp.concatenate(columns, axis=1)
@@ -502,18 +515,32 @@
             def _():
                 vert(4 * step, 4).start()
 
-        @pl.loop(0, radius)
-        def _(x):
-            out_x[sweep, 0, x] = acc[sweep, x].astype(bf16)
-            out_x[sweep, 1, x] = acc[sweep, radius + block_x + x].astype(bf16)
-
-        links.exchange(
+        sums = (
             ghosts_of_sums(
                 links, out_x.at[sweep], out_y.at[sweep], in_x.at[sweep], in_y.at[sweep]
             ),
             acc_send.at[sweep],
             acc_recv.at[sweep],
         )
+
+        @pl.loop(0, edge_turns)
+        def _(turn):
+            adjoint(turn)
+
+        @pl.loop(0, radius)
+        def _(x):
+            out_x[sweep, 0, x] = acc[sweep, x].astype(bf16)
+            out_x[sweep, 1, x] = acc[sweep, radius + block_x + x].astype(bf16)
+
+        links.start(*sums, links.across_x())
+
+        @pl.loop(edge_turns, planes // 4)
+        def _(turn):
+            adjoint(turn)
+
+        links.start(*sums, links.along_y_only())
+        links.finish(*sums, links.across_x())
+        links.finish(*sums, links.along_y_only())
         forwards = [
             pltpu.make_async_remote_copy(
                 src_ref=near.at[sweep],
@@ -551,8 +578,7 @@
                     [first, plane[HALO_Y : block_y - HALO_Y], last], axis=0
                 )
 
-        @pl.loop(0, block_x)
-        def _(x):
+        def update(x):
             plane = acc[sweep, radius + x]
             first = plane[:HALO_Y] + beyond_y(0, radius + x)
             last = plane[block_y - HALO_Y :] + beyond_y(1, radius + x)
@@ -564,6 +590,39 @@
                 publish(
                     links, center.at[sweep], send_low.at[sweep], send_high.at[sweep], x, after
                 )
+
+        if sweep + 1 < ITERS:
+            news = (
+                ghosts_of_estimate(
+                    links,
+                    center.at[sweep],
+                    low.at[sweep],
+                    high.at[sweep],
+                    send_low.at[sweep],
+                    send_high.at[sweep],
+                ),
+                est_send.at[sweep],
+                est_recv.at[sweep],
+            )
+
+            @pl.loop(0, radius)
+            def _(x):
+                update(x)
+                update(block_x - radius + x)
+
+            links.start(*news, links.across_x())
+
+            @pl.loop(radius, block_x - radius)
+            def _(x):
+                update(x)
+
+            links.start(*news, links.along_y_only())
+            links.finish(*news, links.directions)
+        else:
+
+            @pl.loop(0, block_x)
+            def _(x):
+                update(x)
 
 
 def sweeps(
@@ -709,7 +768,7 @@
     back_z = jnp.concatenate(split_high_low(jnp.swapaxes(band_z, 1, 2)), axis=1)
     taps_x = mine_psf[:, 0]
     blurred = first_blur(taps_x, halos, along_y, along_z, block_x)
-    observed, spreads = place(filled, corner_x, corner_y, arrived, blurred, back_z)
+    observed, spreads = place(filled, corner_x, corner_y, arrived, blurred, back_z, radius)
     return sweeps(
         sizes,
         taps_x,

time: 143 us -> 142 us (level)
  no operation moved by 1% of the time
where the time goes in v4:
time: 142 us; the launch traced here: 141 us
  Pallas kernels  64.4 us (45%)
  local copies, waits for them, and re-layouts  27.7 us (20%)
  waiting for transfers between devices  22 us (15%)
  other arithmetic  15.7 us (11%)
  matrix products  5.5 us (4%)
  starting transfers between devices  4.95 us (3%)
    pallas_call x1, Pallas kernels, sweeps(): pl.pallas_call(functools.partial(sweep_kernel, sizes), out_shape=jax.Shap...  39.6 us
    all_to_all x1, waiting for transfers between devices, shards(): lax.all_to_all(outgoing, 'gx', split_axis=0, concat_axis=0, tiled=True)  22 us
    broadcast_in_dim x60, local copies, waits for them, and re-layouts, banded(): jnp.where(difference == tap_index, taps[..., tap_index, None, None], 0.0)  10.7 us
    pallas_call x1, Pallas kernels, first_halos(): pl.pallas_call(functools.partial(halo_kernel, sizes, radius), out_shape=[...  9.03 us
    pallas_call x1, Pallas kernels, place(): pl.pallas_call(functools.partial(place_kernel, 2 * radius), out_shape=[ja...  8.62 us
    pallas_call x1, Pallas kernels, first_blur(): pl.pallas_call(blur_kernel, out_shape=jax.ShapeDtypeStruct(shape, jnp.flo...  7.15 us
    unnamed x54, local copies, waits for them, and re-layouts  6.36 us
    eq x19, other arithmetic, banded(): difference == tap_index  6.11 us
  transfers between devices with their start and end apart: 1, of which 1 were waited for; matrix products, arithmetic and copies ran while one was open for 27% of the time, Pallas kernels for 5%

profile of v4, /device:TPU:0, one launch (start us, length us, event | category | flops | bytes accessed | tf_op | source)
XLA Modules:
  0.0 141.0 jit_solution(1303962556705962470)
XLA Ops:
  0.0 0.8 fusion.227
  1.4 1.2 fusion
  2.6 2.6 %copy.87 = bf16[3,4,8,8,16,128]{5,4,3,2,0,1:T(8,128)(2,1)} copy(bf16[3,4,8,8,16,128]{5,2,4,3,1,0:T(8,128)(2,1)S(1)} %fusion) | data formatting | bytes 6291456 | tf_op jit(solution)/shard_map/vgkj,vjabz->gvkabz/dot_general | solution.py:708
  5.2 9.0 %shard_map.64 = (bf16[48,64,128]{2,1,0:T(8,128)(2,1)S(1)}, bf16[48,8,128]{2,1,0:T(8,128)(2,1)S(1)}, bf16[48,8,128]{2,1,0:T(8,128)(2,1)S(1)}) custom-call(f32[32,64,128]{2,1,0:T(8,128)S(1)} %copy-done.1), custom_call_target="tpu_custom_call" | custom-call | tf_op jit(solution)/shard_map/pallas_call | solution.py:283
  14.3 0.9 copy-done.5
  15.1 4.9 %all-to-all-start = ((bf16[4,3,8,8,16,128]{5,4,3,2,1,0:T(8,128)(2,1)}), bf16[4,3,8,8,16,128]{5,4,3,2,1,0:T(8,128)(2,1)}, u32[]{:S(2)}, u32[]{:S(2)}) async-start(bf16[4,3,8,8,16,128]{5,4,3,2,1,0:T(8,128)(2,1)} %bitcast.62), calls=%async_computation | async-start | bytes 6291456 | tf_op jit(solution)/shard_map/all_to_all | solution.py:717
  20.4 0.6 fusion.110
  21.1 0.6 fusion.112
  21.7 0.6 fusion.114
  22.4 0.6 fusion.116
  23.0 0.6 fusion.118
  23.6 0.7 fusion.120
  24.3 0.6 fusion.122
  24.9 0.6 fusion.124
  29.7 0.6 broadcast_in_dim.1023
  30.4 0.6 broadcast_in_dim.1029
  31.1 0.7 broadcast_in_dim.1035
  31.8 0.7 broadcast_in_dim.1041
  32.6 0.7 broadcast_in_dim.1047
  33.3 0.7 broadcast_in_dim.1053
  34.0 0.7 broadcast_in_dim.1059
  34.8 0.7 broadcast_in_dim.1065
  35.5 0.6 broadcast_in_dim.1071
  36.2 0.7 broadcast_in_dim.1077
  36.9 0.6 broadcast_in_dim.1083
  37.6 0.6 broadcast_in_dim.1089
  40.3 0.9 reduce-precision_convert_fusion.2
  41.8 0.7 fusion.228
  42.7 1.4 %fusion.141 = (s32[3,4,8]{2,1,0:T(4,128)S(1)}, s32[3,4,8]{2,1,0:T(4,128)S(1)}, s32[3,4,8]{2,1,0:T(4,128)S(1)}) fusion(s32[3,4,16]{2,1,0:T(4,128)S(1)} %mul.71, s32[3,4,16]{2,1,0:T(4,128)} %bitcast.81, s32[3,4,16]{2,1,0:T(4,128)S(1)} %dynamic-slice_reduce_fusion, s32[8]{0:T(128)} %copy-done.22, s32[3,4,16]{2,1,0:T(4,128)S(1)} %mul.68), kind=kLoop, calls=%fused_computation.164 | loop fusion | flops 10464 | bytes 4256 | tf_op jit(solution)/shard_map/reduce_sum | solution.py:725
  44.9 0.8 broadcast_add_fusion
  45.7 0.7 ge.35
  46.3 0.7 bitcast_add_fusion
  47.1 0.7 ge.31
  47.7 0.7 copy.88
  48.4 0.7 copy_bitcast_fusion.1
  50.9 1.3 reduce-precision_convert_fusion
  52.3 0.7 broadcast_add_fusion.1
  53.0 0.6 fusion.224
  54.1 0.8 fusion.8
  55.4 0.8 add_reduce_fusion
  56.2 2.8 %fusion.2.refs_4_ = f32[32,64,128]{2,1,0:T(8,128)} fusion(f32[6,32,64]{2,1,0:T(8,128)S(1)} %fusion.61, f32[6,128]{1,0:T(8,128)S(1)} %add_reduce_fusion), kind=kOutput, calls=%fused_computation.4 | convolution fusion | flops 19398656 | bytes 1100800 | tf_op jit(solution)/shard_map/vxy,vz->xyz/dot_general | solution.py:751
  59.0 7.2 %shard_map.65.blurred = f32[3,32,64,128]{3,2,1,0:T(8,128)S(1)} custom-call(f32[3,15]{1,0:T(4,128)S(1)} %bitcast.60, bf16[48,64,128]{2,1,0:T(8,128)(2,1)S(1)} %copy-done.6, bf16[48,8,128]{2,1,0:T(8,128)(2,1)S(1)} %get-tuple-element.19.low, bf16[48,8,128]{2,1,0:T(8,128)(2,1)S(1)} %get-tuple-element.20.high, bf16[192,160]{1,0:T(8,128)(2,1)S(1)} %copy.59.along_y.refs_5_, ...), custom_call_target="tpu_custom_call" | custom-call | flops 10000000000 | bytes 40000000 | tf_op jit(solution)/shard_map/pallas_call | solution.py:301
  66.2 1.7 %copy-done.2 = f32[3,32,64,128]{3,2,1,0:T(8,128)} copy-done((f32[3,32,64,128]{3,2,1,0:T(8,128)}, f32[3,32,64,128]{3,2,1,0:T(8,128)S(1)}, u32[]{:S(2)}) %copy-start.2) | copy-done | bytes 3145752
  67.9 22.0 %all-to-all-done.tiles = bf16[4,3,8,8,16,128]{5,4,3,2,1,0:T(8,128)(2,1)} async-done(((bf16[4,3,8,8,16,128]{5,4,3,2,1,0:T(8,128)(2,1)}), bf16[4,3,8,8,16,128]{5,4,3,2,1,0:T(8,128)(2,1)}, u32[]{:S(2)}, u32[]{:S(2)}) %all-to-all-start) | async-done | bytes 3145760 | tf_op jit(solution)/shard_map/all_to_all | solution.py:717
  89.9 1.9 %copy-done.3 = f32[3,32,64,128]{3,2,1,0:T(8,128)S(1)} copy-done((f32[3,32,64,128]{3,2,1,0:T(8,128)S(1)}, f32[3,32,64,128]{3,2,1,0:T(8,128)}, u32[]{:S(2)}) %copy-start.3) | copy-done | bytes 3145752
  91.8 8.6 %shard_map.66 = (f32[3,32,64,128]{3,2,1,0:T(8,128)S(1)}, f32[3,62,64,128]{3,2,1,0:T(8,128)S(1)}) custom-call(s32[3,32]{1,0:T(4,128)S(1)} %reshape.204.filled, s32[3,32]{1,0:T(4,128)S(1)} %reshape.205.corner_x, s32[3,32]{1,0:T(4,128)S(1)} %reshape.206.corner_y, bf16[4,3,8,8,16,128]{5,4,3,2,1,0:T(8,128)(2,1)} %all-to-all-done.tiles, ...), custom_call_target="tpu_custom_call" | custom-call | tf_op jit(solution)/shard_map/pallas_call | solution.py:359
  100.4 39.6 %shard_map.67 = f32[32,64,128]{2,1,0:T(8,128)S(1)} custom-call(f32[3,15]{1,0:T(4,128)S(1)} %bitcast.61, f32[3,32,64,128]{3,2,1,0:T(8,128)S(1)} %get-tuple-element.21.refs_1_, f32[3,62,64,128]{3,2,1,0:T(8,128)S(1)} %get-tuple-element.22.refs_2_, f32[32,64,128]{2,1,0:T(8,128)S(1)} %copy-done.1, f32[32,64,128]{2,1,0:T(8,128)S(1)} %copy-done.4, ...), custom_call_target="tpu_custom_call" | custom-call | tf_op jit(solution)/shard_map/pallas_call | solution.py:640
  140.0 1.0 copy.91
  (149 shorter events, 11.6 us)
Async XLA Ops:
  0.0 1.4 %copy-start = (bf16[3,1,16,8,16,128]{5,4,3,2,1,0:T(8,128)(2,1)S(1)}, bf16[3,1,16,8,16,128]{5,4,3,2,1,0:T(8,128)(2,1)}, u32[]{:S(2)}) copy-start(bf16[3,1,16,8,16,128]{5,4,3,2,1,0:T(8,128)(2,1)} %param.6) | copy-start | bytes 4718596
  0.0 1.4 %copy-start.22 = (s32[8]{0:T(128)}, s32[8]{0:T(128)S(1)}, u32[]{:S(2)}) copy-start(s32[8]{0:T(128)S(1)} %iota_add_fusion.4) | copy-start | bytes 100
  2.6 2.6 %copy-start.1 = (f32[32,64,128]{2,1,0:T(8,128)S(1)}, f32[32,64,128]{2,1,0:T(8,128)}, u32[]{:S(2)}) copy-start(f32[32,64,128]{2,1,0:T(8,128)} %refs_3_.1) | copy-start | bytes 3145732
  14.2 0.9 copy-start.5
  15.1 13.0 %copy-start.21 = (f32[6,3,15]{2,1,0:T(4,128)S(1)}, f32[6,3,15]{2,1,0:T(4,128)}, u32[]{:S(2)}) copy-start(f32[6,3,15]{2,1,0:T(4,128)} %param.10) | copy-start | bytes 3244
  15.1 74.8 %all-to-all-start = ((bf16[4,3,8,8,16,128]{5,4,3,2,1,0:T(8,128)(2,1)}), bf16[4,3,8,8,16,128]{5,4,3,2,1,0:T(8,128)(2,1)}, u32[]{:S(2)}, u32[]{:S(2)}) async-start(bf16[4,3,8,8,16,128]{5,4,3,2,1,0:T(8,128)(2,1)} %bitcast.62), calls=%async_computation | async-start | bytes 6291456 | tf_op jit(solution)/shard_map/all_to_all | solution.py:717
  20.3 30.5 %copy-start.7 = (pred[128,128]{1,0:T(8,128)(4,1)}, pred[128,128]{1,0:T(8,128)(4,1)S(1)}, u32[]{:S(2)}) copy-start(pred[128,128]{1,0:T(8,128)(4,1)S(1)} %get-tuple-element.173) | copy-start | bytes 49156
  20.3 30.5 %copy-start.9 = (pred[128,128]{1,0:T(8,128)(4,1)}, pred[128,128]{1,0:T(8,128)(4,1)S(1)}, u32[]{:S(2)}) copy-start(pred[128,128]{1,0:T(8,128)(4,1)S(1)} %get-tuple-element.174) | copy-start | bytes 49156
  20.3 30.5 %copy-start.11 = (pred[128,128]{1,0:T(8,128)(4,1)}, pred[128,128]{1,0:T(8,128)(4,1)S(1)}, u32[]{:S(2)}) copy-start(pred[128,128]{1,0:T(8,128)(4,1)S(1)} %get-tuple-element.175) | copy-start | bytes 49156
  20.4 30.5 %copy-start.13 = (pred[128,128]{1,0:T(8,128)(4,1)}, pred[128,128]{1,0:T(8,128)(4,1)S(1)}, u32[]{:S(2)}) copy-start(pred[128,128]{1,0:T(8,128)(4,1)S(1)} %get-tuple-element.176) | copy-start | bytes 49156
  20.4 30.5 %copy-start.15 = (pred[128,128]{1,0:T(8,128)(4,1)}, pred[128,128]{1,0:T(8,128)(4,1)S(1)}, u32[]{:S(2)}) copy-start(pred[128,128]{1,0:T(8,128)(4,1)S(1)} %get-tuple-element.177) | copy-start | bytes 49156
  20.4 31.9 %copy-start.17 = (pred[128,128]{1,0:T(8,128)(4,1)}, pred[128,128]{1,0:T(8,128)(4,1)S(1)}, u32[]{:S(2)}) copy-start(pred[128,128]{1,0:T(8,128)(4,1)S(1)} %fusion.139) | copy-start | bytes 49156
  47.7 6.0 %copy-start.23 = (s32[78]{0:T(128)S(1)}, s32[78]{0:T(128)}, u32[]{:S(2)}) copy-start(s32[78]{0:T(128)} %iota_add_fusion) | copy-start | bytes 940
  47.7 6.1 %copy-start.19 = (s32[6,128]{1,0:T(8,128)S(1)}, s32[6,128]{1,0:T(8,128)}, u32[]{:S(2)}) copy-start(s32[6,128]{1,0:T(8,128)} %ge.35) | copy-start | bytes 9220
  47.7 6.1 %copy-start.20 = (s32[6,128]{1,0:T(8,128)S(1)}, s32[6,128]{1,0:T(8,128)}, u32[]{:S(2)}) copy-start(s32[6,128]{1,0:T(8,128)} %ge.31) | copy-start | bytes 9220
  47.7 6.1 %copy-start.24 = (s32[78]{0:T(128)S(1)}, s32[78]{0:T(128)}, u32[]{:S(2)}) copy-start(s32[78]{0:T(128)} %broadcast_add_fusion.3) | copy-start | bytes 940
  50.9 4.5 %copy-start.8 = (pred[128,128]{1,0:T(8,128)(4,1)S(1)}, pred[128,128]{1,0:T(8,128)(4,1)}, u32[]{:S(2)}) copy-start(pred[128,128]{1,0:T(8,128)(4,1)} %copy-done.7) | copy-start | bytes 49156
  50.9 4.5 %copy-start.10 = (pred[128,128]{1,0:T(8,128)(4,1)S(1)}, pred[128,128]{1,0:T(8,128)(4,1)}, u32[]{:S(2)}) copy-start(pred[128,128]{1,0:T(8,128)(4,1)} %copy-done.9) | copy-start | bytes 49156
  50.9 4.5 %copy-start.12 = (pred[128,128]{1,0:T(8,128)(4,1)S(1)}, pred[128,128]{1,0:T(8,128)(4,1)}, u32[]{:S(2)}) copy-start(pred[128,128]{1,0:T(8,128)(4,1)} %copy-done.11) | copy-start | bytes 49156
  50.9 4.5 %copy-start.14 = (pred[128,128]{1,0:T(8,128)(4,1)S(1)}, pred[128,128]{1,0:T(8,128)(4,1)}, u32[]{:S(2)}) copy-start(pred[128,128]{1,0:T(8,128)(4,1)} %copy-done.13) | copy-start | bytes 49156
  50.9 4.5 %copy-start.16 = (pred[128,128]{1,0:T(8,128)(4,1)S(1)}, pred[128,128]{1,0:T(8,128)(4,1)}, u32[]{:S(2)}) copy-start(pred[128,128]{1,0:T(8,128)(4,1)} %copy-done.15) | copy-start | bytes 49156
  52.3 3.1 %copy-start.18 = (pred[128,128]{1,0:T(8,128)(4,1)S(1)}, pred[128,128]{1,0:T(8,128)(4,1)}, u32[]{:S(2)}) copy-start(pred[128,128]{1,0:T(8,128)(4,1)} %copy-done.17) | copy-start | bytes 49156
  54.8 4.2 %copy-start.6 = (bf16[48,64,128]{2,1,0:T(8,128)(2,1)S(1)}, bf16[48,64,128]{2,1,0:T(8,128)(2,1)}, u32[]{:S(2)}) copy-start(bf16[48,64,128]{2,1,0:T(8,128)(2,1)} %copy-done.5) | copy-start | bytes 2359300
  66.2 1.7 %copy-start.2 = (f32[3,32,64,128]{3,2,1,0:T(8,128)}, f32[3,32,64,128]{3,2,1,0:T(8,128)S(1)}, u32[]{:S(2)}) copy-start(f32[3,32,64,128]{3,2,1,0:T(8,128)S(1)} %shard_map.65.blurred) | copy-start | bytes 9437188
  89.9 1.9 %copy-start.3 = (f32[3,32,64,128]{3,2,1,0:T(8,128)S(1)}, f32[3,32,64,128]{3,2,1,0:T(8,128)}, u32[]{:S(2)}) copy-start(f32[3,32,64,128]{3,2,1,0:T(8,128)} %copy-done.2) | copy-start | bytes 9437188
  91.8 8.6 %copy-start.4 = (f32[32,64,128]{2,1,0:T(8,128)S(1)}, f32[32,64,128]{2,1,0:T(8,128)}, u32[]{:S(2)}) copy-start(f32[32,64,128]{2,1,0:T(8,128)} %fusion.2.refs_4_) | copy-start | bytes 3145732
